TPU v7x, 32 devices: a whole 2x2x4 slice. The times are simulated.
32 devices in a mesh: grp: 4 (over x, core), chan: 8 (over z, y).
Axes of the slice: x: 2, y: 2, z: 4, core: 2. Of those that a mesh axis runs over, the one named last changes fastest.
Arguments:
- voltages: int32 [256, 31, 8192], P('grp', None, 'chan'), may hold values from -128 to 127
- plan: int32 [3, 4], replicated, may hold values from 0 to 3, as said below
Outputs:
- visibility: bfloat16 [3, 256, 2048, 128], P(None, 'grp', 'chan')
Inputs may be any that keep to these rules, and one draw needn't show every extreme that they name: Every row is a perfect matching of the 4 groups: plan[r, plan[r, g]] = g and plan[r, g] != g; the 3 partners of a group are all different.
All inputs are finite; a program needn't handle non-finite values.
Results may differ from a plain program's by a relative error of at most 0.0057.
Values may be sent and summed in bfloat16 or wider, within the bound.
No kernel may reach another device: no remote copies, remote signals or barrier semaphores. Data moves between devices by JAX's collectives and lax.ppermute only.
A program may use at most 128 MiB of HBM per device.

v0:
```python
import math

import jax
import jax.numpy as jnp
from jax import lax
from jax.sharding import PartitionSpec as P

TAPS = 16


def taper_coeff(position, length_total, fft_len):
    window = 0.5 - 0.5 * jnp.cos(2.0 * math.pi * position / length_total)
    return window * jnp.sinc((position - 0.5 * length_total) / fft_len)


def correlate(mine_rows, theirs, sig_count, spec_count):
    half_len = mine_rows.shape[1]
    mine_four = mine_rows.reshape(2, half_len, sig_count, spec_count)
    their_four = theirs.reshape(2, half_len, sig_count, spec_count)
    left_side = jnp.concatenate([mine_four[0], mine_four[1]], axis=-1)
    right_re = jnp.concatenate([their_four[0], their_four[1]], axis=-1)
    right_im = jnp.concatenate([-their_four[1], their_four[0]], axis=-1)
    vis_re = jnp.einsum("kas,kbs->akb", left_side, right_re, preferred_element_type=jnp.float32)
    vis_im = jnp.einsum("kas,kbs->akb", left_side, right_im, preferred_element_type=jnp.float32)
    return jnp.concatenate([vis_re, vis_im], axis=-1) * (1.0 / spec_count)


def local(voltages, plan):
    sig_count, frames, block_len = voltages.shape
    chan_count = lax.axis_size("chan")
    group_count = lax.axis_size("grp")
    spec_count = frames - TAPS + 1
    fft_len = block_len * chan_count
    sub_len = block_len // chan_count
    chan_id = lax.axis_index("chan")
    group_id = lax.axis_index("grp")
    highest = lax.Precision.HIGHEST
    n_global = chan_id * block_len + jnp.arange(block_len)
    tap_ids = jnp.arange(TAPS)[:, None]
    coeffs = taper_coeff(
        (tap_ids * fft_len + n_global[None, :]).astype(jnp.float32), TAPS * fft_len, fft_len
    )
    samples = voltages.astype(jnp.float32)

    def add_tap(tap_index, running):
        weight = lax.dynamic_slice_in_dim(coeffs, tap_index, 1, 0)
        return running + weight * lax.dynamic_slice_in_dim(samples, tap_index, spec_count, 1)

    filtered = lax.fori_loop(
        0, TAPS, add_tap, jnp.zeros((sig_count, spec_count, block_len), jnp.float32)
    )
    row_count = sig_count * spec_count
    flat_rows = filtered.reshape(row_count, block_len).T.reshape(1, block_len, row_count)
    turned = lax.all_to_all(flat_rows, "chan", split_axis=1, concat_axis=0, tiled=True)
    src_ids = jnp.arange(chan_count)
    angle_small = (
        2.0
        * math.pi
        * (src_ids[:, None] * src_ids[None, :] % chan_count).astype(jnp.float32)
        / chan_count
    )
    part_re = jnp.einsum("nk,nmr->kmr", jnp.cos(angle_small), turned, precision=highest)
    part_im = -jnp.einsum("nk,nmr->kmr", jnp.sin(angle_small), turned, precision=highest)
    n_second = chan_id * sub_len + jnp.arange(sub_len)
    twist_angle = (
        2.0
        * math.pi
        * (src_ids[:, None] * n_second[None, :] % fft_len).astype(jnp.float32)
        / fft_len
    )
    twist_cos = jnp.cos(twist_angle)[:, :, None]
    twist_sin = jnp.sin(twist_angle)[:, :, None]
    rot_re = part_re * twist_cos + part_im * twist_sin
    rot_im = part_im * twist_cos - part_re * twist_sin
    stacked = jnp.stack([rot_re, rot_im])
    columns = lax.all_to_all(stacked, "chan", split_axis=1, concat_axis=2, tiled=True)
    col_re = columns[0, 0]
    col_im = columns[1, 0]
    ch_dev = block_len // 2
    out_ids = jnp.arange(ch_dev)
    in_ids = jnp.arange(block_len)
    angle_big = (
        2.0
        * math.pi
        * (out_ids[:, None] * in_ids[None, :] % block_len).astype(jnp.float32)
        / block_len
    )
    cos_big = jnp.cos(angle_big)
    sin_big = jnp.sin(angle_big)
    chan_re = jnp.dot(cos_big, col_re, precision=highest) + jnp.dot(
        sin_big, col_im, precision=highest
    )
    chan_im = jnp.dot(cos_big, col_im, precision=highest) - jnp.dot(
        sin_big, col_re, precision=highest
    )
    gain_const = 1.0 / (64.0 * math.sqrt(fft_len))
    channel = (jnp.stack([chan_re, chan_im]) * gain_const).astype(jnp.bfloat16)
    group_ids = jnp.arange(group_count)
    partner = jnp.sum(jnp.where(group_ids[None, :] == group_id, plan, 0), axis=1)
    half_len = ch_dev // 2
    lower_half = channel[:, :half_len]
    upper_half = channel[:, half_len:]
    listed = jnp.any(partner[:, None] == group_ids[None, :], axis=0)
    slot_ids = group_ids[:, None, None, None]
    chosen_half = jnp.where(slot_ids > group_id, upper_half[None], lower_half[None])
    slot_data = jnp.where(listed[:, None, None, None], chosen_half, jnp.zeros_like(chosen_half))
    received = lax.all_to_all(slot_data, "grp", split_axis=0, concat_axis=0, tiled=True)
    results = []
    for round_index in range(plan.shape[0]):
        partner_id = partner[round_index]
        upper_flag = (group_id > partner_id).astype(jnp.int32)
        mine_rows = lax.dynamic_slice_in_dim(channel, upper_flag * half_len, half_len, 1)
        theirs = lax.dynamic_index_in_dim(received, partner_id, 0, keepdims=False)
        results.append(correlate(mine_rows, theirs, sig_count, spec_count))
    return jnp.stack(results).astype(jnp.bfloat16)


def solution(mesh):
    in_specs = (P("grp", None, "chan"), P())
    out_specs = P(None, "grp", "chan", None)
    return jax.shard_map(local, mesh=mesh, in_specs=in_specs, out_specs=out_specs, check_vma=False)
```

profile of v0, /device:TPU:0, one launch (start us, length us, event | category | flops | bytes accessed | tf_op | source)
XLA Modules:
  0.0 695.1 jit_solution(7186519349170392500)
XLA Ops:
  0.0 11.4 %copy_convert_fusion = f32[64,31,1024]{2,1,0:T(8,128)} fusion(s32[64,31,1024]{2,0,1:T(8,128)} %param.4), kind=kLoop, calls=%fused_computation.10 | loop fusion | flops 2031616 | bytes 16252928 | tf_op jit(solution)/shard_map/convert_element_type | solution.py:43
  11.8 127.8 %while.14 = (s32[]{:T(128)}, f32[64,16,1024]{2,1,0:T(8,128)}, f32[16,1024]{1,0:T(8,128)S(1)}, f32[64,31,1024]{2,1,0:T(8,128)}, s32[]{:T(128)}, /*index=5*/s32[]{:T(128)}) while((s32[]{:T(128)}, f32[64,16,1024]{2,1,0:T(8,128)}, f32[16,1024]{1,0:T(8,128)S(1)}, f32[64,31,1024]{2,1,0:T(8,128)}, s32[]{:T(128)}, ...), condition=%wide.region_3.4_spmd.clone, body=%wide.region_2.3_spmd.clone.sunk | while | flops 3145731 | bytes 12595287 | solution.py:49
  18.6 8.1 %select_add_fusion.2 = f32[64,16,1024]{2,1,0:T(8,128)} fusion(f32[64,16,1024]{2,1,0:T(8,128)} %get-tuple-element.165, f32[64,31,1024]{2,1,0:T(8,128)} %get-tuple-element.173, s32[]{:T(128)} %get-tuple-element.164, f32[1024]{0:T(1024)S(1)} %bitcast.102, pred[]{:T(512)S(6)} %compare.11), kind=kLoop, calls=%fused_computation.clone.1 | loop fusion | flops 3145728 | bytes 12587013 | tf_op jit(solution)/shard_map/while/body/eval_jaxpr/add | solution.py:47
  26.7 8.1 %select_add_fusion.2 = f32[64,16,1024]{2,1,0:T(8,128)} fusion(f32[64,16,1024]{2,1,0:T(8,128)} %get-tuple-element.165, f32[64,31,1024]{2,1,0:T(8,128)} %get-tuple-element.173, s32[]{:T(128)} %get-tuple-element.164, f32[1024]{0:T(1024)S(1)} %bitcast.102, pred[]{:T(512)S(6)} %compare.11), kind=kLoop, calls=%fused_computation.clone.1 | loop fusion | flops 3145728 | bytes 12587013 | tf_op jit(solution)/shard_map/while/body/eval_jaxpr/add | solution.py:47
  34.8 8.1 %select_add_fusion.2 = f32[64,16,1024]{2,1,0:T(8,128)} fusion(f32[64,16,1024]{2,1,0:T(8,128)} %get-tuple-element.165, f32[64,31,1024]{2,1,0:T(8,128)} %get-tuple-element.173, s32[]{:T(128)} %get-tuple-element.164, f32[1024]{0:T(1024)S(1)} %bitcast.102, pred[]{:T(512)S(6)} %compare.11), kind=kLoop, calls=%fused_computation.clone.1 | loop fusion | flops 3145728 | bytes 12587013 | tf_op jit(solution)/shard_map/while/body/eval_jaxpr/add | solution.py:47
  42.8 8.1 %select_add_fusion.2 = f32[64,16,1024]{2,1,0:T(8,128)} fusion(f32[64,16,1024]{2,1,0:T(8,128)} %get-tuple-element.165, f32[64,31,1024]{2,1,0:T(8,128)} %get-tuple-element.173, s32[]{:T(128)} %get-tuple-element.164, f32[1024]{0:T(1024)S(1)} %bitcast.102, pred[]{:T(512)S(6)} %compare.11), kind=kLoop, calls=%fused_computation.clone.1 | loop fusion | flops 3145728 | bytes 12587013 | tf_op jit(solution)/shard_map/while/body/eval_jaxpr/add | solution.py:47
  50.9 8.1 %select_add_fusion.2 = f32[64,16,1024]{2,1,0:T(8,128)} fusion(f32[64,16,1024]{2,1,0:T(8,128)} %get-tuple-element.165, f32[64,31,1024]{2,1,0:T(8,128)} %get-tuple-element.173, s32[]{:T(128)} %get-tuple-element.164, f32[1024]{0:T(1024)S(1)} %bitcast.102, pred[]{:T(512)S(6)} %compare.11), kind=kLoop, calls=%fused_computation.clone.1 | loop fusion | flops 3145728 | bytes 12587013 | tf_op jit(solution)/shard_map/while/body/eval_jaxpr/add | solution.py:47
  59.0 8.1 %select_add_fusion.2 = f32[64,16,1024]{2,1,0:T(8,128)} fusion(f32[64,16,1024]{2,1,0:T(8,128)} %get-tuple-element.165, f32[64,31,1024]{2,1,0:T(8,128)} %get-tuple-element.173, s32[]{:T(128)} %get-tuple-element.164, f32[1024]{0:T(1024)S(1)} %bitcast.102, pred[]{:T(512)S(6)} %compare.11), kind=kLoop, calls=%fused_computation.clone.1 | loop fusion | flops 3145728 | bytes 12587013 | tf_op jit(solution)/shard_map/while/body/eval_jaxpr/add | solution.py:47
  67.0 8.1 %select_add_fusion.2 = f32[64,16,1024]{2,1,0:T(8,128)} fusion(f32[64,16,1024]{2,1,0:T(8,128)} %get-tuple-element.165, f32[64,31,1024]{2,1,0:T(8,128)} %get-tuple-element.173, s32[]{:T(128)} %get-tuple-element.164, f32[1024]{0:T(1024)S(1)} %bitcast.102, pred[]{:T(512)S(6)} %compare.11), kind=kLoop, calls=%fused_computation.clone.1 | loop fusion | flops 3145728 | bytes 12587013 | tf_op jit(solution)/shard_map/while/body/eval_jaxpr/add | solution.py:47
  75.1 8.1 %select_add_fusion.2 = f32[64,16,1024]{2,1,0:T(8,128)} fusion(f32[64,16,1024]{2,1,0:T(8,128)} %get-tuple-element.165, f32[64,31,1024]{2,1,0:T(8,128)} %get-tuple-element.173, s32[]{:T(128)} %get-tuple-element.164, f32[1024]{0:T(1024)S(1)} %bitcast.102, pred[]{:T(512)S(6)} %compare.11), kind=kLoop, calls=%fused_computation.clone.1 | loop fusion | flops 3145728 | bytes 12587013 | tf_op jit(solution)/shard_map/while/body/eval_jaxpr/add | solution.py:47
  83.2 8.1 %select_add_fusion.2 = f32[64,16,1024]{2,1,0:T(8,128)} fusion(f32[64,16,1024]{2,1,0:T(8,128)} %get-tuple-element.165, f32[64,31,1024]{2,1,0:T(8,128)} %get-tuple-element.173, s32[]{:T(128)} %get-tuple-element.164, f32[1024]{0:T(1024)S(1)} %bitcast.102, pred[]{:T(512)S(6)} %compare.11), kind=kLoop, calls=%fused_computation.clone.1 | loop fusion | flops 3145728 | bytes 12587013 | tf_op jit(solution)/shard_map/while/body/eval_jaxpr/add | solution.py:47
  91.2 8.1 %select_add_fusion.2 = f32[64,16,1024]{2,1,0:T(8,128)} fusion(f32[64,16,1024]{2,1,0:T(8,128)} %get-tuple-element.165, f32[64,31,1024]{2,1,0:T(8,128)} %get-tuple-element.173, s32[]{:T(128)} %get-tuple-element.164, f32[1024]{0:T(1024)S(1)} %bitcast.102, pred[]{:T(512)S(6)} %compare.11), kind=kLoop, calls=%fused_computation.clone.1 | loop fusion | flops 3145728 | bytes 12587013 | tf_op jit(solution)/shard_map/while/body/eval_jaxpr/add | solution.py:47
  99.3 8.1 %select_add_fusion.2 = f32[64,16,1024]{2,1,0:T(8,128)} fusion(f32[64,16,1024]{2,1,0:T(8,128)} %get-tuple-element.165, f32[64,31,1024]{2,1,0:T(8,128)} %get-tuple-element.173, s32[]{:T(128)} %get-tuple-element.164, f32[1024]{0:T(1024)S(1)} %bitcast.102, pred[]{:T(512)S(6)} %compare.11), kind=kLoop, calls=%fused_computation.clone.1 | loop fusion | flops 3145728 | bytes 12587013 | tf_op jit(solution)/shard_map/while/body/eval_jaxpr/add | solution.py:47
  107.4 8.1 %select_add_fusion.2 = f32[64,16,1024]{2,1,0:T(8,128)} fusion(f32[64,16,1024]{2,1,0:T(8,128)} %get-tuple-element.165, f32[64,31,1024]{2,1,0:T(8,128)} %get-tuple-element.173, s32[]{:T(128)} %get-tuple-element.164, f32[1024]{0:T(1024)S(1)} %bitcast.102, pred[]{:T(512)S(6)} %compare.11), kind=kLoop, calls=%fused_computation.clone.1 | loop fusion | flops 3145728 | bytes 12587013 | tf_op jit(solution)/shard_map/while/body/eval_jaxpr/add | solution.py:47
  139.6 10.9 %copy.146 = f32[1,1024,1024]{2,0,1:T(1,128)} copy(f32[1,1024,1024]{1,2,0:T(8,128)} %bitcast.77) | data formatting | bytes 8388608 | tf_op jit(solution)/shard_map/reshape | solution.py:53
  158.2 92.9 %all-to-all-done = f32[1,1024,1024]{2,0,1:T(1,128)} async-done(((f32[1,1024,1024]{2,0,1:T(1,128)}), f32[1,1024,1024]{2,0,1:T(1,128)}, u32[]{:S(2)}, u32[]{:S(2)}) %all-to-all-start) | async-done | bytes 4194336 | tf_op jit(solution)/shard_map/all_to_all | solution.py:54
  269.6 8.3 %copy.151 = f32[2,8,128,1024]{3,2,0,1:T(8,128)} copy(f32[2,8,128,1024]{3,1,2,0:T(8,128)S(1)} %pad_maximum_fusion.1) | data formatting | bytes 16777216 | tf_op jit(solution)/shard_map/stack | solution.py:75
  283.6 181.6 %all-to-all-done.1 = f32[2,8,128,1024]{3,2,0,1:T(8,128)} async-done(((f32[2,8,128,1024]{3,2,0,1:T(8,128)}), f32[2,8,128,1024]{3,2,0,1:T(8,128)}, u32[]{:S(2)}, u32[]{:S(2)}) %all-to-all-start.1) | async-done | bytes 8388640 | tf_op jit(solution)/shard_map/all_to_all | solution.py:76
  469.5 14.6 %fusion.27 = f32[512,1024]{1,0:T(8,128)S(1)} fusion(f32[1024,1024]{1,0:T(8,128)S(1)} %bitcast.92), kind=kOutput, calls=%fused_computation.55 | convolution fusion | flops 6449790976 | bytes 6291456 | tf_op jit(solution)/shard_map/dot_general | solution.py:90
  484.2 14.7 %fusion.25 = f32[512,1024]{1,0:T(8,128)S(1)} fusion(f32[1024,1024]{1,0:T(8,128)S(1)} %bitcast.94), kind=kOutput, calls=%fused_computation.54 | convolution fusion | flops 6449790976 | bytes 6291456 | tf_op jit(solution)/shard_map/dot_general | solution.py:93
  498.9 14.9 %add_bitcast_fusion.1 = f32[1,512,1024]{2,1,0:T(8,128)S(1)} fusion(f32[512,1024]{1,0:T(8,128)S(1)} %fusion.27, f32[1024,1024]{1,0:T(8,128)S(1)} %bitcast.95), kind=kOutput, calls=%fused_computation.45 | convolution fusion | flops 6450315264 | bytes 8388608 | tf_op jit(solution)/shard_map/dot_general | solution.py:90
  513.8 14.7 %subtract_bitcast_fusion.1 = f32[1,512,1024]{2,1,0:T(8,128)S(1)} fusion(f32[512,1024]{1,0:T(8,128)S(1)} %fusion.25, f32[1024,1024]{1,0:T(8,128)S(1)} %bitcast.93), kind=kOutput, calls=%fused_computation.44 | convolution fusion | flops 6450315264 | bytes 8388608 | tf_op jit(solution)/shard_map/dot_general | solution.py:93
  575.7 15.6 %all-to-all-done.2 = bf16[4,2,256,1024]{2,3,1,0:T(8,128)(2,1)} async-done(((bf16[4,2,256,1024]{2,3,1,0:T(8,128)(2,1)}), bf16[4,2,256,1024]{2,3,1,0:T(8,128)(2,1)}, u32[]{:S(2)}, u32[]{:S(2)}) %all-to-all-start.2) | async-done | bytes 4194336 | tf_op jit(solution)/shard_map/all_to_all | solution.py:107
  666.9 28.0 %copy.177 = bf16[3,64,256,128]{3,2,1,0:T(8,128)(2,1)} copy(bf16[3,64,256,128]{3,1,2,0:T(8,128)(2,1)S(1)} %pad_maximum_fusion) | data formatting | bytes 25165824 | tf_op jit(solution)/shard_map/stack | solution.py:115
  (110 shorter events, 182.4 us)
Async XLA Ops:
  150.5 100.6 %all-to-all-start = ((f32[1,1024,1024]{2,0,1:T(1,128)}), f32[1,1024,1024]{2,0,1:T(1,128)}, u32[]{:S(2)}, u32[]{:S(2)}) async-start(f32[1,1024,1024]{2,0,1:T(1,128)} %copy.146), calls=%async_computation | async-start | bytes 8388608 | tf_op jit(solution)/shard_map/all_to_all | solution.py:54
  277.9 5.5 copy-start.12
  277.9 187.4 %all-to-all-start.1 = ((f32[2,8,128,1024]{3,2,0,1:T(8,128)}), f32[2,8,128,1024]{3,2,0,1:T(8,128)}, u32[]{:S(2)}, u32[]{:S(2)}) async-start(f32[2,8,128,1024]{3,2,0,1:T(8,128)} %copy.151), calls=%async_computation.1 | async-start | bytes 16777216 | tf_op jit(solution)/shard_map/all_to_all | solution.py:76
  538.2 53.1 %all-to-all-start.2 = ((bf16[4,2,256,1024]{2,3,1,0:T(8,128)(2,1)}), bf16[4,2,256,1024]{2,3,1,0:T(8,128)(2,1)}, u32[]{:S(2)}, u32[]{:S(2)}) async-start(bf16[4,2,256,1024]{2,3,1,0:T(8,128)(2,1)} %select_select_fusion), calls=%async_computation.2 | async-start | bytes 8388608 | tf_op jit(solution)/shard_map/all_to_all | solution.py:107
  553.2 5.0 copy-start.11
  553.2 8.7 %copy-start.10 = (bf16[1,256,1024]{2,1,0:T(8,128)(2,1)S(1)}, bf16[1,256,1024]{2,1,0:T(8,128)(2,1)}, u32[]{:S(2)}) copy-start(bf16[1,256,1024]{2,1,0:T(8,128)(2,1)} %get-tuple-element.122) | copy-start | bytes 1572868
  554.7 11.8 %copy-start.9 = (bf16[1,256,1024]{2,1,0:T(8,128)(2,1)S(1)}, bf16[1,256,1024]{2,1,0:T(8,128)(2,1)}, u32[]{:S(2)}) copy-start(bf16[1,256,1024]{2,1,0:T(8,128)(2,1)} %get-tuple-element.119) | copy-start | bytes 1572868
  645.7 3.4 copy-start.2
  645.7 3.4 copy-start.6
  645.7 3.4 copy-start.8
  650.5 2.4 copy-start.1
  650.5 2.4 copy-start.4
  653.0 1.3 copy-start.5
  653.0 1.5 copy-start.7
  655.9 2.4 copy-start
  655.9 2.4 copy-start.3
where the time goes:
time: 702 us; the launch traced here: 695 us
  waiting for transfers between devices  290 us (41%)
  other arithmetic  167 us (24%)
  local copies, waits for them, and re-layouts  127 us (18%)
  matrix products  84.3 us (12%)
  starting transfers between devices  18.1 us (3%)
  between operations  8.34 us (1%)
    all_to_all x1, waiting for transfers between devices, local(): lax.all_to_all(stacked, 'chan', split_axis=1, concat_axis=2, tiled=True)  182 us
    add x16, other arithmetic, add_tap(): running + weight * lax.dynamic_slice_in_dim(samples, tap_index, spec_coun...  128 us
    all_to_all x1, waiting for transfers between devices, local(): lax.all_to_all(flat_rows, 'chan', split_axis=1, concat_axis=0, tiled=True)  92.9 us
    another operation x1, local copies, waits for them, and re-layouts, local(): return jnp.stack(results).astype(jnp.bfloat16)  28 us
    squeeze x6, local copies, waits for them, and re-layouts, correlate(): right_re = jnp.concatenate([their_four[0], their_four[1]], axis=-1)  21.9 us
    concatenate x3, local copies, waits for them, and re-layouts, correlate(): right_im = jnp.concatenate([-their_four[1], their_four[0]], axis=-1)  16.3 us
    squeeze x6, local copies, waits for them, and re-layouts, correlate(): left_side = jnp.concatenate([mine_four[0], mine_four[1]], axis=-1)  15.9 us
    all_to_all x1, waiting for transfers between devices, local(): lax.all_to_all(slot_data, 'grp', split_axis=0, concat_axis=0, tiled=True)  15.6 us
  transfers between devices with their start and end apart: 3, of which 3 were waited for; matrix products, arithmetic and copies ran while one was open for 4% of the time, Pallas kernels for 0%

commit v1 on v0

v1 whole, which is shorter than its diff:
```python
import functools
import math

import jax
import jax.numpy as jnp
import numpy as np
from jax import lax
from jax.experimental import pallas as pl
from jax.experimental.pallas import tpu as pltpu
from jax.sharding import PartitionSpec as P

TAPS = 16
LANES = 128
RADIX = 64
VMEM_LIMIT = 60 * 1024 * 1024


def tap_table(fft_len):
    position = np.arange(TAPS * fft_len, dtype=np.float64)
    total = TAPS * fft_len
    window = 0.5 - 0.5 * np.cos(2.0 * np.pi * position / total)
    return (window * np.sinc((position - 0.5 * total) / fft_len)).reshape(TAPS, fft_len)


def filter_kernel(chan_ref, volt_ref, coeff_ref, out_ref):
    del chan_ref
    frames, sig_tile, block_len = volt_ref.shape
    spec_count = frames - TAPS + 1

    def one_tile(tile, carry):
        cols = pl.ds(pl.multiple_of(tile * LANES, LANES), LANES)
        coeff = [
            jnp.broadcast_to(coeff_ref[0, t : t + 1, cols], (sig_tile, LANES)) for t in range(TAPS)
        ]
        total = [None] * spec_count
        for frame in range(frames):
            sample = volt_ref[frame, :, cols].astype(jnp.float32)
            for s in range(max(0, frame - TAPS + 1), min(spec_count - 1, frame) + 1):
                term = coeff[frame - s] * sample
                total[s] = term if total[s] is None else total[s] + term
            if frame >= TAPS - 1:
                s = frame - TAPS + 1
                out_ref[s, :, cols] = total[s].astype(jnp.bfloat16)
                total[s] = None
        return carry

    lax.fori_loop(0, block_len // LANES, one_tile, 0)


def filter_taps(frames_first, chan_id, chan_count):
    frames, sig_count, block_len = frames_first.shape
    spec_count = frames - TAPS + 1
    table = tap_table(block_len * chan_count).astype(np.float32)
    table = np.ascontiguousarray(table.reshape(TAPS, chan_count, block_len).transpose(1, 0, 2))
    sig_tile = 16
    return pl.pallas_call(
        filter_kernel,
        out_shape=jax.ShapeDtypeStruct((spec_count, sig_count, block_len), jnp.bfloat16),
        grid_spec=pltpu.PrefetchScalarGridSpec(
            num_scalar_prefetch=1,
            grid=(sig_count // sig_tile,),
            in_specs=[
                pl.BlockSpec((frames, sig_tile, block_len), lambda i, c: (0, i, 0)),
                pl.BlockSpec((1, TAPS, block_len), lambda i, c: (c[0], 0, 0)),
            ],
            out_specs=pl.BlockSpec((spec_count, sig_tile, block_len), lambda i, c: (0, i, 0)),
        ),
        compiler_params=pltpu.CompilerParams(vmem_limit_bytes=VMEM_LIMIT),
        name="filter_taps",
    )(chan_id.reshape(1), frames_first, jnp.asarray(table))


def cadd(a, b):
    if a is None:
        return b
    if b is None:
        return a
    return a + b


def csub(a, b):
    if b is None:
        return a
    if a is None:
        return -b
    return a - b


def scale_by(value, re, im):
    vr, vi = value
    eps = 1e-12

    def mul(x, f):
        if x is None or abs(f) < eps:
            return None
        if abs(f - 1.0) < eps:
            return x
        if abs(f + 1.0) < eps:
            return -x
        return x * f

    return csub(mul(vr, re), mul(vi, im)), cadd(mul(vr, im), mul(vi, re))


def plus(a, b):
    return cadd(a[0], b[0]), cadd(a[1], b[1])


def minus(a, b):
    return csub(a[0], b[0]), csub(a[1], b[1])


def dft(values, wanted=None):
    n = len(values)
    if n == 1:
        return list(values)
    even = dft(values[0::2])
    odd = dft(values[1::2])
    out = [None] * n
    for k in range(n // 2):
        if wanted is not None and k not in wanted and k + n // 2 not in wanted:
            continue
        angle = -2.0 * math.pi * k / n
        turned = scale_by(odd[k], math.cos(angle), math.sin(angle))
        out[k] = plus(even[k], turned)
        out[k + n // 2] = minus(even[k], turned)
    return out


def first_index_list():
    chosen = []
    for c in range(5):
        for e in range(8):
            k1 = c + 8 * e
            if c in (0, 4) and k1 > RADIX // 2:
                continue
            chosen.append(k1)
    return chosen


def turn_tables(fft_len):
    k1 = np.array(first_index_list())[:, None]
    angle = 2.0 * np.pi * ((k1 * np.arange(LANES)[None, :]) % fft_len) / fft_len
    return np.cos(angle), np.sin(angle)


def wave_matrix(fft_len):
    gain = 1.0 / (64.0 * math.sqrt(fft_len))
    half = LANES // 2
    n2 = np.arange(LANES)[None, :]
    k2 = np.arange(half)[:, None]
    rows = []
    for index, flip in ((k2, 1.0), (LANES - 1 - k2, -1.0)):
        angle = 2.0 * np.pi * ((index * n2) % LANES) / LANES
        cos, sin = np.cos(angle) * gain, np.sin(angle) * gain
        rows.append(np.concatenate([cos, sin], axis=1))
        rows.append(np.concatenate([-sin, cos], axis=1) * flip)
    return np.concatenate(rows, axis=0)


def split_two(value):
    high = value.astype(jnp.bfloat16)
    return high, (value - high.astype(jnp.float32)).astype(jnp.bfloat16)


def transform_kernel(
    chan_count, in_ref, cos_ref, sin_ref, wave_high_ref, wave_low_ref, out_ref, mid_ref, high_ref, low_ref
):
    _, rows, block_len = in_ref.shape
    per_block = block_len // LANES
    tile = 16
    chosen = first_index_list()

    def row_tile(step, carry):
        at = pl.ds(pl.multiple_of(step * tile, tile), tile)
        present = set()
        for low_n in range(8):
            column = []
            for high_n in range(8):
                n1 = high_n * 8 + low_n
                lanes = slice((n1 % per_block) * LANES, (n1 % per_block + 1) * LANES)
                column.append((in_ref[n1 // per_block, at, lanes].astype(jnp.float32), None))
            spread = dft(column, wanted=range(5))
            for c in range(5):
                angle = -2.0 * math.pi * low_n * c / RADIX
                re, im = scale_by(spread[c], math.cos(angle), math.sin(angle))
                for part, value in enumerate((re, im)):
                    if value is not None:
                        mid_ref[low_n, c, part] = value
                        present.add((low_n, c, part))
        for c in range(5):
            wanted = [e for e in range(8) if c + 8 * e in chosen]
            values = []
            for low_n in range(8):
                values.append(
                    tuple(
                        mid_ref[low_n, c, part] if (low_n, c, part) in present else None
                        for part in range(2)
                    )
                )
            spread = dft(values, wanted=wanted)
            for e in wanted:
                place = chosen.index(c + 8 * e)
                cos = cos_ref[place : place + 1, :]
                sin = sin_ref[place : place + 1, :]
                re, im = spread[e]
                if im is None:
                    turned_re, turned_im = re * cos, -(re * sin)
                else:
                    turned_re, turned_im = re * cos + im * sin, im * cos - re * sin
                a, b = split_two(turned_re)
                high_ref[place, at, :LANES] = a
                low_ref[place, at, :LANES] = b
                a, b = split_two(turned_im)
                high_ref[place, at, LANES:] = a
                low_ref[place, at, LANES:] = b
        return carry

    lax.fori_loop(0, rows // tile, row_tile, 0)

    dims = (((1,), (1,)), ((), ()))
    wave_high = wave_high_ref[...]
    wave_low = wave_low_ref[...]
    for first in range(0, len(chosen), 2):
        places = [p for p in (first, first + 1) if p < len(chosen)]
        high = high_ref[first : first + len(places)].reshape(len(places) * rows, 2 * LANES)
        low = low_ref[first : first + len(places)].reshape(len(places) * rows, 2 * LANES)
        total = lax.dot_general(wave_high, high, dims, preferred_element_type=jnp.float32)
        total += lax.dot_general(wave_high, low, dims, preferred_element_type=jnp.float32)
        total += lax.dot_general(wave_low, high, dims, preferred_element_type=jnp.float32)
        total = total.astype(jnp.bfloat16)
        for i, place in enumerate(places):
            k1 = chosen[place]
            columns = total[:, i * rows : (i + 1) * rows]
            quarter = LANES // 4
            for side, index in ((0, k1), (1, RADIX - k1)):
                if side == 1 and (k1 == 0 or k1 == RADIX // 2):
                    continue
                for part in range(2):
                    for half in range(2):
                        at = side * LANES + part * 2 * quarter + half * quarter
                        out_ref[index % chan_count, half, index // chan_count, part] = columns[
                            at : at + quarter
                        ]


def transform(samples):
    chan_count, rows, block_len = samples.shape
    fft_len = chan_count * block_len
    count = len(first_index_list())
    cos, sin = turn_tables(fft_len)
    wave = wave_matrix(fft_len)
    wave_high = wave.astype(jnp.bfloat16)
    wave_low = (wave - wave_high.astype(np.float64)).astype(jnp.bfloat16)
    tables = (
        jnp.asarray(cos, jnp.float32),
        jnp.asarray(sin, jnp.float32),
        jnp.asarray(wave_high),
        jnp.asarray(wave_low),
    )
    whole = pl.BlockSpec(memory_space=pltpu.VMEM)
    return pl.pallas_call(
        functools.partial(transform_kernel, chan_count),
        out_shape=jax.ShapeDtypeStruct(
            (chan_count, 2, RADIX // chan_count, 2, LANES // 4, rows), jnp.bfloat16
        ),
        in_specs=[whole] * 5,
        out_specs=whole,
        scratch_shapes=[
            pltpu.VMEM((8, 5, 2, 16, LANES), jnp.float32),
            pltpu.VMEM((count, rows, 2 * LANES), jnp.bfloat16),
            pltpu.VMEM((count, rows, 2 * LANES), jnp.bfloat16),
        ],
        compiler_params=pltpu.CompilerParams(vmem_limit_bytes=VMEM_LIMIT),
        name="transform",
    )(samples, *tables)


def correlate(mine, theirs):
    left = mine.reshape(*mine.shape[:2], -1)
    right_re = theirs.reshape(left.shape)
    right_im = jnp.stack([-theirs[..., 1], theirs[..., 0]], axis=-1).reshape(left.shape)
    vis_re = jnp.einsum("kas,kbs->akb", left, right_re, preferred_element_type=jnp.float32)
    vis_im = jnp.einsum("kas,kbs->akb", left, right_im, preferred_element_type=jnp.float32)
    return jnp.concatenate([vis_re, vis_im], axis=-1) * (1.0 / mine.shape[2])


def by_channel(half, sig_count, spec_count):
    chan_count, per, parts, k2, rows = half.shape
    turned = half.transpose(3, 1, 0, 4, 2).reshape(k2 * per, spec_count, sig_count, parts)
    return turned.transpose(0, 2, 1, 3)


def local(voltages, plan):
    sig_count, frames, block_len = voltages.shape
    chan_count = lax.axis_size("chan")
    group_count = lax.axis_size("grp")
    spec_count = frames - TAPS + 1
    rows = spec_count * sig_count // chan_count
    chan_id = lax.axis_index("chan").astype(jnp.int32)
    group_id = lax.axis_index("grp")

    filtered = filter_taps(voltages.transpose(1, 0, 2), chan_id, chan_count)
    filtered = filtered.reshape(chan_count, rows, block_len)
    frames_here = lax.all_to_all(filtered, "chan", split_axis=0, concat_axis=0, tiled=True)
    spectra = transform(frames_here)
    channel = lax.all_to_all(spectra, "chan", split_axis=0, concat_axis=0, tiled=True)

    lower_half, upper_half = channel[:, 0], channel[:, 1]
    group_ids = jnp.arange(group_count)
    partner = jnp.sum(jnp.where(group_ids[None, :] == group_id, plan, 0), axis=1)
    listed = jnp.any(partner[:, None] == group_ids[None, :], axis=0)
    slot_shape = (group_count,) + (1,) * lower_half.ndim
    chosen_half = jnp.where(
        (group_ids > group_id).reshape(slot_shape), upper_half[None], lower_half[None]
    )
    slots = jnp.where(listed.reshape(slot_shape), chosen_half, jnp.zeros_like(chosen_half))
    received = lax.all_to_all(slots, "grp", split_axis=0, concat_axis=0, tiled=True)
    results = []
    for round_index in range(plan.shape[0]):
        partner_id = partner[round_index]
        upper_flag = (group_id > partner_id).astype(jnp.int32)
        mine = lax.dynamic_index_in_dim(channel, upper_flag, 1, keepdims=False)
        theirs = lax.dynamic_index_in_dim(received, partner_id, 0, keepdims=False)
        results.append(
            correlate(
                by_channel(mine, sig_count, spec_count), by_channel(theirs, sig_count, spec_count)
            )
        )
    return jnp.stack(results).astype(jnp.bfloat16)


def solution(mesh):
    in_specs = (P("grp", None, "chan"), P())
    out_specs = P(None, "grp", "chan", None)
    return jax.shard_map(local, mesh=mesh, in_specs=in_specs, out_specs=out_specs, check_vma=False)
```

time: 702 us -> 286 us (0.41)
  waiting for transfers between devices: 290 us -> 72.2 us
  other arithmetic: 167 us -> 22 us
  matrix products: 84.3 us -> 17.9 us
  blocking collectives: 0 us -> 55.6 us
  local copies, waits for them, and re-layouts: 127 us -> 79.5 us
  Pallas kernels: 0 us -> 16 us
  starting transfers between devices: 18.1 us -> 8.95 us
    all_to_all x3 -> x2, waiting for transfers between devices: 290 us -> 72.2 us  [the longest x1 45 us: local(): lax.all_to_all(spectra, 'chan', split_axis=0, concat_axis=0, tiled=True)]
    add x18 -> x0, other arithmetic: 128 us -> none  [the longest x16 128 us: add_tap(): running + weight * lax.dynamic_slice_in_dim(samples, tap_index, spec_coun...]
    dot_general x12 -> x6, matrix products: 84.3 us -> 17.9 us  [the longest x3 10.6 us: correlate(): jnp.einsum('kas,kbs->akb', left, right_re, preferred_element_type=jnp.flo...]
    all_to_all x0 -> x1, blocking collectives: none -> 55.6 us  [local(): lax.all_to_all(filtered, 'chan', split_axis=0, concat_axis=0, tiled=True)]
    squeeze x12 -> x0, local copies, waits for them, and re-layouts: 37.8 us -> none  [the longest x6 21.9 us: correlate(): right_re = jnp.concatenate([their_four[0], their_four[1]], axis=-1)]
    transpose x0 -> x11, local copies, waits for them, and re-layouts: none -> 29.7 us  [the longest x6 21 us: by_channel(): return turned.transpose(0, 2, 1, 3)]
    slice x12 -> x0, local copies, waits for them, and re-layouts: 21.2 us -> none  [the longest x7 8.06 us: correlate(): left_side = jnp.concatenate([mine_four[0], mine_four[1]], axis=-1)]
    concatenate x3 -> x0, local copies, waits for them, and re-layouts: 16.3 us -> none  [correlate(): right_im = jnp.concatenate([-their_four[1], their_four[0]], axis=-1)]
  transfers between devices with their start and end apart: 3 -> 2, of which waited for: 3 -> 2; matrix products, arithmetic and copies ran while one was open for 4% -> 6% of each run, Pallas kernels for 0% -> 0%
where the time goes in v1:
time: 286 us; the launch traced here: 281 us
  local copies, waits for them, and re-layouts  79.5 us (28%)
  waiting for transfers between devices  72.2 us (25%)
  blocking collectives  55.6 us (19%)
  other arithmetic  22 us (8%)
  matrix products  17.9 us (6%)
  Pallas kernels  16 us (6%)
  starting transfers between devices  8.95 us (3%)
  between operations  8.34 us (3%)
    all_to_all x1, blocking collectives, local(): lax.all_to_all(filtered, 'chan', split_axis=0, concat_axis=0, tiled=True)  55.6 us
    all_to_all x1, waiting for transfers between devices, local(): lax.all_to_all(spectra, 'chan', split_axis=0, concat_axis=0, tiled=True)  45 us
    another operation x1, local copies, waits for them, and re-layouts, local(): return jnp.stack(results).astype(jnp.bfloat16)  28.2 us
    all_to_all x1, waiting for transfers between devices, local(): lax.all_to_all(slots, 'grp', split_axis=0, concat_axis=0, tiled=True)  27.1 us
    transpose x6, local copies, waits for them, and re-layouts, by_channel(): return turned.transpose(0, 2, 1, 3)  21 us
    another operation x3, other arithmetic  11.8 us
    dot_general x3, matrix products, correlate(): jnp.einsum('kas,kbs->akb', left, right_re, preferred_element_type=jnp.flo...  10.6 us
    reshape x6, local copies, waits for them, and re-layouts, by_channel(): half.transpose(3, 1, 0, 4, 2)  9.29 us
  transfers between devices with their start and end apart: 2, of which 2 were waited for; matrix products, arithmetic and copies ran while one was open for 6% of the time, Pallas kernels for 0%

profile of v1, /device:TPU:0, one launch (start us, length us, event | category | flops | bytes accessed | tf_op | source)
XLA Modules:
  0.0 280.6 jit_solution(17352667340123386156)
XLA Ops:
  0.0 8.2 %filter_taps.1 = bf16[16,64,1024]{2,1,0:T(8,128)(2,1)} custom-call(s32[1]{0:T(128)} %bitcast.chan_ref, s32[31,64,1024]{2,1,0:T(8,128)} %bitcast.131, f32[8,16,1024]{2,1,0:T(8,128)} %constant.44.clone.coeff_ref), custom_call_target="tpu_custom_call" | custom-call | tf_op jit(solution)/shard_map/filter_taps/pallas_call | solution.py:56
  8.2 55.6 %all_to_all.15.in_ref = bf16[8,128,1024]{2,1,0:T(8,128)(2,1)} all-to-all(bf16[8,128,1024]{2,1,0:T(8,128)(2,1)} %bitcast.128), channel_id=1, replica_groups=mesh['grp'=4,'chan'=8] {'chan'}, dimensions={0} | all-to-all | bytes 4194304 | tf_op jit(solution)/shard_map/all_to_all | solution.py:305
  63.8 7.8 %transform.1 = bf16[8,2,8,2,32,128]{5,4,3,2,1,0:T(8,128)(2,1)} custom-call(bf16[8,128,1024]{2,1,0:T(8,128)(2,1)} %all_to_all.15.in_ref, f32[33,128]{1,0:T(8,128)} %constant.45.clone.cos_ref, f32[33,128]{1,0:T(8,128)} %constant.46.clone.sin_ref, bf16[256,256]{1,0:T(8,128)(2,1)} %constant.47.clone.wave_high_ref, bf16[256,256]{1,0:T(8,128)(2,1)} %constant.48.clone.wave_low_ref), custom_call_target="tpu_custom_call" | custom-call | tf_op jit(solution)/shard_map/transform/pallas_call | solution.py:262
  71.6 3.7 %all-to-all-start.1 = ((bf16[8,2,8,2,32,128]{5,4,3,2,1,0:T(8,128)(2,1)}), bf16[8,2,8,2,32,128]{5,4,3,2,1,0:T(8,128)(2,1)S(1)}, u32[]{:S(2)}, u32[]{:S(2)}) async-start(bf16[8,2,8,2,32,128]{5,4,3,2,1,0:T(8,128)(2,1)} %transform.1), calls=%async_computation.1 | async-start | bytes 4194304 | tf_op jit(solution)/shard_map/all_to_all | solution.py:307
  78.2 45.0 %all-to-all-done.1 = bf16[8,2,8,2,32,128]{5,4,3,2,1,0:T(8,128)(2,1)S(1)} async-done(((bf16[8,2,8,2,32,128]{5,4,3,2,1,0:T(8,128)(2,1)}), bf16[8,2,8,2,32,128]{5,4,3,2,1,0:T(8,128)(2,1)S(1)}, u32[]{:S(2)}, u32[]{:S(2)}) %all-to-all-start.1) | async-done | bytes 2097184 | tf_op jit(solution)/shard_map/all_to_all | solution.py:307
  127.1 2.6 select_select_fusion
  129.7 5.2 %all-to-all-start.2 = ((bf16[4,8,8,2,32,128]{5,1,3,2,4,0:T(8,128)(2,1)}), bf16[4,8,8,2,32,128]{5,1,3,2,4,0:T(8,128)(2,1)}, u32[]{:S(2)}, u32[]{:S(2)}) async-start(bf16[4,8,8,2,32,128]{5,1,3,2,4,0:T(8,128)(2,1)} %select_select_fusion), calls=%async_computation.2 | async-start | bytes 8388608 | tf_op jit(solution)/shard_map/all_to_all | solution.py:318
  142.3 3.5 %copy.40 = bf16[256,64,16,2]{1,3,2,0:T(2,128)(2,1)} copy(bf16[256,64,16,2]{1,2,3,0:T(8,128)(2,1)S(1)} %bitcast.121) | data formatting | bytes 2097152 | tf_op jit(solution)/shard_map/transpose | solution.py:291
  147.4 3.5 %copy.44 = bf16[256,64,16,2]{1,3,2,0:T(2,128)(2,1)} copy(bf16[256,64,16,2]{1,2,3,0:T(8,128)(2,1)S(1)} %bitcast.122) | data formatting | bytes 2097152 | tf_op jit(solution)/shard_map/transpose | solution.py:291
  152.4 3.6 %copy.48 = bf16[256,64,16,2]{1,3,2,0:T(2,128)(2,1)} copy(bf16[256,64,16,2]{1,2,3,0:T(8,128)(2,1)S(1)} %bitcast.123) | data formatting | bytes 2097152 | tf_op jit(solution)/shard_map/transpose | solution.py:291
  156.0 27.1 %all-to-all-done.2 = bf16[4,8,8,2,32,128]{5,1,3,2,4,0:T(8,128)(2,1)} async-done(((bf16[4,8,8,2,32,128]{5,1,3,2,4,0:T(8,128)(2,1)}), bf16[4,8,8,2,32,128]{5,1,3,2,4,0:T(8,128)(2,1)}, u32[]{:S(2)}, u32[]{:S(2)}) %all-to-all-start.2) | async-done | bytes 4194336 | tf_op jit(solution)/shard_map/all_to_all | solution.py:318
  183.1 4.1 %dynamic-slice_bitcast_fusion.5 = (bf16[32,8,8,128,2]{3,2,4,1,0:T(8,128)(2,1)}, bf16[32,8,8,128,2]{3,2,4,1,0:T(8,128)(2,1)S(1)}, bf16[32,8,8,128,2]{3,2,4,1,0:T(8,128)(2,1)}) fusion(bf16[4,8,8,2,32,128]{5,1,3,2,4,0:T(8,128)(2,1)} %all-to-all-done.2, s32[]{:T(128)S(6)} %select_n.35, s32[]{:T(128)S(6)} %select_n.39, s32[]{:T(128)S(6)} %select_n.37), kind=kLoop, calls=%fused_computation.27 | loop fusion | bytes 6291468 | tf_op jit(solution)/shard_map/transpose | solution.py:290
  187.1 3.2 %reshape.155 = bf16[256,16,64,2]{2,1,3,0:T(8,128)(2,1)S(1)} reshape(bf16[32,8,8,128,2]{3,2,4,1,0:T(8,128)(2,1)} %get-tuple-element.5) | data formatting | bytes 2097152 | tf_op jit(solution)/shard_map/reshape | solution.py:290
  191.9 3.5 %copy.38 = bf16[256,64,16,2]{1,3,2,0:T(2,128)(2,1)} copy(bf16[256,64,16,2]{1,2,3,0:T(8,128)(2,1)S(1)} %bitcast.110) | data formatting | bytes 2097152 | tf_op jit(solution)/shard_map/transpose | solution.py:291
  195.4 2.7 reshape.160
  199.6 3.5 %copy.42 = bf16[256,64,16,2]{1,3,2,0:T(2,128)(2,1)} copy(bf16[256,64,16,2]{1,2,3,0:T(8,128)(2,1)S(1)} %bitcast.112) | data formatting | bytes 2097152 | tf_op jit(solution)/shard_map/transpose | solution.py:291
  203.9 3.5 %copy.46 = bf16[256,64,16,2]{1,3,2,0:T(2,128)(2,1)} copy(bf16[256,64,16,2]{1,2,3,0:T(8,128)(2,1)S(1)} %bitcast.113) | data formatting | bytes 2097152 | tf_op jit(solution)/shard_map/transpose | solution.py:291
  219.7 4.8 %convolution_bitcast_fusion.3 = f32[1,64,256,64]{3,1,2,0:T(8,128)} fusion(bf16[256,64,32]{1,2,0:T(8,128)(2,1)S(1)} %bitcast.125, bf16[256,64,32]{1,2,0:T(8,128)(2,1)S(1)} %bitcast.118), kind=kOutput, calls=%fused_computation.11 | convolution fusion | flops 67108864 | bytes 6291456 | tf_op jit(solution)/shard_map/kas,kbs->akb/dot_general | solution.py:283
  224.9 3.5 %copy.49 = bf16[256,64,16,2]{1,3,2,0:T(2,128)(2,1)} copy(bf16[256,64,16,2]{1,2,3,0:T(8,128)(2,1)S(1)} %pad_maximum_fusion.3) | data formatting | bytes 2097152 | tf_op jit(solution)/shard_map/stack | solution.py:282
  228.3 4.5 %convolution_bitcast_fusion.1 = f32[1,64,256,64]{3,1,2,0:T(8,128)} fusion(bf16[256,64,32]{1,2,0:T(8,128)(2,1)S(1)} %bitcast.124, bf16[256,64,32]{1,2,0:T(8,128)(2,1)S(1)} %bitcast.115), kind=kOutput, calls=%fused_computation.9 | convolution fusion | flops 67108864 | bytes 6291456 | tf_op jit(solution)/shard_map/kas,kbs->akb/dot_general | solution.py:283
  232.9 4.7 %convolution_bitcast_fusion = f32[1,64,256,64]{3,1,2,0:T(8,128)} fusion(bf16[256,64,32]{1,2,0:T(8,128)(2,1)S(1)} %bitcast.127, bf16[256,64,32]{1,2,0:T(8,128)(2,1)S(1)} %bitcast.116), kind=kOutput, calls=%fused_computation.8 | convolution fusion | flops 67108864 | bytes 6291456 | tf_op jit(solution)/shard_map/kas,kbs->akb/dot_general | solution.py:284
  240.0 4.8 %fusion.1 = bf16[1,64,256,128]{3,1,2,0:T(8,128)(2,1)S(1)} fusion(f32[1,64,256,64]{3,1,2,0:T(8,128)S(1)} %convolution_bitcast_fusion.2, f32[1,64,256,64]{3,1,2,0:T(8,128)} %convolution_bitcast_fusion.3), kind=kLoop, calls=%fused_computation.4 | loop fusion | flops 6291456 | bytes 12582912 | tf_op jit(solution)/shard_map/convert.1
  245.8 4.6 %fusion.2 = bf16[1,64,256,128]{3,1,2,0:T(8,128)(2,1)S(1)} fusion(f32[1,64,256,64]{3,1,2,0:T(8,128)S(1)} %copy-done, f32[1,64,256,64]{3,1,2,0:T(8,128)} %convolution_bitcast_fusion.1), kind=kLoop, calls=%fused_computation.6 | loop fusion | flops 6291456 | bytes 12582912 | tf_op jit(solution)/shard_map/convert.2
  252.1 28.2 %copy.50 = bf16[3,64,256,128]{3,2,1,0:T(8,128)(2,1)} copy(bf16[3,64,256,128]{3,1,2,0:T(8,128)(2,1)S(1)} %pad_maximum_fusion) | data formatting | bytes 25165824 | tf_op jit(solution)/shard_map/stack | solution.py:330
  (63 shorter events, 30.8 us)
Async XLA Ops:
  71.6 3.8 %copy-start.17 = (s32[3,4]{1,0:T(4,128)S(1)}, s32[3,4]{1,0:T(4,128)}, u32[]{:S(2)}) copy-start(s32[3,4]{1,0:T(4,128)} %param.8) | copy-start | bytes 148
  71.6 51.6 %all-to-all-start.1 = ((bf16[8,2,8,2,32,128]{5,4,3,2,1,0:T(8,128)(2,1)}), bf16[8,2,8,2,32,128]{5,4,3,2,1,0:T(8,128)(2,1)S(1)}, u32[]{:S(2)}, u32[]{:S(2)}) async-start(bf16[8,2,8,2,32,128]{5,4,3,2,1,0:T(8,128)(2,1)} %transform.1), calls=%async_computation.1 | async-start | bytes 4194304 | tf_op jit(solution)/shard_map/all_to_all | solution.py:307
  129.7 11.1 %copy-start.16 = (bf16[32,8,8,128,2]{3,0,4,1,2:T(8,128)(2,1)S(1)}, bf16[32,8,8,128,2]{3,0,4,1,2:T(8,128)(2,1)}, u32[]{:S(2)}) copy-start(bf16[32,8,8,128,2]{3,0,4,1,2:T(8,128)(2,1)} %get-tuple-element.8) | copy-start | bytes 3145732
  129.7 53.4 %all-to-all-start.2 = ((bf16[4,8,8,2,32,128]{5,1,3,2,4,0:T(8,128)(2,1)}), bf16[4,8,8,2,32,128]{5,1,3,2,4,0:T(8,128)(2,1)}, u32[]{:S(2)}, u32[]{:S(2)}) async-start(bf16[4,8,8,2,32,128]{5,1,3,2,4,0:T(8,128)(2,1)} %select_select_fusion), calls=%async_computation.2 | async-start | bytes 8388608 | tf_op jit(solution)/shard_map/all_to_all | solution.py:318
  142.3 3.5 %copy-start.15 = (bf16[32,8,8,128,2]{3,0,4,1,2:T(8,128)(2,1)S(1)}, bf16[32,8,8,128,2]{3,0,4,1,2:T(8,128)(2,1)}, u32[]{:S(2)}) copy-start(bf16[32,8,8,128,2]{3,0,4,1,2:T(8,128)(2,1)} %get-tuple-element.10) | copy-start | bytes 3145732
  147.4 3.5 %copy-start.14 = (bf16[32,8,8,128,2]{3,0,4,1,2:T(8,128)(2,1)S(1)}, bf16[32,8,8,128,2]{3,0,4,1,2:T(8,128)(2,1)}, u32[]{:S(2)}) copy-start(bf16[32,8,8,128,2]{3,0,4,1,2:T(8,128)(2,1)} %get-tuple-element.9) | copy-start | bytes 3145732
  207.4 1.6 copy-start.12
  207.4 2.3 copy-start.13
  210.1 2.2 copy-start.3
  212.3 1.6 copy-start.6
  213.9 1.3 copy-start.10
  213.9 1.5 copy-start.11
  215.9 2.2 copy-start.2
  218.1 1.6 copy-start.5
  219.7 4.8 %copy-start.8 = (bf16[256,64,16,1]{1,2,3,0:T(8,128)(2,1)S(1)}, bf16[256,64,16,1]{1,2,3,0:T(8,128)(2,1)}, u32[]{:S(2)}) copy-start(bf16[256,64,16,1]{1,2,3,0:T(8,128)(2,1)} %get-tuple-element.17) | copy-start | bytes 1572868
  219.7 4.8 %copy-start.9 = (bf16[256,64,16,1]{1,2,3,0:T(8,128)(2,1)S(1)}, bf16[256,64,16,1]{1,2,3,0:T(8,128)(2,1)}, u32[]{:S(2)}) copy-start(bf16[256,64,16,1]{1,2,3,0:T(8,128)(2,1)} %get-tuple-element.18) | copy-start | bytes 1572868
  224.8 3.5 %copy-start.1 = (bf16[256,64,16,2]{1,3,2,0:T(2,128)(2,1)S(1)}, bf16[256,64,16,2]{1,3,2,0:T(2,128)(2,1)}, u32[]{:S(2)}) copy-start(bf16[256,64,16,2]{1,3,2,0:T(2,128)(2,1)} %copy.48) | copy-start | bytes 3145732
  224.8 3.5 %copy-start.4 = (bf16[256,64,16,2]{1,3,2,0:T(2,128)(2,1)S(1)}, bf16[256,64,16,2]{1,3,2,0:T(2,128)(2,1)}, u32[]{:S(2)}) copy-start(bf16[256,64,16,2]{1,3,2,0:T(2,128)(2,1)} %copy.46) | copy-start | bytes 3145732
  228.3 4.5 %copy-start.7 = (bf16[256,64,16,2]{1,3,2,0:T(2,128)(2,1)S(1)}, bf16[256,64,16,2]{1,3,2,0:T(2,128)(2,1)}, u32[]{:S(2)}) copy-start(bf16[256,64,16,2]{1,3,2,0:T(2,128)(2,1)} %copy.49) | copy-start | bytes 3145732
  240.0 5.8 %copy-start = (f32[1,64,256,64]{3,1,2,0:T(8,128)S(1)}, f32[1,64,256,64]{3,1,2,0:T(8,128)}, u32[]{:S(2)}) copy-start(f32[1,64,256,64]{3,1,2,0:T(8,128)} %convolution_bitcast_fusion) | copy-start | bytes 12582916

commit v2 on v1

--- a/solution.py
+++ b/solution.py
@@ -276,7 +276,119 @@
     )(samples, *tables)
 
 
-def correlate(mine, theirs):
+def correlate_kernel(
+    sig_count, spec_count, halves_ref, mates_ref, mine_ref, mate_ref, out_ref, left_ref, right_ref, sum_ref
+):
+    del halves_ref, mates_ref
+    chan_count, _, per, parts, k2_tile, lanes = mine_ref.shape
+    depth = 2 * parts * chan_count
+    channels = per * k2_tile
+    eight = 8
+    low_lanes = lax.broadcasted_iota(jnp.int32, (eight, lanes), 1) < sig_count
+
+    def roll(value):
+        return pltpu.roll(value, sig_count, 1)
+
+    def spread(step, carry):
+        source = step // per
+        e = step % per
+        for k2 in range(0, k2_tile, eight):
+            at = pl.ds(k2, eight)
+            channel = e * k2_tile + k2
+
+            def put(ref, spectrum, part, value):
+                row = channel * depth + (spectrum * chan_count + source) * parts + part
+                ref[pl.ds(row, eight, stride=depth), :] = value
+
+            left_re = mine_ref[source, 0, e, 0, at, :].astype(jnp.float32)
+            left_im = mine_ref[source, 0, e, 1, at, :].astype(jnp.float32)
+            put(left_ref, 0, 0, left_re)
+            put(left_ref, 0, 1, left_im)
+            put(left_ref, 1, 0, roll(left_re))
+            put(left_ref, 1, 1, roll(left_im))
+            right_re = mate_ref[0, source, e, 0, at, :].astype(jnp.float32)
+            right_im = mate_ref[0, source, e, 1, at, :].astype(jnp.float32)
+            turned_re, turned_im = roll(right_re), roll(right_im)
+            put(right_ref, 0, 0, jnp.where(low_lanes, right_re, -turned_im))
+            put(right_ref, 0, 1, jnp.where(low_lanes, right_im, turned_re))
+            put(right_ref, 1, 0, jnp.where(low_lanes, turned_re, -right_im))
+            put(right_ref, 1, 1, jnp.where(low_lanes, turned_im, right_re))
+        return carry
+
+    lax.fori_loop(0, chan_count * per, spread, 0)
+
+    def pair(step, carry):
+        e = step // (k2_tile // 2)
+        k2 = (step % (k2_tile // 2)) * 2
+        first = pl.multiple_of((e * k2_tile + k2) * depth, 2 * depth)
+        left = left_ref[pl.ds(first, 2 * depth), :].T[:sig_count].astype(jnp.bfloat16)
+        right = right_ref[pl.ds(first, 2 * depth), :].astype(jnp.bfloat16)
+        zero = jnp.zeros((depth, lanes), jnp.bfloat16)
+        weights = jnp.concatenate(
+            [
+                jnp.concatenate([right[:depth], zero], axis=1),
+                jnp.concatenate([zero, right[depth:]], axis=1),
+            ],
+            axis=0,
+        )
+        both = jnp.dot(left, weights, preferred_element_type=jnp.float32)
+        for i in range(2):
+            q = e + per * (k2 + i)
+            for a in range(0, sig_count, eight):
+                sum_ref[pl.ds(a * channels + q, eight, stride=channels), :] = both[
+                    a : a + eight, i * lanes : (i + 1) * lanes
+                ]
+        return carry
+
+    lax.fori_loop(0, channels // 2, pair, 0, unroll=4)
+
+    def finish(a, carry):
+        rows = pl.ds(pl.multiple_of(a * channels, channels), channels)
+        out_ref[0, a] = (sum_ref[rows, :] * (1.0 / spec_count)).astype(jnp.bfloat16)
+        return carry
+
+    lax.fori_loop(0, sig_count, finish, 0)
+
+
+def correlate(mine, theirs, halves, mates, sig_count, spec_count):
+    chan_count, _, per, parts, k2_count, lanes = mine.shape
+    rounds = halves.shape[0]
+    k2_tile = 16
+    channels = per * k2_tile
+    depth = 2 * parts * chan_count
+    return pl.pallas_call(
+        functools.partial(correlate_kernel, sig_count, spec_count),
+        out_shape=jax.ShapeDtypeStruct(
+            (rounds, sig_count, per * k2_count, 2 * sig_count), jnp.bfloat16
+        ),
+        grid_spec=pltpu.PrefetchScalarGridSpec(
+            num_scalar_prefetch=2,
+            grid=(rounds, k2_count // k2_tile),
+            in_specs=[
+                pl.BlockSpec(
+                    (chan_count, 1, per, parts, k2_tile, lanes),
+                    lambda r, i, h, m: (0, h[r], 0, 0, i, 0),
+                ),
+                pl.BlockSpec(
+                    (1, chan_count, per, parts, k2_tile, lanes),
+                    lambda r, i, h, m: (m[r], 0, 0, 0, i, 0),
+                ),
+            ],
+            out_specs=pl.BlockSpec(
+                (1, sig_count, channels, 2 * sig_count), lambda r, i, h, m: (r, 0, i, 0)
+            ),
+            scratch_shapes=[
+                pltpu.VMEM((channels * depth, lanes), jnp.float32),
+                pltpu.VMEM((channels * depth, lanes), jnp.float32),
+                pltpu.VMEM((sig_count * channels, lanes), jnp.float32),
+            ],
+        ),
+        compiler_params=pltpu.CompilerParams(vmem_limit_bytes=VMEM_LIMIT),
+        name="correlate",
+    )(halves, mates, mine, theirs)
+
+
+def correlate_plain(mine, theirs):
     left = mine.reshape(*mine.shape[:2], -1)
     right_re = theirs.reshape(left.shape)
     right_im = jnp.stack([-theirs[..., 1], theirs[..., 0]], axis=-1).reshape(left.shape)
@@ -316,14 +428,15 @@
     )
     slots = jnp.where(listed.reshape(slot_shape), chosen_half, jnp.zeros_like(chosen_half))
     received = lax.all_to_all(slots, "grp", split_axis=0, concat_axis=0, tiled=True)
+    halves = (group_id > partner).astype(jnp.int32)
+    if rows == LANES and rows == 2 * sig_count:
+        return correlate(channel, received, halves, partner, sig_count, spec_count)
     results = []
     for round_index in range(plan.shape[0]):
-        partner_id = partner[round_index]
-        upper_flag = (group_id > partner_id).astype(jnp.int32)
-        mine = lax.dynamic_index_in_dim(channel, upper_flag, 1, keepdims=False)
-        theirs = lax.dynamic_index_in_dim(received, partner_id, 0, keepdims=False)
+        mine = lax.dynamic_index_in_dim(channel, halves[round_index], 1, keepdims=False)
+        theirs = lax.dynamic_index_in_dim(received, partner[round_index], 0, keepdims=False)
         results.append(
-            correlate(
+            correlate_plain(
                 by_channel(mine, sig_count, spec_count), by_channel(theirs, sig_count, spec_count)
             )
         )

time: 286 us -> 269 us (0.941); the launches traced: 281 us -> 268 us
  Pallas kernels: 16 us -> 105 us
  local copies, waits for them, and re-layouts: 79.5 us -> 0.47 us
  waiting for transfers between devices: 72.2 us -> 95.3 us
  other arithmetic: 22 us -> 3.31 us
  matrix products: 17.9 us -> 0 us
  between operations: 8.34 us -> 0.07 us
    pallas_call x0 -> x1, Pallas kernels: none -> 88.9 us  [correlate(): pl.pallas_call(functools.partial(correlate_kernel, sig_count, spec_count)...]
    another operation x4 -> x0, local copies, waits for them, and re-layouts: 36 us -> none  [the longest x1 28.2 us: local(): return jnp.stack(results).astype(jnp.bfloat16)]
    transpose x11 -> x0, local copies, waits for them, and re-layouts: 29.7 us -> none  [the longest x6 21 us: by_channel(): return turned.transpose(0, 2, 1, 3)]
    all_to_all x1, waiting for transfers between devices: 27.1 us -> 47.6 us  [local(): lax.all_to_all(slots, 'grp', split_axis=0, concat_axis=0, tiled=True)]
    dot_general x6 -> x0, matrix products: 17.9 us -> none  [the longest x3 10.6 us: correlate(): jnp.einsum('kas,kbs->akb', left, right_re, preferred_element_type=jnp.flo...]
    another operation x7 -> x0, other arithmetic: 14.6 us -> none
    reshape x6 -> x0, local copies, waits for them, and re-layouts: 9.29 us -> none  [by_channel(): half.transpose(3, 1, 0, 4, 2)]
    neg x3 -> x0, other arithmetic: 4.62 us -> none  [correlate(): -theirs[..., 1]]
  transfers between devices with their start and end apart: 2 -> 2, of which waited for: 2 -> 2; matrix products, arithmetic and copies ran while one was open for 6% -> 0% of each run, Pallas kernels for 0% -> 0%
where the time goes in v2:
time: 269 us; the launch traced here: 268 us
  Pallas kernels  105 us (39%)
  waiting for transfers between devices  95.3 us (35%)
  blocking collectives  55.6 us (21%)
  starting transfers between devices  8.45 us (3%)
  other arithmetic  3.31 us (1%)
    pallas_call x1, Pallas kernels, correlate(): pl.pallas_call(functools.partial(correlate_kernel, sig_count, spec_count)...  88.9 us
    all_to_all x1, blocking collectives, local(): lax.all_to_all(filtered, 'chan', split_axis=0, concat_axis=0, tiled=True)  55.6 us
    all_to_all x1, waiting for transfers between devices, local(): lax.all_to_all(slots, 'grp', split_axis=0, concat_axis=0, tiled=True)  47.6 us
    all_to_all x1, waiting for transfers between devices, local(): lax.all_to_all(spectra, 'chan', split_axis=0, concat_axis=0, tiled=True)  47.6 us
    pallas_call x1, Pallas kernels, filter_taps(): pl.pallas_call(filter_kernel, out_shape=jax.ShapeDtypeStruct((spec_count,...  8.18 us
    pallas_call x1, Pallas kernels, transform(): pl.pallas_call(functools.partial(transform_kernel, chan_count), out_shape...  7.79 us
  transfers between devices with their start and end apart: 2, of which 2 were waited for; matrix products, arithmetic and copies ran while one was open for 0% of the time, Pallas kernels for 0%

profile of v2, /device:TPU:0, one launch (start us, length us, event | category | flops | bytes accessed | tf_op | source)
XLA Modules:
  0.0 268.1 jit_solution(2877127810375304152)
XLA Ops:
  0.0 8.2 %filter_taps.1 = bf16[16,64,1024]{2,1,0:T(8,128)(2,1)} custom-call(s32[1]{0:T(128)} %bitcast.chan_ref, s32[31,64,1024]{2,1,0:T(8,128)} %bitcast.8, f32[8,16,1024]{2,1,0:T(8,128)} %constant.24.clone.coeff_ref), custom_call_target="tpu_custom_call" | custom-call | tf_op jit(solution)/shard_map/filter_taps/pallas_call | solution.py:56
  8.2 55.6 %all_to_all.15.in_ref = bf16[8,128,1024]{2,1,0:T(8,128)(2,1)} all-to-all(bf16[8,128,1024]{2,1,0:T(8,128)(2,1)} %bitcast.7), channel_id=1, replica_groups=mesh['grp'=4,'chan'=8] {'chan'}, dimensions={0} | all-to-all | bytes 4194304 | tf_op jit(solution)/shard_map/all_to_all | solution.py:417
  63.8 0.0 copy-start.2
  63.8 7.8 %transform.1 = bf16[8,2,8,2,32,128]{5,4,3,2,1,0:T(8,128)(2,1)} custom-call(bf16[8,128,1024]{2,1,0:T(8,128)(2,1)} %all_to_all.15.in_ref, f32[33,128]{1,0:T(8,128)} %constant.25.clone.cos_ref, f32[33,128]{1,0:T(8,128)} %constant.26.clone.sin_ref, bf16[256,256]{1,0:T(8,128)(2,1)} %constant.27.clone.wave_high_ref, bf16[256,256]{1,0:T(8,128)(2,1)} %constant.28.clone.wave_low_ref), custom_call_target="tpu_custom_call" | custom-call | tf_op jit(solution)/shard_map/transform/pallas_call | solution.py:262
  71.6 3.6 %all-to-all-start.1 = ((bf16[8,2,8,2,32,128]{5,4,3,2,1,0:T(8,128)(2,1)}), bf16[8,2,8,2,32,128]{5,4,3,2,1,0:T(8,128)(2,1)S(1)}, u32[]{:S(2)}, u32[]{:S(2)}) async-start(bf16[8,2,8,2,32,128]{5,4,3,2,1,0:T(8,128)(2,1)} %transform.1), calls=%async_computation.1 | async-start | bytes 4194304 | tf_op jit(solution)/shard_map/all_to_all | solution.py:419
  75.3 0.0 copy-done.2
  75.3 0.1 select_reduce_fusion.mates_ref
  75.4 0.0 copy-start.1
  75.4 0.1 fusion
  75.5 47.6 %all-to-all-done.1.mine_ref = bf16[8,2,8,2,32,128]{5,4,3,2,1,0:T(8,128)(2,1)S(1)} async-done(((bf16[8,2,8,2,32,128]{5,4,3,2,1,0:T(8,128)(2,1)}), bf16[8,2,8,2,32,128]{5,4,3,2,1,0:T(8,128)(2,1)S(1)}, u32[]{:S(2)}, u32[]{:S(2)}) %all-to-all-start.1) | async-done | bytes 2097184 | tf_op jit(solution)/shard_map/all_to_all | solution.py:419
  123.1 0.0 copy-start
  123.1 0.5 slice_bitcast_fusion.1
  123.6 2.6 select_select_fusion
  126.1 0.0 copy-done
  126.1 4.8 %all-to-all-start.2 = ((bf16[4,8,8,2,32,128]{5,4,3,2,1,0:T(8,128)(2,1)}), bf16[4,8,8,2,32,128]{5,4,3,2,1,0:T(8,128)(2,1)}, u32[]{:S(2)}, u32[]{:S(2)}) async-start(bf16[4,8,8,2,32,128]{5,4,3,2,1,0:T(8,128)(2,1)} %select_select_fusion), calls=%async_computation.2 | async-start | bytes 8388608 | tf_op jit(solution)/shard_map/all_to_all | solution.py:430
  131.0 0.0 copy-done.1
  131.0 0.5 compare_convert_fusion.halves_ref
  131.5 47.6 %all-to-all-done.2.mate_ref = bf16[4,8,8,2,32,128]{5,4,3,2,1,0:T(8,128)(2,1)} async-done(((bf16[4,8,8,2,32,128]{5,4,3,2,1,0:T(8,128)(2,1)}), bf16[4,8,8,2,32,128]{5,4,3,2,1,0:T(8,128)(2,1)}, u32[]{:S(2)}, u32[]{:S(2)}) %all-to-all-start.2) | async-done | bytes 4194336 | tf_op jit(solution)/shard_map/all_to_all | solution.py:430
  179.2 88.9 %correlate.1 = bf16[3,64,256,128]{3,2,1,0:T(8,128)(2,1)} custom-call(s32[3]{0:T(128)} %compare_convert_fusion.halves_ref, s32[3]{0:T(128)} %copy-done.1, bf16[8,2,8,2,32,128]{5,4,3,2,1,0:T(8,128)(2,1)} %copy-done, bf16[4,8,8,2,32,128]{5,4,3,2,1,0:T(8,128)(2,1)} %all-to-all-done.2.mate_ref), custom_call_target="tpu_custom_call" | custom-call | tf_op jit(solution)/shard_map/correlate/pallas_call | solution.py:359
  (2 shorter events, 0.0 us)
Async XLA Ops:
  63.8 11.4 %copy-start.2 = (s32[3,4]{1,0:T(4,128)S(1)}, s32[3,4]{1,0:T(4,128)}, u32[]{:S(2)}) copy-start(s32[3,4]{1,0:T(4,128)} %param.8) | copy-start | bytes 148
  71.6 51.5 %all-to-all-start.1 = ((bf16[8,2,8,2,32,128]{5,4,3,2,1,0:T(8,128)(2,1)}), bf16[8,2,8,2,32,128]{5,4,3,2,1,0:T(8,128)(2,1)S(1)}, u32[]{:S(2)}, u32[]{:S(2)}) async-start(bf16[8,2,8,2,32,128]{5,4,3,2,1,0:T(8,128)(2,1)} %transform.1), calls=%async_computation.1 | async-start | bytes 4194304 | tf_op jit(solution)/shard_map/all_to_all | solution.py:419
  75.4 55.6 %copy-start.1 = (s32[3]{0:T(128)}, s32[3]{0:T(128)S(1)}, u32[]{:S(2)}) copy-start(s32[3]{0:T(128)S(1)} %select_reduce_fusion.mates_ref) | copy-start | bytes 40
  123.1 3.0 %copy-start = (bf16[8,2,8,2,32,128]{5,4,3,2,1,0:T(8,128)(2,1)}, bf16[8,2,8,2,32,128]{5,4,3,2,1,0:T(8,128)(2,1)S(1)}, u32[]{:S(2)}) copy-start(bf16[8,2,8,2,32,128]{5,4,3,2,1,0:T(8,128)(2,1)S(1)} %all-to-all-done.1.mine_ref) | copy-start | bytes 6291460
  126.1 53.0 %all-to-all-start.2 = ((bf16[4,8,8,2,32,128]{5,4,3,2,1,0:T(8,128)(2,1)}), bf16[4,8,8,2,32,128]{5,4,3,2,1,0:T(8,128)(2,1)}, u32[]{:S(2)}, u32[]{:S(2)}) async-start(bf16[4,8,8,2,32,128]{5,4,3,2,1,0:T(8,128)(2,1)} %select_select_fusion), calls=%async_computation.2 | async-start | bytes 8388608 | tf_op jit(solution)/shard_map/all_to_all | solution.py:430

commit v3 on v1

--- a/solution.py
+++ b/solution.py
@@ -47,9 +47,9 @@
     lax.fori_loop(0, block_len // LANES, one_tile, 0)
 
 
-def filter_taps(frames_first, chan_id, chan_count):
-    frames, sig_count, block_len = frames_first.shape
-    spec_count = frames - TAPS + 1
+def filter_taps(frames_first, chan_id, chan_count, first, spec_count):
+    _, sig_count, block_len = frames_first.shape
+    frames = spec_count + TAPS - 1
     table = tap_table(block_len * chan_count).astype(np.float32)
     table = np.ascontiguousarray(table.reshape(TAPS, chan_count, block_len).transpose(1, 0, 2))
     sig_tile = 16
@@ -60,7 +60,10 @@
             num_scalar_prefetch=1,
             grid=(sig_count // sig_tile,),
             in_specs=[
-                pl.BlockSpec((frames, sig_tile, block_len), lambda i, c: (0, i, 0)),
+                pl.BlockSpec(
+                    (pl.Element(frames), pl.Element(sig_tile), pl.Element(block_len)),
+                    lambda i, c: (first, i * sig_tile, 0),
+                ),
                 pl.BlockSpec((1, TAPS, block_len), lambda i, c: (c[0], 0, 0)),
             ],
             out_specs=pl.BlockSpec((spec_count, sig_tile, block_len), lambda i, c: (0, i, 0)),
@@ -164,7 +167,7 @@
 
 
 def transform_kernel(
-    chan_count, in_ref, cos_ref, sin_ref, wave_high_ref, wave_low_ref, out_ref, mid_ref, high_ref, low_ref
+    chan_count, joined, in_ref, cos_ref, sin_ref, wave_high_ref, wave_low_ref, out_ref, mid_ref, high_ref, low_ref
 ):
     _, rows, block_len = in_ref.shape
     per_block = block_len // LANES
@@ -221,30 +224,51 @@
     dims = (((1,), (1,)), ((), ()))
     wave_high = wave_high_ref[...]
     wave_low = wave_low_ref[...]
-    for first in range(0, len(chosen), 2):
-        places = [p for p in (first, first + 1) if p < len(chosen)]
+    quarter = LANES // 4
+    group = max(2, 2 * LANES // rows)
+    for first in range(0, len(chosen), group):
+        places = range(first, min(first + group, len(chosen)))
         high = high_ref[first : first + len(places)].reshape(len(places) * rows, 2 * LANES)
         low = low_ref[first : first + len(places)].reshape(len(places) * rows, 2 * LANES)
         total = lax.dot_general(wave_high, high, dims, preferred_element_type=jnp.float32)
         total += lax.dot_general(wave_high, low, dims, preferred_element_type=jnp.float32)
         total += lax.dot_general(wave_low, high, dims, preferred_element_type=jnp.float32)
-        total = total.astype(jnp.bfloat16)
-        for i, place in enumerate(places):
+
+        def put(place, side, half, part, value):
             k1 = chosen[place]
-            columns = total[:, i * rows : (i + 1) * rows]
-            quarter = LANES // 4
-            for side, index in ((0, k1), (1, RADIX - k1)):
-                if side == 1 and (k1 == 0 or k1 == RADIX // 2):
+            if side == 1 and (k1 == 0 or k1 == RADIX // 2):
+                return
+            index = RADIX - k1 if side else k1
+            at = (index % chan_count, half, index // chan_count)
+            if not joined:
+                at += (part,)
+            out_ref[at] = value.astype(jnp.bfloat16)
+
+        for side in range(2):
+            for half in range(2):
+                row_re = side * LANES + half * quarter
+                row_im = row_re + 2 * quarter
+                if not joined:
+                    for i, place in enumerate(places):
+                        columns = slice(i * rows, (i + 1) * rows)
+                        put(place, side, half, 0, total[row_re : row_re + quarter, columns])
+                        put(place, side, half, 1, total[row_im : row_im + quarter, columns])
                     continue
-                for part in range(2):
-                    for half in range(2):
-                        at = side * LANES + part * 2 * quarter + half * quarter
-                        out_ref[index % chan_count, half, index // chan_count, part] = columns[
-                            at : at + quarter
-                        ]
-
-
-def transform(samples):
+                for i in range(0, len(places), 2):
+                    columns = slice(i * rows, min((i + 2) * rows, len(places) * rows))
+                    re = total[row_re : row_re + quarter, columns]
+                    im = total[row_im : row_im + quarter, columns]
+                    if i + 1 == len(places):
+                        put(places[i], side, half, 0, jnp.concatenate([re, im], axis=1))
+                        continue
+                    low_lanes = lax.broadcasted_iota(jnp.int32, re.shape, 1) < rows
+                    put(places[i], side, half, 0, jnp.where(low_lanes, re, pltpu.roll(im, rows, 1)))
+                    put(
+                        places[i + 1], side, half, 0, jnp.where(low_lanes, pltpu.roll(re, rows, 1), im)
+                    )
+
+
+def transform(samples, joined):
     chan_count, rows, block_len = samples.shape
     fft_len = chan_count * block_len
     count = len(first_index_list())
@@ -259,11 +283,11 @@
         jnp.asarray(wave_low),
     )
     whole = pl.BlockSpec(memory_space=pltpu.VMEM)
+    shape = (chan_count, 2, RADIX // chan_count)
+    shape += (LANES // 4, 2 * rows) if joined else (2, LANES // 4, rows)
     return pl.pallas_call(
-        functools.partial(transform_kernel, chan_count),
-        out_shape=jax.ShapeDtypeStruct(
-            (chan_count, 2, RADIX // chan_count, 2, LANES // 4, rows), jnp.bfloat16
-        ),
+        functools.partial(transform_kernel, chan_count, joined),
+        out_shape=jax.ShapeDtypeStruct(shape, jnp.bfloat16),
         in_specs=[whole] * 5,
         out_specs=whole,
         scratch_shapes=[
@@ -276,7 +300,157 @@
     )(samples, *tables)
 
 
-def correlate(mine, theirs):
+EIGHT = 8
+
+
+def turn_kernel(in_ref, out_ref, wide_ref):
+    chan_count, _, per, k2_count, lanes = in_ref.shape
+    channels = per * k2_count
+
+    def spread(step, carry):
+        source, e = step // per, step % per
+        for k2 in range(0, k2_count, EIGHT):
+            value = in_ref[source, 0, e, k2 : k2 + EIGHT, :].astype(jnp.float32)
+            row = (e + per * k2) * chan_count + source
+            wide_ref[pl.ds(row, EIGHT, stride=per * chan_count), :] = value
+        return carry
+
+    lax.fori_loop(0, chan_count * per, spread, 0, unroll=4)
+
+    def narrow(step, carry):
+        base = pl.multiple_of(step * EIGHT, EIGHT)
+        rows = pl.ds(pl.multiple_of(step * EIGHT * chan_count, EIGHT * chan_count), EIGHT * chan_count)
+        value = wide_ref[rows, :].astype(jnp.bfloat16)
+        out_ref[0, pl.ds(base, EIGHT)] = value.reshape(EIGHT, chan_count, lanes)
+        return carry
+
+    lax.fori_loop(0, channels // EIGHT, narrow, 0, unroll=2)
+
+
+def turn(channel):
+    chan_count, halves, per, k2_count, lanes = channel.shape
+    channels = per * k2_count
+    return pl.pallas_call(
+        turn_kernel,
+        out_shape=jax.ShapeDtypeStruct((halves, channels, chan_count, lanes), jnp.bfloat16),
+        grid=(halves,),
+        in_specs=[
+            pl.BlockSpec((chan_count, 1, per, k2_count, lanes), lambda u: (0, u, 0, 0, 0))
+        ],
+        out_specs=pl.BlockSpec((1, channels, chan_count, lanes), lambda u: (u, 0, 0, 0)),
+        scratch_shapes=[pltpu.VMEM((channels * chan_count, lanes), jnp.float32)],
+        compiler_params=pltpu.CompilerParams(vmem_limit_bytes=VMEM_LIMIT),
+        name="turn",
+    )(channel)
+
+
+def left_kernel(*refs):
+    chunk_refs, out_ref = refs[:-1], refs[-1]
+    _, channels, _, lanes = chunk_refs[0].shape
+    sig_count = lanes // 2
+
+    def pair(step, carry):
+        rows = []
+        for i in range(2):
+            values = [ref[0, 2 * step + i].astype(jnp.float32) for ref in chunk_refs]
+            rows += values + [pltpu.roll(value, sig_count, 1) for value in values]
+        stacked = jnp.concatenate(rows, axis=0)
+        out_ref[0, step] = stacked.T[:sig_count].astype(jnp.bfloat16)
+        return carry
+
+    lax.fori_loop(0, channels // 2, pair, 0, unroll=4)
+
+
+def left_operand(chunks):
+    halves, channels, chan_count, lanes = chunks[0].shape
+    depth = 2 * 2 * len(chunks) * chan_count
+    tile = 64
+    return pl.pallas_call(
+        left_kernel,
+        out_shape=jax.ShapeDtypeStruct((halves, channels // 2, lanes // 2, depth), jnp.bfloat16),
+        grid=(halves, channels // tile),
+        in_specs=[pl.BlockSpec((1, tile, chan_count, lanes), lambda u, i: (u, i, 0, 0))]
+        * len(chunks),
+        out_specs=pl.BlockSpec((1, tile // 2, lanes // 2, depth), lambda u, i: (u, i, 0, 0)),
+        compiler_params=pltpu.CompilerParams(vmem_limit_bytes=VMEM_LIMIT),
+        name="left_operand",
+    )(*chunks)
+
+
+def correlate_kernel(chunk_count, spec_count, place_ref, left_ref, *refs):
+    del place_ref
+    chunk_refs = refs[:chunk_count]
+    out_ref, sum_ref = refs[-2:]
+    _, channels, chan_count, lanes = (1,) + chunk_refs[0].shape
+    sig_count = lanes // 2
+    sign = jnp.where(
+        lax.broadcasted_iota(jnp.int32, (chan_count, lanes), 1) < sig_count, 1.0, -1.0
+    ).astype(jnp.float32)
+
+    def pair(step, carry):
+        blocks = []
+        for i in range(2):
+            values = [ref[2 * step + i].astype(jnp.float32) for ref in chunk_refs]
+            rows = [value * sign for value in values]
+            rows += [pltpu.roll(value, sig_count, 1) for value in values]
+            blocks.append(jnp.concatenate(rows, axis=0).astype(jnp.bfloat16))
+        zero = jnp.zeros_like(blocks[0])
+        weights = jnp.concatenate(
+            [
+                jnp.concatenate([blocks[0], zero], axis=1),
+                jnp.concatenate([zero, blocks[1]], axis=1),
+            ],
+            axis=0,
+        )
+        both = jnp.dot(left_ref[0, step], weights, preferred_element_type=jnp.float32)
+        for i in range(2):
+            q = 2 * step + i
+            for a in range(0, sig_count, EIGHT):
+                sum_ref[pl.ds(a * channels + q, EIGHT, stride=channels), :] = both[
+                    a : a + EIGHT, i * lanes : (i + 1) * lanes
+                ]
+        return carry
+
+    lax.fori_loop(0, channels // 2, pair, 0, unroll=4)
+
+    def finish(a, carry):
+        rows = pl.ds(pl.multiple_of(a * channels, channels), channels)
+        out_ref[0, a] = (sum_ref[rows, :] * (1.0 / spec_count)).astype(jnp.bfloat16)
+        return carry
+
+    lax.fori_loop(0, sig_count, finish, 0, unroll=4)
+
+
+def correlate(left, chunks, place, rounds, spec_count, so_far):
+    channels, chan_count, lanes = chunks[0].shape
+    sig_count, depth = left.shape[2:]
+    tile = 32
+    in_specs = [
+        pl.BlockSpec((1, tile // 2, sig_count, depth), lambda i, p: (p[1], i, 0, 0)),
+    ] + [pl.BlockSpec((tile, chan_count, lanes), lambda i, p: (i, 0, 0))] * len(chunks)
+    operands = [left, *chunks]
+    aliases = {}
+    if so_far is not None:
+        in_specs.append(pl.BlockSpec(memory_space=pl.ANY))
+        operands.append(so_far)
+        aliases = {len(operands): 0}
+    return pl.pallas_call(
+        functools.partial(correlate_kernel, len(chunks), spec_count),
+        out_shape=jax.ShapeDtypeStruct((rounds, sig_count, channels, lanes), jnp.bfloat16),
+        grid_spec=pltpu.PrefetchScalarGridSpec(
+            num_scalar_prefetch=1,
+            grid=(channels // tile,),
+            in_specs=in_specs,
+            out_specs=pl.BlockSpec((1, sig_count, tile, lanes), lambda i, p: (p[0], 0, i, 0)),
+            scratch_shapes=[pltpu.VMEM((sig_count * tile, lanes), jnp.float32)],
+        ),
+        input_output_aliases=aliases,
+        compiler_params=pltpu.CompilerParams(vmem_limit_bytes=VMEM_LIMIT),
+        name="correlate",
+    )(place, *operands)
+
+
+def correlate_plain(mine, theirs):
     left = mine.reshape(*mine.shape[:2], -1)
     right_re = theirs.reshape(left.shape)
     right_im = jnp.stack([-theirs[..., 1], theirs[..., 0]], axis=-1).reshape(left.shape)
@@ -291,7 +465,7 @@
     return turned.transpose(0, 2, 1, 3)
 
 
-def local(voltages, plan):
+def local_plain(voltages, plan):
     sig_count, frames, block_len = voltages.shape
     chan_count = lax.axis_size("chan")
     group_count = lax.axis_size("grp")
@@ -300,10 +474,10 @@
     chan_id = lax.axis_index("chan").astype(jnp.int32)
     group_id = lax.axis_index("grp")
 
-    filtered = filter_taps(voltages.transpose(1, 0, 2), chan_id, chan_count)
+    filtered = filter_taps(voltages.transpose(1, 0, 2), chan_id, chan_count, 0, spec_count)
     filtered = filtered.reshape(chan_count, rows, block_len)
     frames_here = lax.all_to_all(filtered, "chan", split_axis=0, concat_axis=0, tiled=True)
-    spectra = transform(frames_here)
+    spectra = transform(frames_here, False)
     channel = lax.all_to_all(spectra, "chan", split_axis=0, concat_axis=0, tiled=True)
 
     lower_half, upper_half = channel[:, 0], channel[:, 1]
@@ -316,20 +490,73 @@
     )
     slots = jnp.where(listed.reshape(slot_shape), chosen_half, jnp.zeros_like(chosen_half))
     received = lax.all_to_all(slots, "grp", split_axis=0, concat_axis=0, tiled=True)
+    halves = (group_id > partner).astype(jnp.int32)
     results = []
     for round_index in range(plan.shape[0]):
-        partner_id = partner[round_index]
-        upper_flag = (group_id > partner_id).astype(jnp.int32)
-        mine = lax.dynamic_index_in_dim(channel, upper_flag, 1, keepdims=False)
-        theirs = lax.dynamic_index_in_dim(received, partner_id, 0, keepdims=False)
+        mine = lax.dynamic_index_in_dim(channel, halves[round_index], 1, keepdims=False)
+        theirs = lax.dynamic_index_in_dim(received, partner[round_index], 0, keepdims=False)
         results.append(
-            correlate(
+            correlate_plain(
                 by_channel(mine, sig_count, spec_count), by_channel(theirs, sig_count, spec_count)
             )
         )
     return jnp.stack(results).astype(jnp.bfloat16)
 
 
+def local_overlapped(voltages, plan):
+    _, frames, _ = voltages.shape
+    chan_count = lax.axis_size("chan")
+    group_count = lax.axis_size("grp")
+    rounds = plan.shape[0]
+    spec_count = frames - TAPS + 1
+    chan_id = lax.axis_index("chan").astype(jnp.int32)
+    group_id = lax.axis_index("grp").astype(jnp.int32)
+    frames_first = voltages.transpose(1, 0, 2)
+
+    def over_chan(value):
+        return lax.all_to_all(value, "chan", split_axis=0, concat_axis=0, tiled=True)
+
+    def to_mate(value, distance):
+        return lax.ppermute(value, "grp", [(g, g ^ distance) for g in range(group_count)])
+
+    group_ids = jnp.arange(group_count, dtype=jnp.int32)
+    partner = jnp.sum(jnp.where(group_ids[None, :] == group_id, plan, 0), axis=1)
+    turned, near, across, relayed = [], [], [], []
+    for first in range(0, spec_count, chan_count):
+        filtered = filter_taps(frames_first, chan_id, chan_count, first, chan_count)
+        channel = over_chan(transform(over_chan(filtered), True))
+        halves = turn(channel)
+        turned.append(halves)
+        for_near = lax.dynamic_index_in_dim(halves, 1 - group_id % 2, 0, keepdims=False)
+        for_across = lax.dynamic_index_in_dim(halves, 1 - group_id // 2, 0, keepdims=False)
+        near.append(to_mate(for_near, 1))
+        across.append(to_mate(for_across, 2))
+        relayed.append(to_mate(across[-1], 1))
+    left = left_operand(turned)
+    result = None
+    for distance, chunks in ((1, near), (2, across), (3, relayed)):
+        mate = group_id ^ distance
+        round_of = jnp.sum(jnp.where(partner == mate, jnp.arange(rounds, dtype=jnp.int32), 0))
+        place = jnp.stack([round_of, (group_id > mate).astype(jnp.int32)])
+        result = correlate(left, chunks, place, rounds, spec_count, result)
+    return result
+
+
+def local(voltages, plan):
+    sig_count, frames, _ = voltages.shape
+    chan_count = lax.axis_size("chan")
+    group_count = lax.axis_size("grp")
+    if (
+        group_count == 4
+        and plan.shape[0] == group_count - 1
+        and chan_count == EIGHT
+        and (frames - TAPS + 1) % chan_count == 0
+        and 2 * sig_count == LANES
+    ):
+        return local_overlapped(voltages, plan)
+    return local_plain(voltages, plan)
+
+
 def solution(mesh):
     in_specs = (P("grp", None, "chan"), P())
     out_specs = P(None, "grp", "chan", None)

time: 286 us -> 230 us (0.80); the launches traced: 281 us -> 229 us
  Pallas kernels: 16 us -> 93.6 us
  local copies, waits for them, and re-layouts: 79.5 us -> 7.08 us
  blocking collectives: 55.6 us -> 0 us
  waiting for transfers between devices: 72.2 us -> 104 us
  other arithmetic: 22 us -> 3.96 us
  matrix products: 17.9 us -> 0 us
  starting transfers between devices: 8.95 us -> 20.7 us
  between operations: 8.34 us -> 0.07 us
    pallas_call x1 -> x8, Pallas kernels: 7.78 us -> 81.7 us  [the longest x3 46.4 us: correlate(): pl.pallas_call(functools.partial(correlate_kernel, len(chunks), spec_coun...]
    all_to_all x1 -> x0, blocking collectives: 55.6 us -> none  [local(): lax.all_to_all(filtered, 'chan', split_axis=0, concat_axis=0, tiled=True)]
    another operation x4 -> x0, local copies, waits for them, and re-layouts: 36 us -> none  [the longest x1 28.2 us: local(): return jnp.stack(results).astype(jnp.bfloat16)]
    transpose x11 -> x0, local copies, waits for them, and re-layouts: 29.7 us -> none  [the longest x6 21 us: by_channel(): return turned.transpose(0, 2, 1, 3)]
    ppermute x0 -> x6, waiting for transfers between devices: none -> 21.4 us  [to_mate(): lax.ppermute(value, 'grp', [(g, g ^ distance) for g in range(group_count)])]
    dot_general x6 -> x0, matrix products: 17.9 us -> none  [the longest x3 10.6 us: correlate(): jnp.einsum('kas,kbs->akb', left, right_re, preferred_element_type=jnp.flo...]
    another operation x7 -> x2, other arithmetic: 14.6 us -> 3.09 us  [local_overlapped(): place = jnp.stack([round_of, (group_id > mate).astype(jnp.int32)])]
    all_to_all x2 -> x4, waiting for transfers between devices: 72.2 us -> 82.3 us  [over_chan(): lax.all_to_all(value, 'chan', split_axis=0, concat_axis=0, tiled=True)]
  transfers between devices with their start and end apart: 2 -> 10, of which waited for: 2 -> 6; matrix products, arithmetic and copies ran while one was open for 6% -> 2% of each run, Pallas kernels for 0% -> 30%
where the time goes in v3:
time: 230 us; the launch traced here: 229 us
  waiting for transfers between devices  104 us (45%)
  Pallas kernels  93.6 us (41%)
  starting transfers between devices  20.7 us (9%)
  local copies, waits for them, and re-layouts  7.08 us (3%)
  other arithmetic  3.96 us (2%)
    all_to_all x4, waiting for transfers between devices, over_chan(): lax.all_to_all(value, 'chan', split_axis=0, concat_axis=0, tiled=True)  82.3 us
    pallas_call x3, Pallas kernels, correlate(): pl.pallas_call(functools.partial(correlate_kernel, len(chunks), spec_coun...  46.4 us
    ppermute x6, waiting for transfers between devices, to_mate(): lax.ppermute(value, 'grp', [(g, g ^ distance) for g in range(group_count)])  21.4 us
    all_to_all x4, starting transfers between devices, over_chan(): lax.all_to_all(value, 'chan', split_axis=0, concat_axis=0, tiled=True)  18.2 us
    pallas_call x1, Pallas kernels, left_operand(): pl.pallas_call(left_kernel, out_shape=jax.ShapeDtypeStruct((halves, chann...  17 us
    pallas_call x2, Pallas kernels, filter_taps(): pl.pallas_call(filter_kernel, out_shape=jax.ShapeDtypeStruct((spec_count,...  11.9 us
    pallas_call x2, Pallas kernels, transform(): pl.pallas_call(functools.partial(transform_kernel, chan_count, joined), o...  9.85 us
    pallas_call x2, Pallas kernels, turn(): pl.pallas_call(turn_kernel, out_shape=jax.ShapeDtypeStruct((halves, chann...  8.43 us
  transfers between devices with their start and end apart: 10, of which 6 were waited for; matrix products, arithmetic and copies ran while one was open for 2% of the time, Pallas kernels for 30%

profile of v3, /device:TPU:0, one launch (start us, length us, event | category | flops | bytes accessed | tf_op | source)
XLA Modules:
  0.0 229.1 jit_solution(16120053765054805903)
XLA Ops:
  0.0 6.0 %filter_taps.2 = bf16[8,64,1024]{2,1,0:T(8,128)(2,1)} custom-call(s32[1]{0:T(128)} %bitcast.2.chan_ref, s32[31,64,1024]{2,1,0:T(8,128)} %bitcast.16, f32[8,16,1024]{2,1,0:T(8,128)} %constant.62.clone.coeff_ref), custom_call_target="tpu_custom_call" | custom-call | tf_op jit(solution)/shard_map/filter_taps/pallas_call | solution.py:56
  6.0 7.3 %all-to-all-start = ((bf16[8,64,1024]{2,1,0:T(8,128)(2,1)}), bf16[8,64,1024]{2,1,0:T(8,128)(2,1)S(1)}, u32[]{:S(2)}, u32[]{:S(2)}) async-start(bf16[8,64,1024]{2,1,0:T(8,128)(2,1)} %filter_taps.2), calls=%async_computation | async-start | bytes 2097152 | tf_op jit(solution)/shard_map/all_to_all | solution.py:517
  13.3 6.0 %filter_taps.3 = bf16[8,64,1024]{2,1,0:T(8,128)(2,1)} custom-call(s32[1]{0:T(128)} %bitcast.2.chan_ref, s32[31,64,1024]{2,1,0:T(8,128)} %bitcast.17, f32[8,16,1024]{2,1,0:T(8,128)} %constant.62.clone.coeff_ref), custom_call_target="tpu_custom_call" | custom-call | tf_op jit(solution)/shard_map/filter_taps/pallas_call | solution.py:56
  19.3 19.8 %all-to-all-done.in_ref = bf16[8,64,1024]{2,1,0:T(8,128)(2,1)S(1)} async-done(((bf16[8,64,1024]{2,1,0:T(8,128)(2,1)}), bf16[8,64,1024]{2,1,0:T(8,128)(2,1)S(1)}, u32[]{:S(2)}, u32[]{:S(2)}) %all-to-all-start) | async-done | bytes 1048608 | tf_op jit(solution)/shard_map/all_to_all | solution.py:517
  39.0 3.6 %all-to-all-start.2 = ((bf16[8,64,1024]{2,1,0:T(8,128)(2,1)}), bf16[8,64,1024]{2,1,0:T(8,128)(2,1)S(1)}, u32[]{:S(2)}, u32[]{:S(2)}) async-start(bf16[8,64,1024]{2,1,0:T(8,128)(2,1)} %filter_taps.3), calls=%async_computation.2 | async-start | bytes 2097152 | tf_op jit(solution)/shard_map/all_to_all | solution.py:517
  42.6 4.9 %transform.2 = bf16[8,2,8,32,128]{4,3,2,1,0:T(8,128)(2,1)} custom-call(bf16[8,64,1024]{2,1,0:T(8,128)(2,1)} %copy-done.1, f32[33,128]{1,0:T(8,128)} %constant.63.clone.cos_ref, f32[33,128]{1,0:T(8,128)} %constant.64.clone.sin_ref, bf16[256,256]{1,0:T(8,128)(2,1)} %constant.65.clone.wave_high_ref, bf16[256,256]{1,0:T(8,128)(2,1)} %constant.66.clone.wave_low_ref), custom_call_target="tpu_custom_call" | custom-call | tf_op jit(solution)/shard_map/transform/pallas_call | solution.py:288
  47.6 21.0 %all-to-all-done.2.in_ref = bf16[8,64,1024]{2,1,0:T(8,128)(2,1)S(1)} async-done(((bf16[8,64,1024]{2,1,0:T(8,128)(2,1)}), bf16[8,64,1024]{2,1,0:T(8,128)(2,1)S(1)}, u32[]{:S(2)}, u32[]{:S(2)}) %all-to-all-start.2) | async-done | bytes 1048608 | tf_op jit(solution)/shard_map/all_to_all | solution.py:517
  68.6 3.6 %all-to-all-start.1 = ((bf16[8,2,8,32,128]{4,3,2,1,0:T(8,128)(2,1)}), bf16[8,2,8,32,128]{4,3,2,1,0:T(8,128)(2,1)S(1)}, u32[]{:S(2)}, u32[]{:S(2)}) async-start(bf16[8,2,8,32,128]{4,3,2,1,0:T(8,128)(2,1)} %transform.2), calls=%async_computation.1 | async-start | bytes 2097152 | tf_op jit(solution)/shard_map/all_to_all | solution.py:517
  72.2 4.9 %transform.3 = bf16[8,2,8,32,128]{4,3,2,1,0:T(8,128)(2,1)} custom-call(bf16[8,64,1024]{2,1,0:T(8,128)(2,1)} %copy-done, f32[33,128]{1,0:T(8,128)} %constant.63.clone.cos_ref, f32[33,128]{1,0:T(8,128)} %constant.64.clone.sin_ref, bf16[256,256]{1,0:T(8,128)(2,1)} %constant.65.clone.wave_high_ref, bf16[256,256]{1,0:T(8,128)(2,1)} %constant.66.clone.wave_low_ref), custom_call_target="tpu_custom_call" | custom-call | tf_op jit(solution)/shard_map/transform/pallas_call | solution.py:288
  77.2 21.0 %all-to-all-done.1.in_ref = bf16[8,2,8,32,128]{4,3,2,1,0:T(8,128)(2,1)S(1)} async-done(((bf16[8,2,8,32,128]{4,3,2,1,0:T(8,128)(2,1)}), bf16[8,2,8,32,128]{4,3,2,1,0:T(8,128)(2,1)S(1)}, u32[]{:S(2)}, u32[]{:S(2)}) %all-to-all-start.1) | async-done | bytes 1048608 | tf_op jit(solution)/shard_map/all_to_all | solution.py:517
  98.2 3.6 %all-to-all-start.3 = ((bf16[8,2,8,32,128]{4,3,2,1,0:T(8,128)(2,1)}), bf16[8,2,8,32,128]{4,3,2,1,0:T(8,128)(2,1)S(1)}, u32[]{:S(2)}, u32[]{:S(2)}) async-start(bf16[8,2,8,32,128]{4,3,2,1,0:T(8,128)(2,1)} %transform.3), calls=%async_computation.3 | async-start | bytes 2097152 | tf_op jit(solution)/shard_map/all_to_all | solution.py:517
  101.8 4.2 %turn.2.refs_0_ = bf16[2,256,8,128]{3,2,1,0:T(8,128)(2,1)} custom-call(bf16[8,2,8,32,128]{4,3,2,1,0:T(8,128)(2,1)} %copy-done.2), custom_call_target="tpu_custom_call" | custom-call | tf_op jit(solution)/shard_map/turn/pallas_call | solution.py:333
  106.0 1.3 dynamic-slice_bitcast_fusion.1
  107.3 20.5 %all-to-all-done.3.in_ref = bf16[8,2,8,32,128]{4,3,2,1,0:T(8,128)(2,1)S(1)} async-done(((bf16[8,2,8,32,128]{4,3,2,1,0:T(8,128)(2,1)}), bf16[8,2,8,32,128]{4,3,2,1,0:T(8,128)(2,1)S(1)}, u32[]{:S(2)}, u32[]{:S(2)}) %all-to-all-start.3) | async-done | bytes 1048608 | tf_op jit(solution)/shard_map/all_to_all | solution.py:517
  128.7 4.2 %turn.3.refs_1_ = bf16[2,256,8,128]{3,2,1,0:T(8,128)(2,1)} custom-call(bf16[8,2,8,32,128]{4,3,2,1,0:T(8,128)(2,1)} %copy-done.3), custom_call_target="tpu_custom_call" | custom-call | tf_op jit(solution)/shard_map/turn/pallas_call | solution.py:333
  132.9 2.3 dynamic-slice_bitcast_fusion
  135.2 1.5 collective-permute-start
  137.7 12.3 %collective-permute-done.refs_0_ = bf16[256,8,128]{2,1,0:T(8,128)(2,1)S(1)} collective-permute-done((bf16[256,8,128]{2,1,0:T(8,128)(2,1)S(1)}, bf16[256,8,128]{2,1,0:T(8,128)(2,1)S(1)}, u32[]{:S(2)}, u32[]{:S(2)}) %collective-permute-start) | collective-permute-done | bytes 524320 | tf_op jit(solution)/shard_map/ppermute | solution.py:520
  150.0 9.2 %collective-permute-done.2.refs_1_ = bf16[256,8,128]{2,1,0:T(8,128)(2,1)S(1)} collective-permute-done((bf16[256,8,128]{2,1,0:T(8,128)(2,1)}, bf16[256,8,128]{2,1,0:T(8,128)(2,1)S(1)}, u32[]{:S(2)}, u32[]{:S(2)}) %collective-permute-start.2) | collective-permute-done | bytes 524320 | tf_op jit(solution)/shard_map/ppermute | solution.py:520
  161.3 1.8 pad_add_fusion
  163.1 17.0 %left_operand.1.left_ref = bf16[2,128,64,64]{3,2,1,0:T(8,128)(2,1)} custom-call(bf16[2,256,8,128]{3,2,1,0:T(8,128)(2,1)} %turn.2.refs_0_, bf16[2,256,8,128]{3,2,1,0:T(8,128)(2,1)} %turn.3.refs_1_), custom_call_target="tpu_custom_call" | custom-call | tf_op jit(solution)/shard_map/left_operand/pallas_call | solution.py:368
  181.8 15.5 %correlate.3.refs_2_ = bf16[3,64,256,128]{3,2,1,0:T(8,128)(2,1)} custom-call(s32[2]{0:T(128)} %pad_add_fusion.2.place_ref, bf16[2,128,64,64]{3,2,1,0:T(8,128)(2,1)} %left_operand.1.left_ref, bf16[256,8,128]{2,1,0:T(8,128)(2,1)} %copy-done.8, bf16[256,8,128]{2,1,0:T(8,128)(2,1)} %copy-done.9), custom_call_target="tpu_custom_call" | custom-call | tf_op jit(solution)/shard_map/correlate/pallas_call | solution.py:437
  197.2 15.5 %correlate.4.refs_2_ = bf16[3,64,256,128]{3,2,1,0:T(8,128)(2,1)} custom-call(s32[2]{0:T(128)} %get-tuple-element.13.place_ref, bf16[2,128,64,64]{3,2,1,0:T(8,128)(2,1)} %left_operand.1.left_ref, bf16[256,8,128]{2,1,0:T(8,128)(2,1)} %copy-done.4, bf16[256,8,128]{2,1,0:T(8,128)(2,1)} %copy-done.5, ...), custom_call_target="tpu_custom_call", output_to_operand_aliasing={{}: (4, {})} | custom-call | tf_op jit(solution)/shard_map/correlate/pallas_call | solution.py:437
  213.7 15.5 %correlate.5 = bf16[3,64,256,128]{3,2,1,0:T(8,128)(2,1)} custom-call(s32[2]{0:T(128)} %get-tuple-element.12.place_ref, bf16[2,128,64,64]{3,2,1,0:T(8,128)(2,1)} %left_operand.1.left_ref, bf16[256,8,128]{2,1,0:T(8,128)(2,1)} %copy-done.6, bf16[256,8,128]{2,1,0:T(8,128)(2,1)} %copy-done.7, ...), custom_call_target="tpu_custom_call", output_to_operand_aliasing={{}: (4, {})} | custom-call | tf_op jit(solution)/shard_map/correlate/pallas_call | solution.py:437
  (35 shorter events, 6.8 us)
Async XLA Ops:
  6.0 33.1 %all-to-all-start = ((bf16[8,64,1024]{2,1,0:T(8,128)(2,1)}), bf16[8,64,1024]{2,1,0:T(8,128)(2,1)S(1)}, u32[]{:S(2)}, u32[]{:S(2)}) async-start(bf16[8,64,1024]{2,1,0:T(8,128)(2,1)} %filter_taps.2), calls=%async_computation | async-start | bytes 2097152 | tf_op jit(solution)/shard_map/all_to_all | solution.py:517
  13.3 145.9 %copy-start.10 = (s32[3,4]{1,0:T(4,128)S(1)}, s32[3,4]{1,0:T(4,128)}, u32[]{:S(2)}) copy-start(s32[3,4]{1,0:T(4,128)} %param.13) | copy-start | bytes 148
  39.0 3.6 %copy-start.1 = (bf16[8,64,1024]{2,1,0:T(8,128)(2,1)}, bf16[8,64,1024]{2,1,0:T(8,128)(2,1)S(1)}, u32[]{:S(2)}) copy-start(bf16[8,64,1024]{2,1,0:T(8,128)(2,1)S(1)} %all-to-all-done.in_ref) | copy-start | bytes 3145732
  39.0 29.5 %all-to-all-start.2 = ((bf16[8,64,1024]{2,1,0:T(8,128)(2,1)}), bf16[8,64,1024]{2,1,0:T(8,128)(2,1)S(1)}, u32[]{:S(2)}, u32[]{:S(2)}) async-start(bf16[8,64,1024]{2,1,0:T(8,128)(2,1)} %filter_taps.3), calls=%async_computation.2 | async-start | bytes 2097152 | tf_op jit(solution)/shard_map/all_to_all | solution.py:517
  68.6 3.6 %copy-start = (bf16[8,64,1024]{2,1,0:T(8,128)(2,1)}, bf16[8,64,1024]{2,1,0:T(8,128)(2,1)S(1)}, u32[]{:S(2)}) copy-start(bf16[8,64,1024]{2,1,0:T(8,128)(2,1)S(1)} %all-to-all-done.2.in_ref) | copy-start | bytes 3145732
  68.6 29.6 %all-to-all-start.1 = ((bf16[8,2,8,32,128]{4,3,2,1,0:T(8,128)(2,1)}), bf16[8,2,8,32,128]{4,3,2,1,0:T(8,128)(2,1)S(1)}, u32[]{:S(2)}, u32[]{:S(2)}) async-start(bf16[8,2,8,32,128]{4,3,2,1,0:T(8,128)(2,1)} %transform.2), calls=%async_computation.1 | async-start | bytes 2097152 | tf_op jit(solution)/shard_map/all_to_all | solution.py:517
  98.2 3.6 %copy-start.2 = (bf16[8,2,8,32,128]{4,3,2,1,0:T(8,128)(2,1)}, bf16[8,2,8,32,128]{4,3,2,1,0:T(8,128)(2,1)S(1)}, u32[]{:S(2)}) copy-start(bf16[8,2,8,32,128]{4,3,2,1,0:T(8,128)(2,1)S(1)} %all-to-all-done.1.in_ref) | copy-start | bytes 3145732
  98.2 29.6 %all-to-all-start.3 = ((bf16[8,2,8,32,128]{4,3,2,1,0:T(8,128)(2,1)}), bf16[8,2,8,32,128]{4,3,2,1,0:T(8,128)(2,1)S(1)}, u32[]{:S(2)}, u32[]{:S(2)}) async-start(bf16[8,2,8,32,128]{4,3,2,1,0:T(8,128)(2,1)} %transform.3), calls=%async_computation.3 | async-start | bytes 2097152 | tf_op jit(solution)/shard_map/all_to_all | solution.py:517
  127.8 1.0 copy-start.3
  135.2 14.8 %collective-permute-start = (bf16[256,8,128]{2,1,0:T(8,128)(2,1)S(1)}, bf16[256,8,128]{2,1,0:T(8,128)(2,1)S(1)}, u32[]{:S(2)}, u32[]{:S(2)}) collective-permute-start(bf16[256,8,128]{2,1,0:T(8,128)(2,1)S(1)} %get-tuple-element.11), channel_id=1, source_target_pairs={{0,16},{8,24},{16,0},{24,8},{1,17},{9,25},{17,1},{25,9},{2,18},{10... | collective-permute-start | bytes 1572872 | tf_op jit(solution)/shard_map/ppermute | solution.py:520
  136.7 22.5 %collective-permute-start.2 = (bf16[256,8,128]{2,1,0:T(8,128)(2,1)}, bf16[256,8,128]{2,1,0:T(8,128)(2,1)S(1)}, u32[]{:S(2)}, u32[]{:S(2)}) collective-permute-start(bf16[256,8,128]{2,1,0:T(8,128)(2,1)} %get-tuple-element.9), channel_id=1, source_target_pairs={{0,16},{8,24},{16,0},{24,8},{1,17},{9,25},{17,1},{25,9},{2,18},{10... | collective-permute-start | bytes 1572872 | tf_op jit(solution)/shard_map/ppermute | solution.py:520
  137.2 42.9 %collective-permute-start.4 = (bf16[256,8,128]{2,1,0:T(8,128)(2,1)S(1)}, bf16[256,8,128]{2,1,0:T(8,128)(2,1)S(1)}, u32[]{:S(2)}, u32[]{:S(2)}) collective-permute-start(bf16[256,8,128]{2,1,0:T(8,128)(2,1)S(1)} %get-tuple-element.10), channel_id=1, source_target_pairs={{0,8},{8,0},{16,24},{24,16},{1,9},{9,1},{17,25},{25,17},{2,10},{10... | collective-permute-start | bytes 1572872 | tf_op jit(solution)/shard_map/ppermute | solution.py:520
  137.2 42.9 %collective-permute-start.5 = (bf16[256,8,128]{2,1,0:T(8,128)(2,1)}, bf16[256,8,128]{2,1,0:T(8,128)(2,1)S(1)}, u32[]{:S(2)}, u32[]{:S(2)}) collective-permute-start(bf16[256,8,128]{2,1,0:T(8,128)(2,1)} %get-tuple-element.8), channel_id=1, source_target_pairs={{0,8},{8,0},{16,24},{24,16},{1,9},{9,1},{17,25},{25,17},{2,10},{10... | collective-permute-start | bytes 1572872 | tf_op jit(solution)/shard_map/ppermute | solution.py:520
  150.0 47.2 %copy-start.4 = (bf16[256,8,128]{2,1,0:T(8,128)(2,1)}, bf16[256,8,128]{2,1,0:T(8,128)(2,1)S(1)}, u32[]{:S(2)}) copy-start(bf16[256,8,128]{2,1,0:T(8,128)(2,1)S(1)} %collective-permute-done.refs_0_) | copy-start | bytes 1572868
  150.0 62.7 %collective-permute-start.1 = (bf16[256,8,128]{2,1,0:T(8,128)(2,1)S(1)}, bf16[256,8,128]{2,1,0:T(8,128)(2,1)S(1)}, u32[]{:S(2)}, u32[]{:S(2)}) collective-permute-start(bf16[256,8,128]{2,1,0:T(8,128)(2,1)S(1)} %collective-permute-done.refs_0_), channel_id=1, source_target_pairs={{0,8},{8,0},{16,24},{24,16},{1,9},{9,1},{17,25},{25,17},{2,10},{10... | collective-permute-start | bytes 1572872 | tf_op jit(solution)/shard_map/ppermute | solution.py:520
  159.2 38.1 %copy-start.5 = (bf16[256,8,128]{2,1,0:T(8,128)(2,1)}, bf16[256,8,128]{2,1,0:T(8,128)(2,1)S(1)}, u32[]{:S(2)}) copy-start(bf16[256,8,128]{2,1,0:T(8,128)(2,1)S(1)} %collective-permute-done.2.refs_1_) | copy-start | bytes 1572868
  159.2 53.5 %collective-permute-start.3 = (bf16[256,8,128]{2,1,0:T(8,128)(2,1)S(1)}, bf16[256,8,128]{2,1,0:T(8,128)(2,1)S(1)}, u32[]{:S(2)}, u32[]{:S(2)}) collective-permute-start(bf16[256,8,128]{2,1,0:T(8,128)(2,1)S(1)} %collective-permute-done.2.refs_1_), channel_id=1, source_target_pairs={{0,8},{8,0},{16,24},{24,16},{1,9},{9,1},{17,25},{25,17},{2,10},{10... | collective-permute-start | bytes 1572872 | tf_op jit(solution)/shard_map/ppermute | solution.py:520
  180.2 0.8 copy-start.8
  181.0 0.8 copy-start.9
  212.7 0.8 copy-start.6
  212.7 1.0 copy-start.7

commit v4 on v3

--- a/solution.py
+++ b/solution.py
@@ -303,45 +303,67 @@
 EIGHT = 8
 
 
-def turn_kernel(in_ref, out_ref, wide_ref):
+def turn_kernel(group_ref, in_ref, out_ref, near_ref, across_ref, wide_ref):
     chan_count, _, per, k2_count, lanes = in_ref.shape
-    channels = per * k2_count
+    pitch = per * chan_count + 1
 
     def spread(step, carry):
         source, e = step // per, step % per
         for k2 in range(0, k2_count, EIGHT):
             value = in_ref[source, 0, e, k2 : k2 + EIGHT, :].astype(jnp.float32)
-            row = (e + per * k2) * chan_count + source
-            wide_ref[pl.ds(row, EIGHT, stride=per * chan_count), :] = value
+            row = k2 * pitch + e * chan_count + source
+            wide_ref[pl.ds(row, EIGHT, stride=pitch), :] = value
         return carry
 
     lax.fori_loop(0, chan_count * per, spread, 0, unroll=4)
 
-    def narrow(step, carry):
-        base = pl.multiple_of(step * EIGHT, EIGHT)
-        rows = pl.ds(pl.multiple_of(step * EIGHT * chan_count, EIGHT * chan_count), EIGHT * chan_count)
-        value = wide_ref[rows, :].astype(jnp.bfloat16)
-        out_ref[0, pl.ds(base, EIGHT)] = value.reshape(EIGHT, chan_count, lanes)
+    def narrow(k2, carry):
+        base = pl.multiple_of(k2 * per, per)
+        for e in range(per):
+            rows = pl.ds(k2 * pitch + e * chan_count, chan_count)
+            out_ref[0, base + e] = wide_ref[rows, :].astype(jnp.bfloat16)
         return carry
 
-    lax.fori_loop(0, channels // EIGHT, narrow, 0, unroll=2)
-
-
-def turn(channel):
+    lax.fori_loop(0, k2_count, narrow, 0, unroll=2)
+
+    half, group = pl.program_id(0), group_ref[0]
+
+    @pl.when(half == 1 - group % 2)
+    def _():
+        near_ref[...] = out_ref[0]
+
+    @pl.when(half == 1 - group // 2)
+    def _():
+        across_ref[...] = out_ref[0]
+
+
+def turn(channel, group_id):
     chan_count, halves, per, k2_count, lanes = channel.shape
     channels = per * k2_count
+    one_half = (channels, chan_count, lanes)
     return pl.pallas_call(
         turn_kernel,
-        out_shape=jax.ShapeDtypeStruct((halves, channels, chan_count, lanes), jnp.bfloat16),
-        grid=(halves,),
-        in_specs=[
-            pl.BlockSpec((chan_count, 1, per, k2_count, lanes), lambda u: (0, u, 0, 0, 0))
+        out_shape=[
+            jax.ShapeDtypeStruct((halves,) + one_half, jnp.bfloat16),
+            jax.ShapeDtypeStruct(one_half, jnp.bfloat16),
+            jax.ShapeDtypeStruct(one_half, jnp.bfloat16),
         ],
-        out_specs=pl.BlockSpec((1, channels, chan_count, lanes), lambda u: (u, 0, 0, 0)),
-        scratch_shapes=[pltpu.VMEM((channels * chan_count, lanes), jnp.float32)],
+        grid_spec=pltpu.PrefetchScalarGridSpec(
+            num_scalar_prefetch=1,
+            grid=(halves,),
+            in_specs=[
+                pl.BlockSpec((chan_count, 1, per, k2_count, lanes), lambda u, g: (0, u, 0, 0, 0))
+            ],
+            out_specs=[
+                pl.BlockSpec((1,) + one_half, lambda u, g: (u, 0, 0, 0)),
+                pl.BlockSpec(one_half, lambda u, g: (0, 0, 0)),
+                pl.BlockSpec(one_half, lambda u, g: (0, 0, 0)),
+            ],
+            scratch_shapes=[pltpu.VMEM((k2_count * (per * chan_count + 1), lanes), jnp.float32)],
+        ),
         compiler_params=pltpu.CompilerParams(vmem_limit_bytes=VMEM_LIMIT),
         name="turn",
-    )(channel)
+    )(group_id, channel)
 
 
 def left_kernel(*refs):
@@ -358,13 +380,13 @@
         out_ref[0, step] = stacked.T[:sig_count].astype(jnp.bfloat16)
         return carry
 
-    lax.fori_loop(0, channels // 2, pair, 0, unroll=4)
+    lax.fori_loop(0, channels // 2, pair, 0, unroll=32)
 
 
 def left_operand(chunks):
     halves, channels, chan_count, lanes = chunks[0].shape
     depth = 2 * 2 * len(chunks) * chan_count
-    tile = 64
+    tile = 128
     return pl.pallas_call(
         left_kernel,
         out_shape=jax.ShapeDtypeStruct((halves, channels // 2, lanes // 2, depth), jnp.bfloat16),
@@ -377,12 +399,13 @@
     )(*chunks)
 
 
-def correlate_kernel(chunk_count, spec_count, place_ref, left_ref, *refs):
-    del place_ref
+def correlate_kernel(chunk_count, spec_count, group_ref, plan_ref, left_ref, *refs):
+    del group_ref, plan_ref
     chunk_refs = refs[:chunk_count]
     out_ref, sum_ref = refs[-2:]
     _, channels, chan_count, lanes = (1,) + chunk_refs[0].shape
     sig_count = lanes // 2
+    pitch = channels + 1
     sign = jnp.where(
         lax.broadcasted_iota(jnp.int32, (chan_count, lanes), 1) < sig_count, 1.0, -1.0
     ).astype(jnp.float32)
@@ -406,48 +429,67 @@
         for i in range(2):
             q = 2 * step + i
             for a in range(0, sig_count, EIGHT):
-                sum_ref[pl.ds(a * channels + q, EIGHT, stride=channels), :] = both[
+                sum_ref[pl.ds(a * pitch + q, EIGHT, stride=pitch), :] = both[
                     a : a + EIGHT, i * lanes : (i + 1) * lanes
                 ]
         return carry
 
-    lax.fori_loop(0, channels // 2, pair, 0, unroll=4)
+    lax.fori_loop(0, channels // 2, pair, 0, unroll=32)
 
     def finish(a, carry):
-        rows = pl.ds(pl.multiple_of(a * channels, channels), channels)
+        rows = pl.ds(a * pitch, channels)
         out_ref[0, a] = (sum_ref[rows, :] * (1.0 / spec_count)).astype(jnp.bfloat16)
         return carry
 
-    lax.fori_loop(0, sig_count, finish, 0, unroll=4)
-
-
-def correlate(left, chunks, place, rounds, spec_count, so_far):
+    lax.fori_loop(0, sig_count, finish, 0, unroll=16)
+
+
+def correlate(left, chunks, group_id, plan, distance, spec_count, so_far):
     channels, chan_count, lanes = chunks[0].shape
     sig_count, depth = left.shape[2:]
-    tile = 32
+    rounds = plan.shape[0]
+    tile = 128
+
+    def half_of(group):
+        return (group[0] > (group[0] ^ distance)).astype(jnp.int32)
+
+    def round_of(group, plan):
+        mate = group[0] ^ distance
+        found = jnp.int32(0)
+        for r in range(1, rounds):
+            found = jnp.where(plan[r, group[0]] == mate, r, found)
+        return found
+
     in_specs = [
-        pl.BlockSpec((1, tile // 2, sig_count, depth), lambda i, p: (p[1], i, 0, 0)),
-    ] + [pl.BlockSpec((tile, chan_count, lanes), lambda i, p: (i, 0, 0))] * len(chunks)
+        pl.BlockSpec((1, tile // 2, sig_count, depth), lambda i, g, p: (half_of(g), i, 0, 0)),
+    ] + [pl.BlockSpec((tile, chan_count, lanes), lambda i, g, p: (i, 0, 0))] * len(chunks)
     operands = [left, *chunks]
     aliases = {}
     if so_far is not None:
         in_specs.append(pl.BlockSpec(memory_space=pl.ANY))
         operands.append(so_far)
-        aliases = {len(operands): 0}
+        aliases = {len(operands) + 1: 0}
     return pl.pallas_call(
         functools.partial(correlate_kernel, len(chunks), spec_count),
         out_shape=jax.ShapeDtypeStruct((rounds, sig_count, channels, lanes), jnp.bfloat16),
         grid_spec=pltpu.PrefetchScalarGridSpec(
-            num_scalar_prefetch=1,
+            num_scalar_prefetch=2,
             grid=(channels // tile,),
             in_specs=in_specs,
-            out_specs=pl.BlockSpec((1, sig_count, tile, lanes), lambda i, p: (p[0], 0, i, 0)),
-            scratch_shapes=[pltpu.VMEM((sig_count * tile, lanes), jnp.float32)],
+            out_specs=pl.BlockSpec(
+                (1, sig_count, tile, lanes), lambda i, g, p: (round_of(g, p), 0, i, 0)
+            ),
+            scratch_shapes=[pltpu.VMEM((sig_count * (tile + 1), lanes), jnp.float32)],
         ),
         input_output_aliases=aliases,
         compiler_params=pltpu.CompilerParams(vmem_limit_bytes=VMEM_LIMIT),
+        cost_estimate=pl.CostEstimate(
+            flops=2 * channels * sig_count * depth * lanes,
+            bytes_accessed=16 * 1024 * 1024,
+            transcendentals=0,
+        ),
         name="correlate",
-    )(place, *operands)
+    )(group_id, plan, *operands)
 
 
 def correlate_plain(mine, theirs):
@@ -507,10 +549,9 @@
     _, frames, _ = voltages.shape
     chan_count = lax.axis_size("chan")
     group_count = lax.axis_size("grp")
-    rounds = plan.shape[0]
     spec_count = frames - TAPS + 1
     chan_id = lax.axis_index("chan").astype(jnp.int32)
-    group_id = lax.axis_index("grp").astype(jnp.int32)
+    group_id = lax.axis_index("grp").astype(jnp.int32).reshape(1)
     frames_first = voltages.transpose(1, 0, 2)
 
     def over_chan(value):
@@ -519,27 +560,28 @@
     def to_mate(value, distance):
         return lax.ppermute(value, "grp", [(g, g ^ distance) for g in range(group_count)])
 
-    group_ids = jnp.arange(group_count, dtype=jnp.int32)
-    partner = jnp.sum(jnp.where(group_ids[None, :] == group_id, plan, 0), axis=1)
     turned, near, across, relayed = [], [], [], []
+    channels = []
     for first in range(0, spec_count, chan_count):
         filtered = filter_taps(frames_first, chan_id, chan_count, first, chan_count)
-        channel = over_chan(transform(over_chan(filtered), True))
-        halves = turn(channel)
+        channels.append(over_chan(transform(over_chan(filtered), True)))
+    for index, channel in enumerate(channels):
+        if index:
+            channel, near, across, relayed = lax.optimization_barrier(
+                (channel, near, across, relayed)
+            )
+        halves, for_near, for_across = turn(channel, group_id)
         turned.append(halves)
-        for_near = lax.dynamic_index_in_dim(halves, 1 - group_id % 2, 0, keepdims=False)
-        for_across = lax.dynamic_index_in_dim(halves, 1 - group_id // 2, 0, keepdims=False)
-        near.append(to_mate(for_near, 1))
-        across.append(to_mate(for_across, 2))
-        relayed.append(to_mate(across[-1], 1))
+        near = near + [to_mate(for_near, 1)]
+        across = across + [to_mate(for_across, 2)]
+        if index + 1 < len(channels):
+            relayed = relayed + [to_mate(across[-1], 1)]
     left = left_operand(turned)
-    result = None
-    for distance, chunks in ((1, near), (2, across), (3, relayed)):
-        mate = group_id ^ distance
-        round_of = jnp.sum(jnp.where(partner == mate, jnp.arange(rounds, dtype=jnp.int32), 0))
-        place = jnp.stack([round_of, (group_id > mate).astype(jnp.int32)])
-        result = correlate(left, chunks, place, rounds, spec_count, result)
-    return result
+    result = correlate(left, near, group_id, plan, 1, spec_count, None)
+    across, result = lax.optimization_barrier((across, result))
+    relayed = relayed + [to_mate(across[-1], 1)]
+    result = correlate(left, across, group_id, plan, 2, spec_count, result)
+    return correlate(left, relayed, group_id, plan, 3, spec_count, result)
 
 
 def local(voltages, plan):

time: 230 us -> 162 us (0.70)
  Pallas kernels: 93.6 us -> 53.6 us
  waiting for transfers between devices: 104 us -> 82.6 us
  other arithmetic: 3.96 us -> 0 us
  local copies, waits for them, and re-layouts: 7.08 us -> 3.13 us
    pallas_call x3, Pallas kernels: 46.4 us -> 17.9 us  [correlate(): pl.pallas_call(functools.partial(correlate_kernel, len(chunks), spec_coun...]
    all_to_all x4, waiting for transfers between devices: 82.3 us -> 70.4 us  [over_chan(): lax.all_to_all(value, 'chan', split_axis=0, concat_axis=0, tiled=True)]
    pallas_call x1, Pallas kernels: 17 us -> 6.45 us  [left_operand(): pl.pallas_call(left_kernel, out_shape=jax.ShapeDtypeStruct((halves, chann...]
    ppermute x6, waiting for transfers between devices: 21.4 us -> 12.3 us  [to_mate(): lax.ppermute(value, 'grp', [(g, g ^ distance) for g in range(group_count)])]
    squeeze x2 -> x0, local copies, waits for them, and re-layouts: 3.52 us -> none  [local_overlapped(): lax.dynamic_index_in_dim(halves, 1 - group_id % 2, 0, keepdims=False)]
    another operation x2 -> x0, other arithmetic: 3.09 us -> none  [local_overlapped(): place = jnp.stack([round_of, (group_id > mate).astype(jnp.int32)])]
  transfers between devices with their start and end apart: 10 -> 10, of which waited for: 6 -> 5; matrix products, arithmetic and copies ran while one was open for 2% -> 0% of each run, Pallas kernels for 30% -> 24%
where the time goes in v4:
time: 162 us; the launch traced here: 161 us
  waiting for transfers between devices  82.6 us (51%)
  Pallas kernels  53.6 us (33%)
  starting transfers between devices  21.5 us (13%)
  local copies, waits for them, and re-layouts  3.13 us (2%)
    all_to_all x4, waiting for transfers between devices, over_chan(): lax.all_to_all(value, 'chan', split_axis=0, concat_axis=0, tiled=True)  70.4 us
    all_to_all x4, starting transfers between devices, over_chan(): lax.all_to_all(value, 'chan', split_axis=0, concat_axis=0, tiled=True)  18.2 us
    pallas_call x3, Pallas kernels, correlate(): pl.pallas_call(functools.partial(correlate_kernel, len(chunks), spec_coun...  17.9 us
    ppermute x6, waiting for transfers between devices, to_mate(): lax.ppermute(value, 'grp', [(g, g ^ distance) for g in range(group_count)])  12.3 us
    pallas_call x2, Pallas kernels, filter_taps(): pl.pallas_call(filter_kernel, out_shape=jax.ShapeDtypeStruct((spec_count,...  11.9 us
    pallas_call x2, Pallas kernels, transform(): pl.pallas_call(functools.partial(transform_kernel, chan_count, joined), o...  9.83 us
    pallas_call x2, Pallas kernels, turn(): pl.pallas_call(turn_kernel, out_shape=[jax.ShapeDtypeStruct((halves,) + o...  7.58 us
    pallas_call x1, Pallas kernels, left_operand(): pl.pallas_call(left_kernel, out_shape=jax.ShapeDtypeStruct((halves, chann...  6.45 us
  transfers between devices with their start and end apart: 10, of which 5 were waited for; matrix products, arithmetic and copies ran while one was open for 0% of the time, Pallas kernels for 24%

profile of v4, /device:TPU:0, one launch (start us, length us, event | category | flops | bytes accessed | tf_op | source)
XLA Modules:
  0.0 160.9 jit_solution(1066674906094018210)
XLA Ops:
  0.0 6.0 %filter_taps.2 = bf16[8,64,1024]{2,1,0:T(8,128)(2,1)} custom-call(s32[1]{0:T(128)} %bitcast.1.chan_ref, s32[31,64,1024]{2,1,0:T(8,128)} %bitcast.3, f32[8,16,1024]{2,1,0:T(8,128)} %constant.18.clone.coeff_ref), custom_call_target="tpu_custom_call" | custom-call | tf_op jit(solution)/shard_map/filter_taps/pallas_call | solution.py:56
  6.0 7.3 %all-to-all-start = ((bf16[8,64,1024]{2,1,0:T(8,128)(2,1)}), bf16[8,64,1024]{2,1,0:T(8,128)(2,1)S(1)}, u32[]{:S(2)}, u32[]{:S(2)}) async-start(bf16[8,64,1024]{2,1,0:T(8,128)(2,1)} %filter_taps.2), calls=%async_computation | async-start | bytes 2097152 | tf_op jit(solution)/shard_map/all_to_all | solution.py:558
  13.3 6.0 %filter_taps.3 = bf16[8,64,1024]{2,1,0:T(8,128)(2,1)} custom-call(s32[1]{0:T(128)} %bitcast.1.chan_ref, s32[31,64,1024]{2,1,0:T(8,128)} %bitcast.4, f32[8,16,1024]{2,1,0:T(8,128)} %constant.18.clone.coeff_ref), custom_call_target="tpu_custom_call" | custom-call | tf_op jit(solution)/shard_map/filter_taps/pallas_call | solution.py:56
  19.2 19.8 %all-to-all-done.in_ref = bf16[8,64,1024]{2,1,0:T(8,128)(2,1)S(1)} async-done(((bf16[8,64,1024]{2,1,0:T(8,128)(2,1)}), bf16[8,64,1024]{2,1,0:T(8,128)(2,1)S(1)}, u32[]{:S(2)}, u32[]{:S(2)}) %all-to-all-start) | async-done | bytes 1048608 | tf_op jit(solution)/shard_map/all_to_all | solution.py:558
  39.0 3.6 %all-to-all-start.2 = ((bf16[8,64,1024]{2,1,0:T(8,128)(2,1)}), bf16[8,64,1024]{2,1,0:T(8,128)(2,1)S(1)}, u32[]{:S(2)}, u32[]{:S(2)}) async-start(bf16[8,64,1024]{2,1,0:T(8,128)(2,1)} %filter_taps.3), calls=%async_computation.2 | async-start | bytes 2097152 | tf_op jit(solution)/shard_map/all_to_all | solution.py:558
  42.6 4.9 %transform.2 = bf16[8,2,8,32,128]{4,3,2,1,0:T(8,128)(2,1)} custom-call(bf16[8,64,1024]{2,1,0:T(8,128)(2,1)} %copy-done.1, f32[33,128]{1,0:T(8,128)} %constant.19.clone.cos_ref, f32[33,128]{1,0:T(8,128)} %constant.20.clone.sin_ref, bf16[256,256]{1,0:T(8,128)(2,1)} %constant.21.clone.wave_high_ref, bf16[256,256]{1,0:T(8,128)(2,1)} %constant.22.clone.wave_low_ref), custom_call_target="tpu_custom_call" | custom-call | tf_op jit(solution)/shard_map/transform/pallas_call | solution.py:288
  47.5 21.0 %all-to-all-done.2.in_ref = bf16[8,64,1024]{2,1,0:T(8,128)(2,1)S(1)} async-done(((bf16[8,64,1024]{2,1,0:T(8,128)(2,1)}), bf16[8,64,1024]{2,1,0:T(8,128)(2,1)S(1)}, u32[]{:S(2)}, u32[]{:S(2)}) %all-to-all-start.2) | async-done | bytes 1048608 | tf_op jit(solution)/shard_map/all_to_all | solution.py:558
  68.6 3.6 %all-to-all-start.1 = ((bf16[8,2,8,32,128]{4,3,2,1,0:T(8,128)(2,1)}), bf16[8,2,8,32,128]{4,3,2,1,0:T(8,128)(2,1)S(1)}, u32[]{:S(2)}, u32[]{:S(2)}) async-start(bf16[8,2,8,32,128]{4,3,2,1,0:T(8,128)(2,1)} %transform.2), calls=%async_computation.1 | async-start | bytes 2097152 | tf_op jit(solution)/shard_map/all_to_all | solution.py:558
  72.2 4.9 %transform.3 = bf16[8,2,8,32,128]{4,3,2,1,0:T(8,128)(2,1)} custom-call(bf16[8,64,1024]{2,1,0:T(8,128)(2,1)} %copy-done, f32[33,128]{1,0:T(8,128)} %constant.19.clone.cos_ref, f32[33,128]{1,0:T(8,128)} %constant.20.clone.sin_ref, bf16[256,256]{1,0:T(8,128)(2,1)} %constant.21.clone.wave_high_ref, bf16[256,256]{1,0:T(8,128)(2,1)} %constant.22.clone.wave_low_ref), custom_call_target="tpu_custom_call" | custom-call | tf_op jit(solution)/shard_map/transform/pallas_call | solution.py:288
  77.2 21.0 %all-to-all-done.1.in_ref = bf16[8,2,8,32,128]{4,3,2,1,0:T(8,128)(2,1)S(1)} async-done(((bf16[8,2,8,32,128]{4,3,2,1,0:T(8,128)(2,1)}), bf16[8,2,8,32,128]{4,3,2,1,0:T(8,128)(2,1)S(1)}, u32[]{:S(2)}, u32[]{:S(2)}) %all-to-all-start.1) | async-done | bytes 1048608 | tf_op jit(solution)/shard_map/all_to_all | solution.py:558
  98.2 3.6 %all-to-all-start.3 = ((bf16[8,2,8,32,128]{4,3,2,1,0:T(8,128)(2,1)}), bf16[8,2,8,32,128]{4,3,2,1,0:T(8,128)(2,1)S(1)}, u32[]{:S(2)}, u32[]{:S(2)}) async-start(bf16[8,2,8,32,128]{4,3,2,1,0:T(8,128)(2,1)} %transform.3), calls=%async_computation.3 | async-start | bytes 2097152 | tf_op jit(solution)/shard_map/all_to_all | solution.py:558
  101.8 3.7 %turn.2 = (bf16[2,256,8,128]{3,2,1,0:T(8,128)(2,1)}, bf16[256,8,128]{2,1,0:T(8,128)(2,1)}, bf16[256,8,128]{2,1,0:T(8,128)(2,1)}) custom-call(s32[1]{0:T(128)} %bitcast.group_ref, bf16[8,2,8,32,128]{4,3,2,1,0:T(8,128)(2,1)} %copy-done.3), custom_call_target="tpu_custom_call" | custom-call | tf_op jit(solution)/shard_map/turn/pallas_call | solution.py:344
  105.5 1.5 collective-permute-start.1
  107.0 12.3 %collective-permute-done.1.refs_0_ = bf16[256,8,128]{2,1,0:T(8,128)(2,1)S(1)} collective-permute-done((bf16[256,8,128]{2,1,0:T(8,128)(2,1)}, bf16[256,8,128]{2,1,0:T(8,128)(2,1)S(1)}, u32[]{:S(2)}, u32[]{:S(2)}) %collective-permute-start.1) | collective-permute-done | bytes 524320 | tf_op jit(solution)/shard_map/ppermute | solution.py:561
  119.3 8.5 %all-to-all-done.3.in_ref = bf16[8,2,8,32,128]{4,3,2,1,0:T(8,128)(2,1)S(1)} async-done(((bf16[8,2,8,32,128]{4,3,2,1,0:T(8,128)(2,1)}), bf16[8,2,8,32,128]{4,3,2,1,0:T(8,128)(2,1)S(1)}, u32[]{:S(2)}, u32[]{:S(2)}) %all-to-all-start.3) | async-done | bytes 1048608 | tf_op jit(solution)/shard_map/all_to_all | solution.py:558
  127.8 1.0 copy-done.2
  128.7 3.9 %turn.3 = (bf16[2,256,8,128]{3,2,1,0:T(8,128)(2,1)}, bf16[256,8,128]{2,1,0:T(8,128)(2,1)}, bf16[256,8,128]{2,1,0:T(8,128)(2,1)}) custom-call(s32[1]{0:T(128)} %bitcast.group_ref, bf16[8,2,8,32,128]{4,3,2,1,0:T(8,128)(2,1)} %copy-done.2), custom_call_target="tpu_custom_call" | custom-call | tf_op jit(solution)/shard_map/turn/pallas_call | solution.py:344
  132.7 1.6 collective-permute-start.3
  134.2 6.5 %left_operand.1.left_ref = bf16[2,128,64,64]{3,2,1,0:T(8,128)(2,1)} custom-call(bf16[2,256,8,128]{3,2,1,0:T(8,128)(2,1)} %get-tuple-element.18.refs_0_, bf16[2,256,8,128]{3,2,1,0:T(8,128)(2,1)} %get-tuple-element.22.refs_1_), custom_call_target="tpu_custom_call" | custom-call | tf_op jit(solution)/shard_map/left_operand/pallas_call | solution.py:390
  140.7 0.8 copy-done.9
  141.5 6.0 %correlate.3.refs_2_ = bf16[3,64,256,128]{3,2,1,0:T(8,128)(2,1)} custom-call(s32[1]{0:T(128)} %bitcast.group_ref, s32[3,4]{1,0:T(4,128)} %plan_ref.5, bf16[2,128,64,64]{3,2,1,0:T(8,128)(2,1)} %left_operand.1.left_ref, bf16[256,8,128]{2,1,0:T(8,128)(2,1)} %copy-done.8, bf16[256,8,128]{2,1,0:T(8,128)(2,1)} %copy-done.9), custom_call_target="tpu_custom_call" | custom-call | flops 268435456 | bytes 16777216 | tf_op jit(solution)/shard_map/correlate/pallas_call | solution.py:472
  148.2 5.9 %correlate.4.refs_2_ = bf16[3,64,256,128]{3,2,1,0:T(8,128)(2,1)} custom-call(s32[1]{0:T(128)} %bitcast.group_ref, s32[3,4]{1,0:T(4,128)} %plan_ref.5, bf16[2,128,64,64]{3,2,1,0:T(8,128)(2,1)} %left_operand.1.left_ref, bf16[256,8,128]{2,1,0:T(8,128)(2,1)} %copy-done.4, bf16[256,8,128]{2,1,0:T(8,128)(2,1)} %copy-done.6, ...), custom_call_target="tpu_custom_call", output_to_operand_aliasing={{}: (5, {})} | custom-call | flops 268435456 | bytes 16777216 | tf_op jit(solution)/shard_map/correlate/pallas_call | solution.py:472
  154.2 0.8 copy-done.7
  155.0 6.0 %correlate.5 = bf16[3,64,256,128]{3,2,1,0:T(8,128)(2,1)} custom-call(s32[1]{0:T(128)} %bitcast.group_ref, s32[3,4]{1,0:T(4,128)} %plan_ref.5, bf16[2,128,64,64]{3,2,1,0:T(8,128)(2,1)} %left_operand.1.left_ref, bf16[256,8,128]{2,1,0:T(8,128)(2,1)} %copy-done.5, bf16[256,8,128]{2,1,0:T(8,128)(2,1)} %copy-done.7, ...), custom_call_target="tpu_custom_call", output_to_operand_aliasing={{}: (5, {})} | custom-call | flops 268435456 | bytes 16777216 | tf_op jit(solution)/shard_map/correlate/pallas_call | solution.py:472
  (26 shorter events, 0.8 us)
Async XLA Ops:
  6.0 33.1 %all-to-all-start = ((bf16[8,64,1024]{2,1,0:T(8,128)(2,1)}), bf16[8,64,1024]{2,1,0:T(8,128)(2,1)S(1)}, u32[]{:S(2)}, u32[]{:S(2)}) async-start(bf16[8,64,1024]{2,1,0:T(8,128)(2,1)} %filter_taps.2), calls=%async_computation | async-start | bytes 2097152 | tf_op jit(solution)/shard_map/all_to_all | solution.py:558
  39.0 3.6 %copy-start.1 = (bf16[8,64,1024]{2,1,0:T(8,128)(2,1)}, bf16[8,64,1024]{2,1,0:T(8,128)(2,1)S(1)}, u32[]{:S(2)}) copy-start(bf16[8,64,1024]{2,1,0:T(8,128)(2,1)S(1)} %all-to-all-done.in_ref) | copy-start | bytes 3145732
  39.0 29.5 %all-to-all-start.2 = ((bf16[8,64,1024]{2,1,0:T(8,128)(2,1)}), bf16[8,64,1024]{2,1,0:T(8,128)(2,1)S(1)}, u32[]{:S(2)}, u32[]{:S(2)}) async-start(bf16[8,64,1024]{2,1,0:T(8,128)(2,1)} %filter_taps.3), calls=%async_computation.2 | async-start | bytes 2097152 | tf_op jit(solution)/shard_map/all_to_all | solution.py:558
  68.6 3.6 %copy-start = (bf16[8,64,1024]{2,1,0:T(8,128)(2,1)}, bf16[8,64,1024]{2,1,0:T(8,128)(2,1)S(1)}, u32[]{:S(2)}) copy-start(bf16[8,64,1024]{2,1,0:T(8,128)(2,1)S(1)} %all-to-all-done.2.in_ref) | copy-start | bytes 3145732
  68.6 29.6 %all-to-all-start.1 = ((bf16[8,2,8,32,128]{4,3,2,1,0:T(8,128)(2,1)}), bf16[8,2,8,32,128]{4,3,2,1,0:T(8,128)(2,1)S(1)}, u32[]{:S(2)}, u32[]{:S(2)}) async-start(bf16[8,2,8,32,128]{4,3,2,1,0:T(8,128)(2,1)} %transform.2), calls=%async_computation.1 | async-start | bytes 2097152 | tf_op jit(solution)/shard_map/all_to_all | solution.py:558
  98.2 3.6 %copy-start.3 = (bf16[8,2,8,32,128]{4,3,2,1,0:T(8,128)(2,1)}, bf16[8,2,8,32,128]{4,3,2,1,0:T(8,128)(2,1)S(1)}, u32[]{:S(2)}) copy-start(bf16[8,2,8,32,128]{4,3,2,1,0:T(8,128)(2,1)S(1)} %all-to-all-done.1.in_ref) | copy-start | bytes 3145732
  98.2 29.6 %all-to-all-start.3 = ((bf16[8,2,8,32,128]{4,3,2,1,0:T(8,128)(2,1)}), bf16[8,2,8,32,128]{4,3,2,1,0:T(8,128)(2,1)S(1)}, u32[]{:S(2)}, u32[]{:S(2)}) async-start(bf16[8,2,8,32,128]{4,3,2,1,0:T(8,128)(2,1)} %transform.3), calls=%async_computation.3 | async-start | bytes 2097152 | tf_op jit(solution)/shard_map/all_to_all | solution.py:558
  105.5 13.8 %collective-permute-start.1 = (bf16[256,8,128]{2,1,0:T(8,128)(2,1)}, bf16[256,8,128]{2,1,0:T(8,128)(2,1)S(1)}, u32[]{:S(2)}, u32[]{:S(2)}) collective-permute-start(bf16[256,8,128]{2,1,0:T(8,128)(2,1)} %get-tuple-element.20), channel_id=1, source_target_pairs={{0,16},{8,24},{16,0},{24,8},{1,17},{9,25},{17,1},{25,9},{2,18},{10... | collective-permute-start | bytes 1572872 | tf_op jit(solution)/shard_map/ppermute | solution.py:561
  107.0 20.8 %collective-permute-start = (bf16[256,8,128]{2,1,0:T(8,128)(2,1)}, bf16[256,8,128]{2,1,0:T(8,128)(2,1)S(1)}, u32[]{:S(2)}, u32[]{:S(2)}) collective-permute-start(bf16[256,8,128]{2,1,0:T(8,128)(2,1)} %get-tuple-element.19), channel_id=1, source_target_pairs={{0,8},{8,0},{16,24},{24,16},{1,9},{9,1},{17,25},{25,17},{2,10},{10... | collective-permute-start | bytes 1572872 | tf_op jit(solution)/shard_map/ppermute | solution.py:561
  119.3 28.4 %copy-start.4 = (bf16[256,8,128]{2,1,0:T(8,128)(2,1)}, bf16[256,8,128]{2,1,0:T(8,128)(2,1)S(1)}, u32[]{:S(2)}) copy-start(bf16[256,8,128]{2,1,0:T(8,128)(2,1)S(1)} %collective-permute-done.1.refs_0_) | copy-start | bytes 1572868
  119.3 8.5 %collective-permute-start.2 = (bf16[256,8,128]{2,1,0:T(8,128)(2,1)S(1)}, bf16[256,8,128]{2,1,0:T(8,128)(2,1)S(1)}, u32[]{:S(2)}, u32[]{:S(2)}) collective-permute-start(bf16[256,8,128]{2,1,0:T(8,128)(2,1)S(1)} %collective-permute-done.1.refs_0_), channel_id=1, source_target_pairs={{0,8},{8,0},{16,24},{24,16},{1,9},{9,1},{17,25},{25,17},{2,10},{10... | collective-permute-start | bytes 1572872 | tf_op jit(solution)/shard_map/ppermute | solution.py:561
  127.8 1.0 copy-start.2
  127.8 12.9 %copy-start.8 = (bf16[256,8,128]{2,1,0:T(8,128)(2,1)}, bf16[256,8,128]{2,1,0:T(8,128)(2,1)S(1)}, u32[]{:S(2)}) copy-start(bf16[256,8,128]{2,1,0:T(8,128)(2,1)S(1)} %collective-permute-done.refs_0_) | copy-start | bytes 1572868
  128.7 18.7 %copy-start.5 = (bf16[256,8,128]{2,1,0:T(8,128)(2,1)}, bf16[256,8,128]{2,1,0:T(8,128)(2,1)S(1)}, u32[]{:S(2)}) copy-start(bf16[256,8,128]{2,1,0:T(8,128)(2,1)S(1)} %collective-permute-done.2.refs_0_) | copy-start | bytes 1572868
  132.6 8.0 %collective-permute-start.4 = (bf16[256,8,128]{2,1,0:T(8,128)(2,1)}, bf16[256,8,128]{2,1,0:T(8,128)(2,1)S(1)}, u32[]{:S(2)}, u32[]{:S(2)}) collective-permute-start(bf16[256,8,128]{2,1,0:T(8,128)(2,1)} %get-tuple-element.27), channel_id=1, source_target_pairs={{0,8},{8,0},{16,24},{24,16},{1,9},{9,1},{17,25},{25,17},{2,10},{10... | collective-permute-start | bytes 1572872 | tf_op jit(solution)/shard_map/ppermute | solution.py:561
  132.7 14.8 %collective-permute-start.3 = (bf16[256,8,128]{2,1,0:T(8,128)(2,1)}, bf16[256,8,128]{2,1,0:T(8,128)(2,1)S(1)}, u32[]{:S(2)}, u32[]{:S(2)}) collective-permute-start(bf16[256,8,128]{2,1,0:T(8,128)(2,1)} %get-tuple-element.25), channel_id=1, source_target_pairs={{0,16},{8,24},{16,0},{24,8},{1,17},{9,25},{17,1},{25,9},{2,18},{10... | collective-permute-start | bytes 1572872 | tf_op jit(solution)/shard_map/ppermute | solution.py:561
  140.7 0.8 copy-start.9
  147.4 0.8 copy-start.6
  147.4 6.7 %collective-permute-start.5 = (bf16[256,8,128]{2,1,0:T(8,128)(2,1)S(1)}, bf16[256,8,128]{2,1,0:T(8,128)(2,1)S(1)}, u32[]{:S(2)}, u32[]{:S(2)}) collective-permute-start(bf16[256,8,128]{2,1,0:T(8,128)(2,1)S(1)} %collective-permute-done.3.refs_1_), channel_id=1, source_target_pairs={{0,8},{8,0},{16,24},{24,16},{1,9},{9,1},{17,25},{25,17},{2,10},{10... | collective-permute-start | bytes 1572872 | tf_op jit(solution)/shard_map/ppermute | solution.py:561
  154.2 0.8 copy-start.7

commit v5 on v4

--- a/solution.py
+++ b/solution.py
@@ -8,6 +8,7 @@
 from jax.experimental import pallas as pl
 from jax.experimental.pallas import tpu as pltpu
 from jax.sharding import PartitionSpec as P
+
 
 TAPS = 16
 LANES = 128
@@ -70,7 +71,42 @@
         ),
         compiler_params=pltpu.CompilerParams(vmem_limit_bytes=VMEM_LIMIT),
         name="filter_taps",
-    )(chan_id.reshape(1), frames_first, jnp.asarray(table))
+    )(chan_id, frames_first, jnp.asarray(table))
+
+
+def filter_by_shift_kernel(chan_ref, volt_ref, coeff_ref, *refs):
+    out_refs, block_ref = refs[:-1], refs[-1]
+    filter_kernel(chan_ref, volt_ref, coeff_ref, block_ref)
+    count = len(out_refs)
+    for shift, out_ref in enumerate(out_refs):
+        out_ref[...] = block_ref[lax.rem(chan_ref[0] + shift, count)]
+
+
+def filter_by_shift(frames_first, chan_id, chan_count, first):
+    _, sig_count, block_len = frames_first.shape
+    frames = chan_count + TAPS - 1
+    table = tap_table(block_len * chan_count).astype(np.float32)
+    table = np.ascontiguousarray(table.reshape(TAPS, chan_count, block_len).transpose(1, 0, 2))
+    sig_tile = 16
+    return pl.pallas_call(
+        filter_by_shift_kernel,
+        out_shape=[jax.ShapeDtypeStruct((sig_count, block_len), jnp.bfloat16)] * chan_count,
+        grid_spec=pltpu.PrefetchScalarGridSpec(
+            num_scalar_prefetch=1,
+            grid=(sig_count // sig_tile,),
+            in_specs=[
+                pl.BlockSpec(
+                    (pl.Element(frames), pl.Element(sig_tile), pl.Element(block_len)),
+                    lambda i, c: (first, i * sig_tile, 0),
+                ),
+                pl.BlockSpec((1, TAPS, block_len), lambda i, c: (c[0], 0, 0)),
+            ],
+            out_specs=[pl.BlockSpec((sig_tile, block_len), lambda i, c: (i, 0))] * chan_count,
+            scratch_shapes=[pltpu.VMEM((chan_count, sig_tile, block_len), jnp.bfloat16)],
+        ),
+        compiler_params=pltpu.CompilerParams(vmem_limit_bytes=VMEM_LIMIT),
+        name="filter_by_shift",
+    )(chan_id, frames_first, jnp.asarray(table))
 
 
 def cadd(a, b):
@@ -268,54 +304,107 @@
                     )
 
 
-def transform(samples, joined):
-    chan_count, rows, block_len = samples.shape
-    fft_len = chan_count * block_len
-    count = len(first_index_list())
+def transform_tables(fft_len):
     cos, sin = turn_tables(fft_len)
     wave = wave_matrix(fft_len)
     wave_high = wave.astype(jnp.bfloat16)
     wave_low = (wave - wave_high.astype(np.float64)).astype(jnp.bfloat16)
-    tables = (
+    return (
         jnp.asarray(cos, jnp.float32),
         jnp.asarray(sin, jnp.float32),
         jnp.asarray(wave_high),
         jnp.asarray(wave_low),
     )
+
+
+def transform_scratch(rows):
+    count = len(first_index_list())
+    return [
+        pltpu.VMEM((8, 5, 2, 16, LANES), jnp.float32),
+        pltpu.VMEM((count, rows, 2 * LANES), jnp.bfloat16),
+        pltpu.VMEM((count, rows, 2 * LANES), jnp.bfloat16),
+    ]
+
+
+def transform(samples):
+    chan_count, rows, block_len = samples.shape
     whole = pl.BlockSpec(memory_space=pltpu.VMEM)
-    shape = (chan_count, 2, RADIX // chan_count)
-    shape += (LANES // 4, 2 * rows) if joined else (2, LANES // 4, rows)
+    shape = (chan_count, 2, RADIX // chan_count, 2, LANES // 4, rows)
     return pl.pallas_call(
-        functools.partial(transform_kernel, chan_count, joined),
+        functools.partial(transform_kernel, chan_count, False),
         out_shape=jax.ShapeDtypeStruct(shape, jnp.bfloat16),
         in_specs=[whole] * 5,
         out_specs=whole,
-        scratch_shapes=[
-            pltpu.VMEM((8, 5, 2, 16, LANES), jnp.float32),
-            pltpu.VMEM((count, rows, 2 * LANES), jnp.bfloat16),
-            pltpu.VMEM((count, rows, 2 * LANES), jnp.bfloat16),
-        ],
+        scratch_shapes=transform_scratch(rows),
         compiler_params=pltpu.CompilerParams(vmem_limit_bytes=VMEM_LIMIT),
         name="transform",
-    )(samples, *tables)
+    )(samples, *transform_tables(chan_count * block_len))
+
+
+def transform_by_shift_kernel(chan_count, *refs):
+    chan_ref, tables = refs[0], refs[1:5]
+    in_refs, out_refs = refs[5 : 5 + chan_count], refs[5 + chan_count : 5 + 2 * chan_count]
+    block_ref, result_ref, mid_ref, high_ref, low_ref, in_sem, out_sem = refs[5 + 2 * chan_count :]
+    chan = chan_ref[0]
+    fetches = []
+    for shift, in_ref in enumerate(in_refs):
+        source = lax.rem(chan + chan_count - shift, chan_count)
+        fetches.append(pltpu.make_async_copy(in_ref, block_ref.at[source], in_sem.at[shift]))
+        fetches[-1].start()
+    for fetch in fetches:
+        fetch.wait()
+    transform_kernel(
+        chan_count, True, block_ref, *tables, result_ref, mid_ref, high_ref, low_ref
+    )
+    sends = []
+    for shift, out_ref in enumerate(out_refs):
+        target = lax.rem(chan + shift, chan_count)
+        sends.append(pltpu.make_async_copy(result_ref.at[target], out_ref, out_sem.at[shift]))
+        sends[-1].start()
+    for send in sends:
+        send.wait()
+
+
+def transform_by_shift(blocks, chan_id):
+    chan_count = len(blocks)
+    rows, block_len = blocks[0].shape
+    whole = pl.BlockSpec(memory_space=pltpu.VMEM)
+    apart = pl.BlockSpec(memory_space=pltpu.HBM)
+    shape = (2, RADIX // chan_count, LANES // 4, 2 * rows)
+    return pl.pallas_call(
+        functools.partial(transform_by_shift_kernel, chan_count),
+        out_shape=[jax.ShapeDtypeStruct(shape, jnp.bfloat16)] * chan_count,
+        in_specs=[pl.BlockSpec(memory_space=pltpu.SMEM)] + [whole] * 4 + [apart] * chan_count,
+        out_specs=[apart] * chan_count,
+        scratch_shapes=[
+            pltpu.VMEM((chan_count, rows, block_len), jnp.bfloat16),
+            pltpu.VMEM((chan_count,) + shape, jnp.bfloat16),
+        ]
+        + transform_scratch(rows)
+        + [pltpu.SemaphoreType.DMA((chan_count,)), pltpu.SemaphoreType.DMA((chan_count,))],
+        compiler_params=pltpu.CompilerParams(vmem_limit_bytes=VMEM_LIMIT),
+        name="transform_by_shift",
+    )(chan_id, *transform_tables(chan_count * block_len), *blocks)
 
 
 EIGHT = 8
 
 
-def turn_kernel(group_ref, in_ref, out_ref, near_ref, across_ref, wide_ref):
-    chan_count, _, per, k2_count, lanes = in_ref.shape
+def turn_kernel(group_ref, *refs):
+    in_refs, (out_ref, near_ref, across_ref, wide_ref) = refs[:-4], refs[-4:]
+    chan_count = len(in_refs)
+    _, per, k2_count, _ = in_refs[0].shape
     pitch = per * chan_count + 1
 
-    def spread(step, carry):
-        source, e = step // per, step % per
-        for k2 in range(0, k2_count, EIGHT):
-            value = in_ref[source, 0, e, k2 : k2 + EIGHT, :].astype(jnp.float32)
-            row = k2 * pitch + e * chan_count + source
-            wide_ref[pl.ds(row, EIGHT, stride=pitch), :] = value
+    def spread(e, carry):
+        for source, in_ref in enumerate(in_refs):
+            for k2 in range(0, k2_count, EIGHT):
+                value = in_ref[0, e, k2 : k2 + EIGHT, :].astype(jnp.float32)
+                row = k2 * pitch + e * chan_count + source
+                wide_ref[pl.ds(row, EIGHT, stride=pitch), :] = value
         return carry
 
-    lax.fori_loop(0, chan_count * per, spread, 0, unroll=4)
+    lax.fori_loop(0, per, spread, 0)
 
     def narrow(k2, carry):
         base = pl.multiple_of(k2 * per, per)
@@ -337,10 +426,10 @@
         across_ref[...] = out_ref[0]
 
 
-def turn(channel, group_id):
-    chan_count, halves, per, k2_count, lanes = channel.shape
-    channels = per * k2_count
-    one_half = (channels, chan_count, lanes)
+def turn(blocks, group_id):
+    chan_count = len(blocks)
+    halves, per, k2_count, lanes = blocks[0].shape
+    one_half = (per * k2_count, chan_count, lanes)
     return pl.pallas_call(
         turn_kernel,
         out_shape=[
@@ -351,9 +440,8 @@
         grid_spec=pltpu.PrefetchScalarGridSpec(
             num_scalar_prefetch=1,
             grid=(halves,),
-            in_specs=[
-                pl.BlockSpec((chan_count, 1, per, k2_count, lanes), lambda u, g: (0, u, 0, 0, 0))
-            ],
+            in_specs=[pl.BlockSpec((1, per, k2_count, lanes), lambda u, g: (u, 0, 0, 0))]
+            * chan_count,
             out_specs=[
                 pl.BlockSpec((1,) + one_half, lambda u, g: (u, 0, 0, 0)),
                 pl.BlockSpec(one_half, lambda u, g: (0, 0, 0)),
@@ -363,7 +451,7 @@
         ),
         compiler_params=pltpu.CompilerParams(vmem_limit_bytes=VMEM_LIMIT),
         name="turn",
-    )(group_id, channel)
+    )(group_id, *blocks)
 
 
 def left_kernel(*refs):
@@ -502,7 +590,7 @@
 
 
 def by_channel(half, sig_count, spec_count):
-    chan_count, per, parts, k2, rows = half.shape
+    _, per, parts, k2, _ = half.shape
     turned = half.transpose(3, 1, 0, 4, 2).reshape(k2 * per, spec_count, sig_count, parts)
     return turned.transpose(0, 2, 1, 3)
 
@@ -516,10 +604,11 @@
     chan_id = lax.axis_index("chan").astype(jnp.int32)
     group_id = lax.axis_index("grp")
 
-    filtered = filter_taps(voltages.transpose(1, 0, 2), chan_id, chan_count, 0, spec_count)
+    frames_first = voltages.transpose(1, 0, 2)
+    filtered = filter_taps(frames_first, chan_id.reshape(1), chan_count, 0, spec_count)
     filtered = filtered.reshape(chan_count, rows, block_len)
     frames_here = lax.all_to_all(filtered, "chan", split_axis=0, concat_axis=0, tiled=True)
-    spectra = transform(frames_here, False)
+    spectra = transform(frames_here)
     channel = lax.all_to_all(spectra, "chan", split_axis=0, concat_axis=0, tiled=True)
 
     lower_half, upper_half = channel[:, 0], channel[:, 1]
@@ -550,23 +639,30 @@
     chan_count = lax.axis_size("chan")
     group_count = lax.axis_size("grp")
     spec_count = frames - TAPS + 1
-    chan_id = lax.axis_index("chan").astype(jnp.int32)
+    chan_id = lax.axis_index("chan").astype(jnp.int32).reshape(1)
     group_id = lax.axis_index("grp").astype(jnp.int32).reshape(1)
     frames_first = voltages.transpose(1, 0, 2)
 
-    def over_chan(value):
-        return lax.all_to_all(value, "chan", split_axis=0, concat_axis=0, tiled=True)
+    def over_chan(blocks):
+        moved = [blocks[0]]
+        for shift in range(1, chan_count):
+            pairs = [(c, (c + shift) % chan_count) for c in range(chan_count)]
+            moved.append(lax.ppermute(blocks[shift], "chan", pairs))
+        return moved
 
     def to_mate(value, distance):
         return lax.ppermute(value, "grp", [(g, g ^ distance) for g in range(group_count)])
 
     turned, near, across, relayed = [], [], [], []
     channels = []
-    for first in range(0, spec_count, chan_count):
-        filtered = filter_taps(frames_first, chan_id, chan_count, first, chan_count)
-        channels.append(over_chan(transform(over_chan(filtered), True)))
-    for index, channel in enumerate(channels):
-        if index:
+    chunks = spec_count // chan_count
+    for chunk in range(chunks):
+        blocks = filter_by_shift(frames_first, chan_id, chan_count, chunk * chan_count)
+        blocks = over_chan(blocks)
+        blocks = transform_by_shift(blocks, chan_id)
+        channels.append(over_chan(blocks))
+    for chunk, channel in enumerate(channels):
+        if chunk:
             channel, near, across, relayed = lax.optimization_barrier(
                 (channel, near, across, relayed)
             )
@@ -574,7 +670,7 @@
         turned.append(halves)
         near = near + [to_mate(for_near, 1)]
         across = across + [to_mate(for_across, 2)]
-        if index + 1 < len(channels):
+        if chunk + 1 < chunks:
             relayed = relayed + [to_mate(across[-1], 1)]
     left = left_operand(turned)
     result = correlate(left, near, group_id, plan, 1, spec_count, None)
@@ -584,15 +680,18 @@
     return correlate(left, relayed, group_id, plan, 3, spec_count, result)
 
 
+def overlaps(group_count, chan_count):
+    return group_count == 4 and chan_count == EIGHT
+
+
 def local(voltages, plan):
     sig_count, frames, _ = voltages.shape
     chan_count = lax.axis_size("chan")
     group_count = lax.axis_size("grp")
     if (
-        group_count == 4
+        overlaps(group_count, chan_count)
         and plan.shape[0] == group_count - 1
-        and chan_count == EIGHT
-        and (frames - TAPS + 1) % chan_count == 0
+        and frames - TAPS + 1 == 2 * chan_count
         and 2 * sig_count == LANES
     ):
         return local_overlapped(voltages, plan)

time: 162 us -> 176 us (1.086)
  starting transfers between devices: 21.5 us -> 81.2 us
  waiting for transfers between devices: 82.6 us -> 34.6 us
  local copies, waits for them, and re-layouts: 3.13 us -> 5.05 us
    ppermute x0 -> x28, starting transfers between devices: none -> 78.5 us  [over_chan(): moved.append(lax.ppermute(blocks[shift], 'chan', pairs))]
    all_to_all x4 -> x0, waiting for transfers between devices: 70.4 us -> none  [over_chan(): lax.all_to_all(value, 'chan', split_axis=0, concat_axis=0, tiled=True)]
    ppermute x0 -> x28, waiting for transfers between devices: none -> 33.9 us  [over_chan(): moved.append(lax.ppermute(blocks[shift], 'chan', pairs))]
    all_to_all x4 -> x0, starting transfers between devices: 18.2 us -> none  [over_chan(): lax.all_to_all(value, 'chan', split_axis=0, concat_axis=0, tiled=True)]
    ppermute x6, waiting for transfers between devices: 12.3 us -> 0.72 us  [to_mate(): lax.ppermute(value, 'grp', [(g, g ^ distance) for g in range(group_count)])]
    pallas_call x4, Pallas kernels: 21.8 us -> 24 us  [the longest x2 12 us: filter_by_shift(): pl.pallas_call(filter_by_shift_kernel, out_shape=[jax.ShapeDtypeStruct((s...]
    unnamed x20 -> x68, local copies, waits for them, and re-layouts: 3.13 us -> 5.05 us
    pallas_call x2, Pallas kernels: 7.58 us -> 5.79 us  [turn(): pl.pallas_call(turn_kernel, out_shape=[jax.ShapeDtypeStruct((halves,) + o...]
  transfers between devices with their start and end apart: 10 -> 34, of which waited for: 5 -> 12; matrix products, arithmetic and copies ran while one was open for 0% -> 0% of each run, Pallas kernels for 24% -> 17%
where the time goes in v5:
time: 176 us; the launch traced here: 175 us
  starting transfers between devices  81.2 us (46%)
  Pallas kernels  54.1 us (31%)
  waiting for transfers between devices  34.6 us (20%)
  local copies, waits for them, and re-layouts  5.05 us (3%)
    ppermute x28, starting transfers between devices, over_chan(): moved.append(lax.ppermute(blocks[shift], 'chan', pairs))  78.5 us
    ppermute x28, waiting for transfers between devices, over_chan(): moved.append(lax.ppermute(blocks[shift], 'chan', pairs))  33.9 us
    pallas_call x3, Pallas kernels, correlate(): pl.pallas_call(functools.partial(correlate_kernel, len(chunks), spec_coun...  17.9 us
    pallas_call x2, Pallas kernels, filter_by_shift(): pl.pallas_call(filter_by_shift_kernel, out_shape=[jax.ShapeDtypeStruct((s...  12 us
    pallas_call x2, Pallas kernels, transform_by_shift(): pl.pallas_call(functools.partial(transform_by_shift_kernel, chan_count),...  12 us
    pallas_call x1, Pallas kernels, left_operand(): pl.pallas_call(left_kernel, out_shape=jax.ShapeDtypeStruct((halves, chann...  6.45 us
    pallas_call x2, Pallas kernels, turn(): pl.pallas_call(turn_kernel, out_shape=[jax.ShapeDtypeStruct((halves,) + o...  5.79 us
    unnamed x68, local copies, waits for them, and re-layouts  5.05 us
  transfers between devices with their start and end apart: 34, of which 12 were waited for; matrix products, arithmetic and copies ran while one was open for 0% of the time, Pallas kernels for 17%

profile of v5, /device:TPU:0, one launch (start us, length us, event | category | flops | bytes accessed | tf_op | source)
XLA Modules:
  0.0 175.3 jit_solution(7473593717021059587)
XLA Ops:
  0.0 6.0 %filter_by_shift.2 = (bf16[64,1024]{1,0:T(8,128)(2,1)}, bf16[64,1024]{1,0:T(8,128)(2,1)}, bf16[64,1024]{1,0:T(8,128)(2,1)}, bf16[64,1024]{1,0:T(8,128)(2,1)}, bf...) custom-call(s32[1]{0:T(128)} %bitcast.1.chan_ref.refs_0_, ...), custom_call_target="tpu_custom_call" | custom-call | tf_op jit(solution)/shard_map/filter_by_shift/pallas_call | solution.py:91
  6.0 3.1 %collective-permute-start = (bf16[64,1024]{1,0:T(8,128)(2,1)}, bf16[64,1024]{1,0:T(8,128)(2,1)S(1)}, u32[]{:S(2)}, u32[]{:S(2)}) collective-permute-start(bf16[64,1024]{1,0:T(8,128)(2,1)} %get-tuple-element.58), channel_id=1, source_target_pairs={{0,1},{1,2},{2,3},{3,4},{4,5},{5,6},{6,7},{7,0},{8,9},{9,10},{10,1... | collective-permute-start | bytes 393224 | tf_op jit(solution)/shard_map/ppermute | solution.py:650
  20.7 6.5 %collective-permute-done.2.refs_8_ = bf16[64,1024]{1,0:T(8,128)(2,1)S(1)} collective-permute-done((bf16[64,1024]{1,0:T(8,128)(2,1)}, bf16[64,1024]{1,0:T(8,128)(2,1)S(1)}, u32[]{:S(2)}, u32[]{:S(2)}) %collective-permute-start.2) | collective-permute-done | bytes 131104 | tf_op jit(solution)/shard_map/ppermute | solution.py:650
  28.3 6.0 %transform_by_shift.2 = (bf16[2,8,32,128]{3,2,1,0:T(8,128)(2,1)}, bf16[2,8,32,128]{3,2,1,0:T(8,128)(2,1)}, bf16[2,8,32,128]{3,2,1,0:T(8,128)(2,1)}, bf16[2,8,32,...) custom-call(s32[1]{0:T(128)} %bitcast.1.chan_ref.refs_0_, ...), custom_call_target="tpu_custom_call" | custom-call | tf_op jit(solution)/shard_map/transform_by_shift/pallas_call | solution.py:374
  34.3 4.3 %collective-permute-start.7 = (bf16[2,8,32,128]{3,2,1,0:T(8,128)(2,1)}, bf16[2,8,32,128]{3,2,1,0:T(8,128)(2,1)S(1)}, u32[]{:S(2)}, u32[]{:S(2)}) collective-permute-start(bf16[2,8,32,128]{3,2,1,0:T(8,128)(2,1)} %get-tuple-element.66), channel_id=1, source_target_pairs={{0,1},{1,2},{2,3},{3,4},{4,5},{5,6},{6,7},{7,0},{8,9},{9,10},{10,1... | collective-permute-start | bytes 393224 | tf_op jit(solution)/shard_map/ppermute | solution.py:650
  38.6 5.9 %collective-permute-start.8 = (bf16[2,8,32,128]{3,2,1,0:T(8,128)(2,1)}, bf16[2,8,32,128]{3,2,1,0:T(8,128)(2,1)S(1)}, u32[]{:S(2)}, u32[]{:S(2)}) collective-permute-start(bf16[2,8,32,128]{3,2,1,0:T(8,128)(2,1)} %get-tuple-element.67), channel_id=1, source_target_pairs={{0,2},{1,3},{2,4},{3,5},{4,6},{5,7},{6,0},{7,1},{8,10},{9,11},{10,... | collective-permute-start | bytes 393224 | tf_op jit(solution)/shard_map/ppermute | solution.py:650
  46.8 3.3 %collective-permute-start.11 = (bf16[2,8,32,128]{3,2,1,0:T(8,128)(2,1)}, bf16[2,8,32,128]{3,2,1,0:T(8,128)(2,1)S(1)}, u32[]{:S(2)}, u32[]{:S(2)}) collective-permute-start(bf16[2,8,32,128]{3,2,1,0:T(8,128)(2,1)} %get-tuple-element.70), channel_id=1, source_target_pairs={{0,5},{1,6},{2,7},{3,0},{4,1},{5,2},{6,3},{7,4},{8,13},{9,14},{10,... | collective-permute-start | bytes 393224 | tf_op jit(solution)/shard_map/ppermute | solution.py:650
  52.3 6.5 %collective-permute-done.9.refs_3_ = bf16[2,8,32,128]{3,2,1,0:T(8,128)(2,1)S(1)} collective-permute-done((bf16[2,8,32,128]{3,2,1,0:T(8,128)(2,1)}, bf16[2,8,32,128]{3,2,1,0:T(8,128)(2,1)S(1)}, u32[]{:S(2)}, u32[]{:S(2)}) %collective-permute-start.9) | collective-permute-done | bytes 131104 | tf_op jit(solution)/shard_map/ppermute | solution.py:650
  66.6 6.0 %filter_by_shift.3 = (bf16[64,1024]{1,0:T(8,128)(2,1)}, bf16[64,1024]{1,0:T(8,128)(2,1)}, bf16[64,1024]{1,0:T(8,128)(2,1)}, bf16[64,1024]{1,0:T(8,128)(2,1)}, bf...) custom-call(s32[1]{0:T(128)} %bitcast.1.chan_ref.refs_0_, ...), custom_call_target="tpu_custom_call" | custom-call | tf_op jit(solution)/shard_map/filter_by_shift/pallas_call | solution.py:91
  72.7 3.0 %collective-permute-start.14 = (bf16[64,1024]{1,0:T(8,128)(2,1)}, bf16[64,1024]{1,0:T(8,128)(2,1)S(1)}, u32[]{:S(2)}, u32[]{:S(2)}) collective-permute-start(bf16[64,1024]{1,0:T(8,128)(2,1)} %get-tuple-element.75), channel_id=1, source_target_pairs={{0,1},{1,2},{2,3},{3,4},{4,5},{5,6},{6,7},{7,0},{8,9},{9,10},{10,1... | collective-permute-start | bytes 393224 | tf_op jit(solution)/shard_map/ppermute | solution.py:650
  75.6 6.0 %collective-permute-start.15 = (bf16[64,1024]{1,0:T(8,128)(2,1)}, bf16[64,1024]{1,0:T(8,128)(2,1)S(1)}, u32[]{:S(2)}, u32[]{:S(2)}) collective-permute-start(bf16[64,1024]{1,0:T(8,128)(2,1)} %get-tuple-element.76), channel_id=1, source_target_pairs={{0,2},{1,3},{2,4},{3,5},{4,6},{5,7},{6,0},{7,1},{8,10},{9,11},{10,... | collective-permute-start | bytes 393224 | tf_op jit(solution)/shard_map/ppermute | solution.py:650
  89.1 6.4 %collective-permute-done.16.refs_8_ = bf16[64,1024]{1,0:T(8,128)(2,1)S(1)} collective-permute-done((bf16[64,1024]{1,0:T(8,128)(2,1)}, bf16[64,1024]{1,0:T(8,128)(2,1)S(1)}, u32[]{:S(2)}, u32[]{:S(2)}) %collective-permute-start.16) | collective-permute-done | bytes 131104 | tf_op jit(solution)/shard_map/ppermute | solution.py:650
  95.5 7.1 %collective-permute-start.20 = (bf16[64,1024]{1,0:T(8,128)(2,1)}, bf16[64,1024]{1,0:T(8,128)(2,1)S(1)}, u32[]{:S(2)}, u32[]{:S(2)}) collective-permute-start(bf16[64,1024]{1,0:T(8,128)(2,1)} %get-tuple-element.81), channel_id=1, source_target_pairs={{0,7},{1,0},{2,1},{3,2},{4,3},{5,4},{6,5},{7,6},{8,15},{9,8},{10,9... | collective-permute-start | bytes 393224 | tf_op jit(solution)/shard_map/ppermute | solution.py:650
  106.0 6.0 %transform_by_shift.3 = (bf16[2,8,32,128]{3,2,1,0:T(8,128)(2,1)}, bf16[2,8,32,128]{3,2,1,0:T(8,128)(2,1)}, bf16[2,8,32,128]{3,2,1,0:T(8,128)(2,1)}, bf16[2,8,32,...) custom-call(s32[1]{0:T(128)} %bitcast.1.chan_ref.refs_0_, ...), custom_call_target="tpu_custom_call" | custom-call | tf_op jit(solution)/shard_map/transform_by_shift/pallas_call | solution.py:374
  112.1 3.3 %collective-permute-start.22 = (bf16[2,8,32,128]{3,2,1,0:T(8,128)(2,1)}, bf16[2,8,32,128]{3,2,1,0:T(8,128)(2,1)S(1)}, u32[]{:S(2)}, u32[]{:S(2)}) collective-permute-start(bf16[2,8,32,128]{3,2,1,0:T(8,128)(2,1)} %get-tuple-element.84), channel_id=1, source_target_pairs={{0,2},{1,3},{2,4},{3,5},{4,6},{5,7},{6,0},{7,1},{8,10},{9,11},{10,... | collective-permute-start | bytes 393224 | tf_op jit(solution)/shard_map/ppermute | solution.py:650
  115.5 3.3 %collective-permute-start.23 = (bf16[2,8,32,128]{3,2,1,0:T(8,128)(2,1)}, bf16[2,8,32,128]{3,2,1,0:T(8,128)(2,1)S(1)}, u32[]{:S(2)}, u32[]{:S(2)}) collective-permute-start(bf16[2,8,32,128]{3,2,1,0:T(8,128)(2,1)} %get-tuple-element.85), channel_id=1, source_target_pairs={{0,3},{1,4},{2,5},{3,6},{4,7},{5,0},{6,1},{7,2},{8,11},{9,12},{10,... | collective-permute-start | bytes 393224 | tf_op jit(solution)/shard_map/ppermute | solution.py:650
  118.7 3.0 %collective-permute-done.21.refs_1_ = bf16[2,8,32,128]{3,2,1,0:T(8,128)(2,1)S(1)} collective-permute-done((bf16[2,8,32,128]{3,2,1,0:T(8,128)(2,1)}, bf16[2,8,32,128]{3,2,1,0:T(8,128)(2,1)S(1)}, u32[]{:S(2)}, u32[]{:S(2)}) %collective-permute-start.21) | collective-permute-done | bytes 131104 | tf_op jit(solution)/shard_map/ppermute | solution.py:650
  122.5 12.5 %collective-permute-start.25 = (bf16[2,8,32,128]{3,2,1,0:T(8,128)(2,1)}, bf16[2,8,32,128]{3,2,1,0:T(8,128)(2,1)S(1)}, u32[]{:S(2)}, u32[]{:S(2)}) collective-permute-start(bf16[2,8,32,128]{3,2,1,0:T(8,128)(2,1)} %get-tuple-element.87), channel_id=1, source_target_pairs={{0,5},{1,6},{2,7},{3,0},{4,1},{5,2},{6,3},{7,4},{8,13},{9,14},{10,... | collective-permute-start | bytes 393224 | tf_op jit(solution)/shard_map/ppermute | solution.py:650
  135.0 3.4 %collective-permute-start.26 = (bf16[2,8,32,128]{3,2,1,0:T(8,128)(2,1)}, bf16[2,8,32,128]{3,2,1,0:T(8,128)(2,1)S(1)}, u32[]{:S(2)}, u32[]{:S(2)}) collective-permute-start(bf16[2,8,32,128]{3,2,1,0:T(8,128)(2,1)} %get-tuple-element.88), channel_id=1, source_target_pairs={{0,6},{1,7},{2,0},{3,1},{4,2},{5,3},{6,4},{7,5},{8,14},{9,15},{10,... | collective-permute-start | bytes 393224 | tf_op jit(solution)/shard_map/ppermute | solution.py:650
  144.2 3.0 %turn.3 = (bf16[2,256,8,128]{3,2,1,0:T(8,128)(2,1)}, bf16[256,8,128]{2,1,0:T(8,128)(2,1)}, bf16[256,8,128]{2,1,0:T(8,128)(2,1)}) custom-call(s32[1]{0:T(128)} %bitcast.group_ref, bf16[2,8,32,128]{3,2,1,0:T(8,128)(2,1)} %get-tuple-element.92.refs_0_, bf16[2,8,32,128]{3,2,1,0:T(8,128)(2,1)} %copy-done.21, bf16[2,8,32,128]{3,2,1,0:T(8,128)(2,1)} %copy-done.23, ...), custom_call_target="tpu_custom_call" | custom-call | tf_op jit(solution)/shard_map/turn/pallas_call | solution.py:433
  147.8 6.5 %left_operand.1.left_ref = bf16[2,128,64,64]{3,2,1,0:T(8,128)(2,1)} custom-call(bf16[2,256,8,128]{3,2,1,0:T(8,128)(2,1)} %get-tuple-element.73.refs_0_, bf16[2,256,8,128]{3,2,1,0:T(8,128)(2,1)} %get-tuple-element.100.refs_1_), custom_call_target="tpu_custom_call" | custom-call | tf_op jit(solution)/shard_map/left_operand/pallas_call | solution.py:478
  155.1 5.9 %correlate.3.refs_2_ = bf16[3,64,256,128]{3,2,1,0:T(8,128)(2,1)} custom-call(s32[1]{0:T(128)} %bitcast.group_ref, s32[3,4]{1,0:T(4,128)} %plan_ref.5, bf16[2,128,64,64]{3,2,1,0:T(8,128)(2,1)} %left_operand.1.left_ref, bf16[256,8,128]{2,1,0:T(8,128)(2,1)} %copy-done.4, bf16[256,8,128]{2,1,0:T(8,128)(2,1)} %copy-done.5), custom_call_target="tpu_custom_call" | custom-call | flops 268435456 | bytes 16777216 | tf_op jit(solution)/shard_map/correlate/pallas_call | solution.py:560
  162.6 6.0 %correlate.4.refs_2_ = bf16[3,64,256,128]{3,2,1,0:T(8,128)(2,1)} custom-call(s32[1]{0:T(128)} %bitcast.group_ref, s32[3,4]{1,0:T(4,128)} %plan_ref.5, bf16[2,128,64,64]{3,2,1,0:T(8,128)(2,1)} %left_operand.1.left_ref, bf16[256,8,128]{2,1,0:T(8,128)(2,1)} %copy-done, bf16[256,8,128]{2,1,0:T(8,128)(2,1)} %copy-done.2, ...), custom_call_target="tpu_custom_call", output_to_operand_aliasing={{}: (5, {})} | custom-call | flops 268435456 | bytes 16777216 | tf_op jit(solution)/shard_map/correlate/pallas_call | solution.py:560
  169.3 6.0 %correlate.5 = bf16[3,64,256,128]{3,2,1,0:T(8,128)(2,1)} custom-call(s32[1]{0:T(128)} %bitcast.group_ref, s32[3,4]{1,0:T(4,128)} %plan_ref.5, bf16[2,128,64,64]{3,2,1,0:T(8,128)(2,1)} %left_operand.1.left_ref, bf16[256,8,128]{2,1,0:T(8,128)(2,1)} %copy-done.1, bf16[256,8,128]{2,1,0:T(8,128)(2,1)} %copy-done.3, ...), custom_call_target="tpu_custom_call", output_to_operand_aliasing={{}: (5, {})} | custom-call | flops 268435456 | bytes 16777216 | tf_op jit(solution)/shard_map/correlate/pallas_call | solution.py:560
  (122 shorter events, 46.2 us)
Async XLA Ops:
  6.0 11.1 %collective-permute-start = (bf16[64,1024]{1,0:T(8,128)(2,1)}, bf16[64,1024]{1,0:T(8,128)(2,1)S(1)}, u32[]{:S(2)}, u32[]{:S(2)}) collective-permute-start(bf16[64,1024]{1,0:T(8,128)(2,1)} %get-tuple-element.58), channel_id=1, source_target_pairs={{0,1},{1,2},{2,3},{3,4},{4,5},{5,6},{6,7},{7,0},{8,9},{9,10},{10,1... | collective-permute-start | bytes 393224 | tf_op jit(solution)/shard_map/ppermute | solution.py:650
  10.6 16.5 %collective-permute-start.2 = (bf16[64,1024]{1,0:T(8,128)(2,1)}, bf16[64,1024]{1,0:T(8,128)(2,1)S(1)}, u32[]{:S(2)}, u32[]{:S(2)}) collective-permute-start(bf16[64,1024]{1,0:T(8,128)(2,1)} %get-tuple-element.60), channel_id=1, source_target_pairs={{0,3},{1,4},{2,5},{3,6},{4,7},{5,0},{6,1},{7,2},{8,11},{9,12},{10,... | collective-permute-start | bytes 393224 | tf_op jit(solution)/shard_map/ppermute | solution.py:650
  13.2 14.3 %collective-permute-start.3 = (bf16[64,1024]{1,0:T(8,128)(2,1)}, bf16[64,1024]{1,0:T(8,128)(2,1)S(1)}, u32[]{:S(2)}, u32[]{:S(2)}) collective-permute-start(bf16[64,1024]{1,0:T(8,128)(2,1)} %get-tuple-element.61), channel_id=1, source_target_pairs={{0,4},{1,5},{2,6},{3,7},{4,0},{5,1},{6,2},{7,3},{8,12},{9,13},{10,... | collective-permute-start | bytes 393224 | tf_op jit(solution)/shard_map/ppermute | solution.py:650
  14.4 13.1 %collective-permute-start.4 = (bf16[64,1024]{1,0:T(8,128)(2,1)}, bf16[64,1024]{1,0:T(8,128)(2,1)S(1)}, u32[]{:S(2)}, u32[]{:S(2)}) collective-permute-start(bf16[64,1024]{1,0:T(8,128)(2,1)} %get-tuple-element.62), channel_id=1, source_target_pairs={{0,5},{1,6},{2,7},{3,0},{4,1},{5,2},{6,3},{7,4},{8,13},{9,14},{10,... | collective-permute-start | bytes 393224 | tf_op jit(solution)/shard_map/ppermute | solution.py:650
  17.1 10.5 %collective-permute-start.5 = (bf16[64,1024]{1,0:T(8,128)(2,1)}, bf16[64,1024]{1,0:T(8,128)(2,1)S(1)}, u32[]{:S(2)}, u32[]{:S(2)}) collective-permute-start(bf16[64,1024]{1,0:T(8,128)(2,1)} %get-tuple-element.63), channel_id=1, source_target_pairs={{0,6},{1,7},{2,0},{3,1},{4,2},{5,3},{6,4},{7,5},{8,14},{9,15},{10,... | collective-permute-start | bytes 393224 | tf_op jit(solution)/shard_map/ppermute | solution.py:650
  34.3 15.7 %collective-permute-start.7 = (bf16[2,8,32,128]{3,2,1,0:T(8,128)(2,1)}, bf16[2,8,32,128]{3,2,1,0:T(8,128)(2,1)S(1)}, u32[]{:S(2)}, u32[]{:S(2)}) collective-permute-start(bf16[2,8,32,128]{3,2,1,0:T(8,128)(2,1)} %get-tuple-element.66), channel_id=1, source_target_pairs={{0,1},{1,2},{2,3},{3,4},{4,5},{5,6},{6,7},{7,0},{8,9},{9,10},{10,1... | collective-permute-start | bytes 393224 | tf_op jit(solution)/shard_map/ppermute | solution.py:650
  38.6 13.1 %collective-permute-start.8 = (bf16[2,8,32,128]{3,2,1,0:T(8,128)(2,1)}, bf16[2,8,32,128]{3,2,1,0:T(8,128)(2,1)S(1)}, u32[]{:S(2)}, u32[]{:S(2)}) collective-permute-start(bf16[2,8,32,128]{3,2,1,0:T(8,128)(2,1)} %get-tuple-element.67), channel_id=1, source_target_pairs={{0,2},{1,3},{2,4},{3,5},{4,6},{5,7},{6,0},{7,1},{8,10},{9,11},{10,... | collective-permute-start | bytes 393224 | tf_op jit(solution)/shard_map/ppermute | solution.py:650
  44.5 14.3 %collective-permute-start.9 = (bf16[2,8,32,128]{3,2,1,0:T(8,128)(2,1)}, bf16[2,8,32,128]{3,2,1,0:T(8,128)(2,1)S(1)}, u32[]{:S(2)}, u32[]{:S(2)}) collective-permute-start(bf16[2,8,32,128]{3,2,1,0:T(8,128)(2,1)} %get-tuple-element.68), channel_id=1, source_target_pairs={{0,3},{1,4},{2,5},{3,6},{4,7},{5,0},{6,1},{7,2},{8,11},{9,12},{10,... | collective-permute-start | bytes 393224 | tf_op jit(solution)/shard_map/ppermute | solution.py:650
  45.1 15.1 %collective-permute-start.10 = (bf16[2,8,32,128]{3,2,1,0:T(8,128)(2,1)}, bf16[2,8,32,128]{3,2,1,0:T(8,128)(2,1)S(1)}, u32[]{:S(2)}, u32[]{:S(2)}) collective-permute-start(bf16[2,8,32,128]{3,2,1,0:T(8,128)(2,1)} %get-tuple-element.69), channel_id=1, source_target_pairs={{0,4},{1,5},{2,6},{3,7},{4,0},{5,1},{6,2},{7,3},{8,12},{9,13},{10,... | collective-permute-start | bytes 393224 | tf_op jit(solution)/shard_map/ppermute | solution.py:650
  46.8 13.4 %collective-permute-start.11 = (bf16[2,8,32,128]{3,2,1,0:T(8,128)(2,1)}, bf16[2,8,32,128]{3,2,1,0:T(8,128)(2,1)S(1)}, u32[]{:S(2)}, u32[]{:S(2)}) collective-permute-start(bf16[2,8,32,128]{3,2,1,0:T(8,128)(2,1)} %get-tuple-element.70), channel_id=1, source_target_pairs={{0,5},{1,6},{2,7},{3,0},{4,1},{5,2},{6,3},{7,4},{8,13},{9,14},{10,... | collective-permute-start | bytes 393224 | tf_op jit(solution)/shard_map/ppermute | solution.py:650
  65.1 37.5 %collective-permute-start.29 = (bf16[256,8,128]{2,1,0:T(8,128)(2,1)}, bf16[256,8,128]{2,1,0:T(8,128)(2,1)S(1)}, u32[]{:S(2)}, u32[]{:S(2)}) collective-permute-start(bf16[256,8,128]{2,1,0:T(8,128)(2,1)} %get-tuple-element.91), channel_id=1, source_target_pairs={{0,16},{8,24},{16,0},{24,8},{1,17},{9,25},{17,1},{25,9},{2,18},{10... | collective-permute-start | bytes 1572872 | tf_op jit(solution)/shard_map/ppermute | solution.py:654
  72.7 13.4 %collective-permute-start.14 = (bf16[64,1024]{1,0:T(8,128)(2,1)}, bf16[64,1024]{1,0:T(8,128)(2,1)S(1)}, u32[]{:S(2)}, u32[]{:S(2)}) collective-permute-start(bf16[64,1024]{1,0:T(8,128)(2,1)} %get-tuple-element.75), channel_id=1, source_target_pairs={{0,1},{1,2},{2,3},{3,4},{4,5},{5,6},{6,7},{7,0},{8,9},{9,10},{10,1... | collective-permute-start | bytes 393224 | tf_op jit(solution)/shard_map/ppermute | solution.py:650
  75.6 11.8 %collective-permute-start.15 = (bf16[64,1024]{1,0:T(8,128)(2,1)}, bf16[64,1024]{1,0:T(8,128)(2,1)S(1)}, u32[]{:S(2)}, u32[]{:S(2)}) collective-permute-start(bf16[64,1024]{1,0:T(8,128)(2,1)} %get-tuple-element.76), channel_id=1, source_target_pairs={{0,2},{1,3},{2,4},{3,5},{4,6},{5,7},{6,0},{7,1},{8,10},{9,11},{10,... | collective-permute-start | bytes 393224 | tf_op jit(solution)/shard_map/ppermute | solution.py:650
  81.6 13.9 %collective-permute-start.16 = (bf16[64,1024]{1,0:T(8,128)(2,1)}, bf16[64,1024]{1,0:T(8,128)(2,1)S(1)}, u32[]{:S(2)}, u32[]{:S(2)}) collective-permute-start(bf16[64,1024]{1,0:T(8,128)(2,1)} %get-tuple-element.77), channel_id=1, source_target_pairs={{0,3},{1,4},{2,5},{3,6},{4,7},{5,0},{6,1},{7,2},{8,11},{9,12},{10,... | collective-permute-start | bytes 393224 | tf_op jit(solution)/shard_map/ppermute | solution.py:650
  82.0 20.5 %collective-permute-start.17 = (bf16[64,1024]{1,0:T(8,128)(2,1)}, bf16[64,1024]{1,0:T(8,128)(2,1)S(1)}, u32[]{:S(2)}, u32[]{:S(2)}) collective-permute-start(bf16[64,1024]{1,0:T(8,128)(2,1)} %get-tuple-element.78), channel_id=1, source_target_pairs={{0,4},{1,5},{2,6},{3,7},{4,0},{5,1},{6,2},{7,3},{8,12},{9,13},{10,... | collective-permute-start | bytes 393224 | tf_op jit(solution)/shard_map/ppermute | solution.py:650
  86.1 17.0 %collective-permute-start.18 = (bf16[64,1024]{1,0:T(8,128)(2,1)}, bf16[64,1024]{1,0:T(8,128)(2,1)S(1)}, u32[]{:S(2)}, u32[]{:S(2)}) collective-permute-start(bf16[64,1024]{1,0:T(8,128)(2,1)} %get-tuple-element.79), channel_id=1, source_target_pairs={{0,5},{1,6},{2,7},{3,0},{4,1},{5,2},{6,3},{7,4},{8,13},{9,14},{10,... | collective-permute-start | bytes 393224 | tf_op jit(solution)/shard_map/ppermute | solution.py:650
  87.5 15.6 %collective-permute-start.19 = (bf16[64,1024]{1,0:T(8,128)(2,1)}, bf16[64,1024]{1,0:T(8,128)(2,1)S(1)}, u32[]{:S(2)}, u32[]{:S(2)}) collective-permute-start(bf16[64,1024]{1,0:T(8,128)(2,1)} %get-tuple-element.80), channel_id=1, source_target_pairs={{0,6},{1,7},{2,0},{3,1},{4,2},{5,3},{6,4},{7,5},{8,14},{9,15},{10,... | collective-permute-start | bytes 393224 | tf_op jit(solution)/shard_map/ppermute | solution.py:650
  102.6 40.9 %collective-permute-start.28 = (bf16[256,8,128]{2,1,0:T(8,128)(2,1)}, bf16[256,8,128]{2,1,0:T(8,128)(2,1)S(1)}, u32[]{:S(2)}, u32[]{:S(2)}) collective-permute-start(bf16[256,8,128]{2,1,0:T(8,128)(2,1)} %get-tuple-element.90), channel_id=1, source_target_pairs={{0,8},{8,0},{16,24},{24,16},{1,9},{9,1},{17,25},{25,17},{2,10},{10... | collective-permute-start | bytes 1572872 | tf_op jit(solution)/shard_map/ppermute | solution.py:654
  102.6 40.9 %collective-permute-start.30 = (bf16[256,8,128]{2,1,0:T(8,128)(2,1)S(1)}, bf16[256,8,128]{2,1,0:T(8,128)(2,1)S(1)}, u32[]{:S(2)}, u32[]{:S(2)}) collective-permute-start(bf16[256,8,128]{2,1,0:T(8,128)(2,1)S(1)} %collective-permute-done.29.refs_0_), channel_id=1, source_target_pairs={{0,8},{8,0},{16,24},{24,16},{1,9},{9,1},{17,25},{25,17},{2,10},{10... | collective-permute-start | bytes 1572872 | tf_op jit(solution)/shard_map/ppermute | solution.py:654
  112.1 10.3 %collective-permute-start.22 = (bf16[2,8,32,128]{3,2,1,0:T(8,128)(2,1)}, bf16[2,8,32,128]{3,2,1,0:T(8,128)(2,1)S(1)}, u32[]{:S(2)}, u32[]{:S(2)}) collective-permute-start(bf16[2,8,32,128]{3,2,1,0:T(8,128)(2,1)} %get-tuple-element.84), channel_id=1, source_target_pairs={{0,2},{1,3},{2,4},{3,5},{4,6},{5,7},{6,0},{7,1},{8,10},{9,11},{10,... | collective-permute-start | bytes 393224 | tf_op jit(solution)/shard_map/ppermute | solution.py:650
  115.5 19.5 %collective-permute-start.23 = (bf16[2,8,32,128]{3,2,1,0:T(8,128)(2,1)}, bf16[2,8,32,128]{3,2,1,0:T(8,128)(2,1)S(1)}, u32[]{:S(2)}, u32[]{:S(2)}) collective-permute-start(bf16[2,8,32,128]{3,2,1,0:T(8,128)(2,1)} %get-tuple-element.85), channel_id=1, source_target_pairs={{0,3},{1,4},{2,5},{3,6},{4,7},{5,0},{6,1},{7,2},{8,11},{9,12},{10,... | collective-permute-start | bytes 393224 | tf_op jit(solution)/shard_map/ppermute | solution.py:650
  121.8 16.5 %collective-permute-start.24 = (bf16[2,8,32,128]{3,2,1,0:T(8,128)(2,1)}, bf16[2,8,32,128]{3,2,1,0:T(8,128)(2,1)S(1)}, u32[]{:S(2)}, u32[]{:S(2)}) collective-permute-start(bf16[2,8,32,128]{3,2,1,0:T(8,128)(2,1)} %get-tuple-element.86), channel_id=1, source_target_pairs={{0,4},{1,5},{2,6},{3,7},{4,0},{5,1},{6,2},{7,3},{8,12},{9,13},{10,... | collective-permute-start | bytes 393224 | tf_op jit(solution)/shard_map/ppermute | solution.py:650
  122.5 17.2 %collective-permute-start.25 = (bf16[2,8,32,128]{3,2,1,0:T(8,128)(2,1)}, bf16[2,8,32,128]{3,2,1,0:T(8,128)(2,1)S(1)}, u32[]{:S(2)}, u32[]{:S(2)}) collective-permute-start(bf16[2,8,32,128]{3,2,1,0:T(8,128)(2,1)} %get-tuple-element.87), channel_id=1, source_target_pairs={{0,5},{1,6},{2,7},{3,0},{4,1},{5,2},{6,3},{7,4},{8,13},{9,14},{10,... | collective-permute-start | bytes 393224 | tf_op jit(solution)/shard_map/ppermute | solution.py:650
  147.2 14.5 %collective-permute-start.31 = (bf16[256,8,128]{2,1,0:T(8,128)(2,1)}, bf16[256,8,128]{2,1,0:T(8,128)(2,1)S(1)}, u32[]{:S(2)}, u32[]{:S(2)}) collective-permute-start(bf16[256,8,128]{2,1,0:T(8,128)(2,1)} %get-tuple-element.103), channel_id=1, source_target_pairs={{0,16},{8,24},{16,0},{24,8},{1,17},{9,25},{17,1},{25,9},{2,18},{10... | collective-permute-start | bytes 1572872 | tf_op jit(solution)/shard_map/ppermute | solution.py:654
  (44 other events, 343.6 us)

commit v6 on v5

--- a/solution.py
+++ b/solution.py
@@ -644,16 +644,16 @@
     frames_first = voltages.transpose(1, 0, 2)
 
     def over_chan(blocks):
-        moved = [blocks[0]]
-        for shift in range(1, chan_count):
+        moved = list(blocks)
+        for shift in farthest_first(chan_count):
             pairs = [(c, (c + shift) % chan_count) for c in range(chan_count)]
-            moved.append(lax.ppermute(blocks[shift], "chan", pairs))
+            moved[shift] = lax.ppermute(blocks[shift], "chan", pairs)
         return moved
 
     def to_mate(value, distance):
         return lax.ppermute(value, "grp", [(g, g ^ distance) for g in range(group_count)])
 
-    turned, near, across, relayed = [], [], [], []
+    turned, near, across = [], [], []
     channels = []
     chunks = spec_count // chan_count
     for chunk in range(chunks):
@@ -661,23 +661,21 @@
         blocks = over_chan(blocks)
         blocks = transform_by_shift(blocks, chan_id)
         channels.append(over_chan(blocks))
-    for chunk, channel in enumerate(channels):
-        if chunk:
-            channel, near, across, relayed = lax.optimization_barrier(
-                (channel, near, across, relayed)
-            )
+    for channel in channels:
         halves, for_near, for_across = turn(channel, group_id)
         turned.append(halves)
         near = near + [to_mate(for_near, 1)]
         across = across + [to_mate(for_across, 2)]
-        if chunk + 1 < chunks:
-            relayed = relayed + [to_mate(across[-1], 1)]
     left = left_operand(turned)
     result = correlate(left, near, group_id, plan, 1, spec_count, None)
     across, result = lax.optimization_barrier((across, result))
-    relayed = relayed + [to_mate(across[-1], 1)]
+    relayed = [to_mate(value, 1) for value in across]
     result = correlate(left, across, group_id, plan, 2, spec_count, result)
     return correlate(left, relayed, group_id, plan, 3, spec_count, result)
+
+
+def farthest_first(chan_count):
+    return sorted(range(1, chan_count), key=lambda shift: abs(shift - chan_count // 2))
 
 
 def overlaps(group_count, chan_count):

time: 176 us -> 156 us (0.89)
  waiting for transfers between devices: 34.6 us -> 19.9 us
  starting transfers between devices: 81.2 us -> 75.1 us
    ppermute x28, waiting for transfers between devices: 33.9 us -> 10.2 us  [over_chan(): moved[shift] = lax.ppermute(blocks[shift], 'chan', pairs)]
    ppermute x6, waiting for transfers between devices: 0.72 us -> 9.66 us  [to_mate(): lax.ppermute(value, 'grp', [(g, g ^ distance) for g in range(group_count)])]
    ppermute x28, starting transfers between devices: 78.5 us -> 72.4 us  [over_chan(): moved[shift] = lax.ppermute(blocks[shift], 'chan', pairs)]
  transfers between devices with their start and end apart: 34 -> 34, of which waited for: 12 -> 5; matrix products, arithmetic and copies ran while one was open for 0% -> 0% of each run, Pallas kernels for 17% -> 27%
where the time goes in v6:
time: 156 us; the launch traced here: 155 us
  starting transfers between devices  75.1 us (48%)
  Pallas kernels  54.2 us (35%)
  waiting for transfers between devices  19.9 us (13%)
  local copies, waits for them, and re-layouts  5.45 us (3%)
    ppermute x28, starting transfers between devices, over_chan(): moved[shift] = lax.ppermute(blocks[shift], 'chan', pairs)  72.4 us
    pallas_call x3, Pallas kernels, correlate(): pl.pallas_call(functools.partial(correlate_kernel, len(chunks), spec_coun...  17.9 us
    pallas_call x2, Pallas kernels, transform_by_shift(): pl.pallas_call(functools.partial(transform_by_shift_kernel, chan_count),...  12.1 us
    pallas_call x2, Pallas kernels, filter_by_shift(): pl.pallas_call(filter_by_shift_kernel, out_shape=[jax.ShapeDtypeStruct((s...  12 us
    ppermute x28, waiting for transfers between devices, over_chan(): moved[shift] = lax.ppermute(blocks[shift], 'chan', pairs)  10.2 us
    ppermute x6, waiting for transfers between devices, to_mate(): lax.ppermute(value, 'grp', [(g, g ^ distance) for g in range(group_count)])  9.66 us
    pallas_call x1, Pallas kernels, left_operand(): pl.pallas_call(left_kernel, out_shape=jax.ShapeDtypeStruct((halves, chann...  6.45 us
    pallas_call x2, Pallas kernels, turn(): pl.pallas_call(turn_kernel, out_shape=[jax.ShapeDtypeStruct((halves,) + o...  5.76 us
  transfers between devices with their start and end apart: 34, of which 5 were waited for; matrix products, arithmetic and copies ran while one was open for 0% of the time, Pallas kernels for 27%

profile of v6, /device:TPU:0, one launch (start us, length us, event | category | flops | bytes accessed | tf_op | source)
XLA Modules:
  0.0 155.0 jit_solution(10391363498069237498)
XLA Ops:
  0.0 6.0 %filter_by_shift.3 = (bf16[64,1024]{1,0:T(8,128)(2,1)}, bf16[64,1024]{1,0:T(8,128)(2,1)}, bf16[64,1024]{1,0:T(8,128)(2,1)}, bf16[64,1024]{1,0:T(8,128)(2,1)}, bf...) custom-call(s32[1]{0:T(128)} %bitcast.1.chan_ref.refs_0_, ...), custom_call_target="tpu_custom_call" | custom-call | tf_op jit(solution)/shard_map/filter_by_shift/pallas_call | solution.py:91
  6.0 3.1 %collective-permute-start.14 = (bf16[64,1024]{1,0:T(8,128)(2,1)}, bf16[64,1024]{1,0:T(8,128)(2,1)S(1)}, u32[]{:S(2)}, u32[]{:S(2)}) collective-permute-start(bf16[64,1024]{1,0:T(8,128)(2,1)} %get-tuple-element.64), channel_id=1, source_target_pairs={{0,1},{1,2},{2,3},{3,4},{4,5},{5,6},{6,7},{7,0},{8,9},{9,10},{10,1... | collective-permute-start | bytes 393224 | tf_op jit(solution)/shard_map/ppermute | solution.py:650
  10.7 2.5 %collective-permute-start.16 = (bf16[64,1024]{1,0:T(8,128)(2,1)}, bf16[64,1024]{1,0:T(8,128)(2,1)S(1)}, u32[]{:S(2)}, u32[]{:S(2)}) collective-permute-start(bf16[64,1024]{1,0:T(8,128)(2,1)} %get-tuple-element.66), channel_id=1, source_target_pairs={{0,3},{1,4},{2,5},{3,6},{4,7},{5,0},{6,1},{7,2},{8,11},{9,12},{10,... | collective-permute-start | bytes 393224 | tf_op jit(solution)/shard_map/ppermute | solution.py:650
  14.4 2.6 %collective-permute-start.18 = (bf16[64,1024]{1,0:T(8,128)(2,1)}, bf16[64,1024]{1,0:T(8,128)(2,1)S(1)}, u32[]{:S(2)}, u32[]{:S(2)}) collective-permute-start(bf16[64,1024]{1,0:T(8,128)(2,1)} %get-tuple-element.68), channel_id=1, source_target_pairs={{0,5},{1,6},{2,7},{3,0},{4,1},{5,2},{6,3},{7,4},{8,13},{9,14},{10,... | collective-permute-start | bytes 393224 | tf_op jit(solution)/shard_map/ppermute | solution.py:650
  17.1 6.0 %filter_by_shift.2 = (bf16[64,1024]{1,0:T(8,128)(2,1)}, bf16[64,1024]{1,0:T(8,128)(2,1)}, bf16[64,1024]{1,0:T(8,128)(2,1)}, bf16[64,1024]{1,0:T(8,128)(2,1)}, bf...) custom-call(s32[1]{0:T(128)} %bitcast.1.chan_ref.refs_0_, ...), custom_call_target="tpu_custom_call" | custom-call | tf_op jit(solution)/shard_map/filter_by_shift/pallas_call | solution.py:91
  27.5 5.8 %collective-permute-start.1 = (bf16[64,1024]{1,0:T(8,128)(2,1)}, bf16[64,1024]{1,0:T(8,128)(2,1)S(1)}, u32[]{:S(2)}, u32[]{:S(2)}) collective-permute-start(bf16[64,1024]{1,0:T(8,128)(2,1)} %get-tuple-element.48), channel_id=1, source_target_pairs={{0,2},{1,3},{2,4},{3,5},{4,6},{5,7},{6,0},{7,1},{8,10},{9,11},{10,... | collective-permute-start | bytes 393224 | tf_op jit(solution)/shard_map/ppermute | solution.py:650
  33.3 4.1 %collective-permute-start.2 = (bf16[64,1024]{1,0:T(8,128)(2,1)}, bf16[64,1024]{1,0:T(8,128)(2,1)S(1)}, u32[]{:S(2)}, u32[]{:S(2)}) collective-permute-start(bf16[64,1024]{1,0:T(8,128)(2,1)} %get-tuple-element.49), channel_id=1, source_target_pairs={{0,3},{1,4},{2,5},{3,6},{4,7},{5,0},{6,1},{7,2},{8,11},{9,12},{10,... | collective-permute-start | bytes 393224 | tf_op jit(solution)/shard_map/ppermute | solution.py:650
  37.4 2.8 %collective-permute-start.3 = (bf16[64,1024]{1,0:T(8,128)(2,1)}, bf16[64,1024]{1,0:T(8,128)(2,1)S(1)}, u32[]{:S(2)}, u32[]{:S(2)}) collective-permute-start(bf16[64,1024]{1,0:T(8,128)(2,1)} %get-tuple-element.50), channel_id=1, source_target_pairs={{0,4},{1,5},{2,6},{3,7},{4,0},{5,1},{6,2},{7,3},{8,12},{9,13},{10,... | collective-permute-start | bytes 393224 | tf_op jit(solution)/shard_map/ppermute | solution.py:650
  40.3 4.0 %collective-permute-start.4 = (bf16[64,1024]{1,0:T(8,128)(2,1)}, bf16[64,1024]{1,0:T(8,128)(2,1)S(1)}, u32[]{:S(2)}, u32[]{:S(2)}) collective-permute-start(bf16[64,1024]{1,0:T(8,128)(2,1)} %get-tuple-element.51), channel_id=1, source_target_pairs={{0,5},{1,6},{2,7},{3,0},{4,1},{5,2},{6,3},{7,4},{8,13},{9,14},{10,... | collective-permute-start | bytes 393224 | tf_op jit(solution)/shard_map/ppermute | solution.py:650
  44.3 3.3 %collective-permute-start.5 = (bf16[64,1024]{1,0:T(8,128)(2,1)}, bf16[64,1024]{1,0:T(8,128)(2,1)S(1)}, u32[]{:S(2)}, u32[]{:S(2)}) collective-permute-start(bf16[64,1024]{1,0:T(8,128)(2,1)} %get-tuple-element.52), channel_id=1, source_target_pairs={{0,6},{1,7},{2,0},{3,1},{4,2},{5,3},{6,4},{7,5},{8,14},{9,15},{10,... | collective-permute-start | bytes 393224 | tf_op jit(solution)/shard_map/ppermute | solution.py:650
  47.8 6.1 %transform_by_shift.3 = (bf16[2,8,32,128]{3,2,1,0:T(8,128)(2,1)}, bf16[2,8,32,128]{3,2,1,0:T(8,128)(2,1)}, bf16[2,8,32,128]{3,2,1,0:T(8,128)(2,1)}, bf16[2,8,32,...) custom-call(s32[1]{0:T(128)} %bitcast.1.chan_ref.refs_0_, ...), custom_call_target="tpu_custom_call" | custom-call | tf_op jit(solution)/shard_map/transform_by_shift/pallas_call | solution.py:374
  57.2 6.0 %transform_by_shift.2 = (bf16[2,8,32,128]{3,2,1,0:T(8,128)(2,1)}, bf16[2,8,32,128]{3,2,1,0:T(8,128)(2,1)}, bf16[2,8,32,128]{3,2,1,0:T(8,128)(2,1)}, bf16[2,8,32,...) custom-call(s32[1]{0:T(128)} %bitcast.1.chan_ref.refs_0_, ...), custom_call_target="tpu_custom_call" | custom-call | tf_op jit(solution)/shard_map/transform_by_shift/pallas_call | solution.py:374
  64.7 2.9 %collective-permute-start.8 = (bf16[2,8,32,128]{3,2,1,0:T(8,128)(2,1)}, bf16[2,8,32,128]{3,2,1,0:T(8,128)(2,1)S(1)}, u32[]{:S(2)}, u32[]{:S(2)}) collective-permute-start(bf16[2,8,32,128]{3,2,1,0:T(8,128)(2,1)} %get-tuple-element.56), channel_id=1, source_target_pairs={{0,2},{1,3},{2,4},{3,5},{4,6},{5,7},{6,0},{7,1},{8,10},{9,11},{10,... | collective-permute-start | bytes 393224 | tf_op jit(solution)/shard_map/ppermute | solution.py:650
  70.5 2.1 %collective-permute-start.11 = (bf16[2,8,32,128]{3,2,1,0:T(8,128)(2,1)}, bf16[2,8,32,128]{3,2,1,0:T(8,128)(2,1)S(1)}, u32[]{:S(2)}, u32[]{:S(2)}) collective-permute-start(bf16[2,8,32,128]{3,2,1,0:T(8,128)(2,1)} %get-tuple-element.59), channel_id=1, source_target_pairs={{0,5},{1,6},{2,7},{3,0},{4,1},{5,2},{6,3},{7,4},{8,13},{9,14},{10,... | collective-permute-start | bytes 393224 | tf_op jit(solution)/shard_map/ppermute | solution.py:650
  75.3 7.1 %collective-permute-done.9.refs_3_ = bf16[2,8,32,128]{3,2,1,0:T(8,128)(2,1)S(1)} collective-permute-done((bf16[2,8,32,128]{3,2,1,0:T(8,128)(2,1)}, bf16[2,8,32,128]{3,2,1,0:T(8,128)(2,1)S(1)}, u32[]{:S(2)}, u32[]{:S(2)}) %collective-permute-start.9) | collective-permute-done | bytes 131104 | tf_op jit(solution)/shard_map/ppermute | solution.py:650
  82.4 8.3 %collective-permute-start.23 = (bf16[2,8,32,128]{3,2,1,0:T(8,128)(2,1)}, bf16[2,8,32,128]{3,2,1,0:T(8,128)(2,1)S(1)}, u32[]{:S(2)}, u32[]{:S(2)}) collective-permute-start(bf16[2,8,32,128]{3,2,1,0:T(8,128)(2,1)} %get-tuple-element.74), channel_id=1, source_target_pairs={{0,3},{1,4},{2,5},{3,6},{4,7},{5,0},{6,1},{7,2},{8,11},{9,12},{10,... | collective-permute-start | bytes 393224 | tf_op jit(solution)/shard_map/ppermute | solution.py:650
  92.0 14.2 %collective-permute-start.26 = (bf16[2,8,32,128]{3,2,1,0:T(8,128)(2,1)}, bf16[2,8,32,128]{3,2,1,0:T(8,128)(2,1)S(1)}, u32[]{:S(2)}, u32[]{:S(2)}) collective-permute-start(bf16[2,8,32,128]{3,2,1,0:T(8,128)(2,1)} %get-tuple-element.77), channel_id=1, source_target_pairs={{0,6},{1,7},{2,0},{3,1},{4,2},{5,3},{6,4},{7,5},{8,14},{9,15},{10,... | collective-permute-start | bytes 393224 | tf_op jit(solution)/shard_map/ppermute | solution.py:650
  106.8 2.9 %turn.2 = (bf16[2,256,8,128]{3,2,1,0:T(8,128)(2,1)}, bf16[256,8,128]{2,1,0:T(8,128)(2,1)}, bf16[256,8,128]{2,1,0:T(8,128)(2,1)}) custom-call(s32[1]{0:T(128)} %bitcast.group_ref, bf16[2,8,32,128]{3,2,1,0:T(8,128)(2,1)} %get-tuple-element.54.refs_0_, bf16[2,8,32,128]{3,2,1,0:T(8,128)(2,1)} %copy-done.22, bf16[2,8,32,128]{3,2,1,0:T(8,128)(2,1)} %copy-done.23, ...), custom_call_target="tpu_custom_call" | custom-call | tf_op jit(solution)/shard_map/turn/pallas_call | solution.py:433
  112.0 2.9 %turn.3 = (bf16[2,256,8,128]{3,2,1,0:T(8,128)(2,1)}, bf16[256,8,128]{2,1,0:T(8,128)(2,1)}, bf16[256,8,128]{2,1,0:T(8,128)(2,1)}) custom-call(s32[1]{0:T(128)} %bitcast.group_ref, bf16[2,8,32,128]{3,2,1,0:T(8,128)(2,1)} %get-tuple-element.71.refs_0_, bf16[2,8,32,128]{3,2,1,0:T(8,128)(2,1)} %copy-done.20, bf16[2,8,32,128]{3,2,1,0:T(8,128)(2,1)} %copy-done.21, ...), custom_call_target="tpu_custom_call" | custom-call | tf_op jit(solution)/shard_map/turn/pallas_call | solution.py:433
  117.0 6.5 %left_operand.1.left_ref = bf16[2,128,64,64]{3,2,1,0:T(8,128)(2,1)} custom-call(bf16[2,256,8,128]{3,2,1,0:T(8,128)(2,1)} %get-tuple-element.62.refs_0_, bf16[2,256,8,128]{3,2,1,0:T(8,128)(2,1)} %get-tuple-element.79.refs_1_), custom_call_target="tpu_custom_call" | custom-call | tf_op jit(solution)/shard_map/left_operand/pallas_call | solution.py:478
  125.1 6.0 %correlate.3.refs_2_ = bf16[3,64,256,128]{3,2,1,0:T(8,128)(2,1)} custom-call(s32[1]{0:T(128)} %bitcast.group_ref, s32[3,4]{1,0:T(4,128)} %plan_ref.5, bf16[2,128,64,64]{3,2,1,0:T(8,128)(2,1)} %left_operand.1.left_ref, bf16[256,8,128]{2,1,0:T(8,128)(2,1)} %copy-done.4, bf16[256,8,128]{2,1,0:T(8,128)(2,1)} %copy-done.5), custom_call_target="tpu_custom_call" | custom-call | flops 268435456 | bytes 16777216 | tf_op jit(solution)/shard_map/correlate/pallas_call | solution.py:560
  131.1 9.6 %collective-permute-done.29.refs_1_ = bf16[256,8,128]{2,1,0:T(8,128)(2,1)S(1)} collective-permute-done((bf16[256,8,128]{2,1,0:T(8,128)(2,1)}, bf16[256,8,128]{2,1,0:T(8,128)(2,1)S(1)}, u32[]{:S(2)}, u32[]{:S(2)}) %collective-permute-start.29) | collective-permute-done | bytes 524320 | tf_op jit(solution)/shard_map/ppermute | solution.py:654
  141.5 6.0 %correlate.4.refs_2_ = bf16[3,64,256,128]{3,2,1,0:T(8,128)(2,1)} custom-call(s32[1]{0:T(128)} %bitcast.group_ref, s32[3,4]{1,0:T(4,128)} %plan_ref.5, bf16[2,128,64,64]{3,2,1,0:T(8,128)(2,1)} %left_operand.1.left_ref, bf16[256,8,128]{2,1,0:T(8,128)(2,1)} %copy-done, bf16[256,8,128]{2,1,0:T(8,128)(2,1)} %copy-done.1, ...), custom_call_target="tpu_custom_call", output_to_operand_aliasing={{}: (5, {})} | custom-call | flops 268435456 | bytes 16777216 | tf_op jit(solution)/shard_map/correlate/pallas_call | solution.py:560
  149.0 6.0 %correlate.5 = bf16[3,64,256,128]{3,2,1,0:T(8,128)(2,1)} custom-call(s32[1]{0:T(128)} %bitcast.group_ref, s32[3,4]{1,0:T(4,128)} %plan_ref.5, bf16[2,128,64,64]{3,2,1,0:T(8,128)(2,1)} %left_operand.1.left_ref, bf16[256,8,128]{2,1,0:T(8,128)(2,1)} %copy-done.2, bf16[256,8,128]{2,1,0:T(8,128)(2,1)} %copy-done.3, ...), custom_call_target="tpu_custom_call", output_to_operand_aliasing={{}: (5, {})} | custom-call | flops 268435456 | bytes 16777216 | tf_op jit(solution)/shard_map/correlate/pallas_call | solution.py:560
  (122 shorter events, 27.9 us)
Async XLA Ops:
  6.0 17.1 %collective-permute-start.14 = (bf16[64,1024]{1,0:T(8,128)(2,1)}, bf16[64,1024]{1,0:T(8,128)(2,1)S(1)}, u32[]{:S(2)}, u32[]{:S(2)}) collective-permute-start(bf16[64,1024]{1,0:T(8,128)(2,1)} %get-tuple-element.64), channel_id=1, source_target_pairs={{0,1},{1,2},{2,3},{3,4},{4,5},{5,6},{6,7},{7,0},{8,9},{9,10},{10,1... | collective-permute-start | bytes 393224 | tf_op jit(solution)/shard_map/ppermute | solution.py:650
  9.1 15.4 %collective-permute-start.15 = (bf16[64,1024]{1,0:T(8,128)(2,1)}, bf16[64,1024]{1,0:T(8,128)(2,1)S(1)}, u32[]{:S(2)}, u32[]{:S(2)}) collective-permute-start(bf16[64,1024]{1,0:T(8,128)(2,1)} %get-tuple-element.65), channel_id=1, source_target_pairs={{0,2},{1,3},{2,4},{3,5},{4,6},{5,7},{6,0},{7,1},{8,10},{9,11},{10,... | collective-permute-start | bytes 393224 | tf_op jit(solution)/shard_map/ppermute | solution.py:650
  10.7 16.6 %collective-permute-start.16 = (bf16[64,1024]{1,0:T(8,128)(2,1)}, bf16[64,1024]{1,0:T(8,128)(2,1)S(1)}, u32[]{:S(2)}, u32[]{:S(2)}) collective-permute-start(bf16[64,1024]{1,0:T(8,128)(2,1)} %get-tuple-element.66), channel_id=1, source_target_pairs={{0,3},{1,4},{2,5},{3,6},{4,7},{5,0},{6,1},{7,2},{8,11},{9,12},{10,... | collective-permute-start | bytes 393224 | tf_op jit(solution)/shard_map/ppermute | solution.py:650
  13.2 14.3 %collective-permute-start.17 = (bf16[64,1024]{1,0:T(8,128)(2,1)}, bf16[64,1024]{1,0:T(8,128)(2,1)S(1)}, u32[]{:S(2)}, u32[]{:S(2)}) collective-permute-start(bf16[64,1024]{1,0:T(8,128)(2,1)} %get-tuple-element.67), channel_id=1, source_target_pairs={{0,4},{1,5},{2,6},{3,7},{4,0},{5,1},{6,2},{7,3},{8,12},{9,13},{10,... | collective-permute-start | bytes 393224 | tf_op jit(solution)/shard_map/ppermute | solution.py:650
  14.4 18.9 %collective-permute-start.18 = (bf16[64,1024]{1,0:T(8,128)(2,1)}, bf16[64,1024]{1,0:T(8,128)(2,1)S(1)}, u32[]{:S(2)}, u32[]{:S(2)}) collective-permute-start(bf16[64,1024]{1,0:T(8,128)(2,1)} %get-tuple-element.68), channel_id=1, source_target_pairs={{0,5},{1,6},{2,7},{3,0},{4,1},{5,2},{6,3},{7,4},{8,13},{9,14},{10,... | collective-permute-start | bytes 393224 | tf_op jit(solution)/shard_map/ppermute | solution.py:650
  24.5 15.8 %collective-permute-start.20 = (bf16[64,1024]{1,0:T(8,128)(2,1)}, bf16[64,1024]{1,0:T(8,128)(2,1)S(1)}, u32[]{:S(2)}, u32[]{:S(2)}) collective-permute-start(bf16[64,1024]{1,0:T(8,128)(2,1)} %get-tuple-element.70), channel_id=1, source_target_pairs={{0,7},{1,0},{2,1},{3,2},{4,3},{5,4},{6,5},{7,6},{8,15},{9,8},{10,9... | collective-permute-start | bytes 393224 | tf_op jit(solution)/shard_map/ppermute | solution.py:650
  27.3 17.0 %collective-permute-start = (bf16[64,1024]{1,0:T(8,128)(2,1)}, bf16[64,1024]{1,0:T(8,128)(2,1)S(1)}, u32[]{:S(2)}, u32[]{:S(2)}) collective-permute-start(bf16[64,1024]{1,0:T(8,128)(2,1)} %get-tuple-element.47), channel_id=1, source_target_pairs={{0,1},{1,2},{2,3},{3,4},{4,5},{5,6},{6,7},{7,0},{8,9},{9,10},{10,1... | collective-permute-start | bytes 393224 | tf_op jit(solution)/shard_map/ppermute | solution.py:650
  27.5 20.1 %collective-permute-start.1 = (bf16[64,1024]{1,0:T(8,128)(2,1)}, bf16[64,1024]{1,0:T(8,128)(2,1)S(1)}, u32[]{:S(2)}, u32[]{:S(2)}) collective-permute-start(bf16[64,1024]{1,0:T(8,128)(2,1)} %get-tuple-element.48), channel_id=1, source_target_pairs={{0,2},{1,3},{2,4},{3,5},{4,6},{5,7},{6,0},{7,1},{8,10},{9,11},{10,... | collective-permute-start | bytes 393224 | tf_op jit(solution)/shard_map/ppermute | solution.py:650
  33.3 20.6 %collective-permute-start.2 = (bf16[64,1024]{1,0:T(8,128)(2,1)}, bf16[64,1024]{1,0:T(8,128)(2,1)S(1)}, u32[]{:S(2)}, u32[]{:S(2)}) collective-permute-start(bf16[64,1024]{1,0:T(8,128)(2,1)} %get-tuple-element.49), channel_id=1, source_target_pairs={{0,3},{1,4},{2,5},{3,6},{4,7},{5,0},{6,1},{7,2},{8,11},{9,12},{10,... | collective-permute-start | bytes 393224 | tf_op jit(solution)/shard_map/ppermute | solution.py:650
  37.4 18.4 %collective-permute-start.3 = (bf16[64,1024]{1,0:T(8,128)(2,1)}, bf16[64,1024]{1,0:T(8,128)(2,1)S(1)}, u32[]{:S(2)}, u32[]{:S(2)}) collective-permute-start(bf16[64,1024]{1,0:T(8,128)(2,1)} %get-tuple-element.50), channel_id=1, source_target_pairs={{0,4},{1,5},{2,6},{3,7},{4,0},{5,1},{6,2},{7,3},{8,12},{9,13},{10,... | collective-permute-start | bytes 393224 | tf_op jit(solution)/shard_map/ppermute | solution.py:650
  40.3 16.2 %collective-permute-start.4 = (bf16[64,1024]{1,0:T(8,128)(2,1)}, bf16[64,1024]{1,0:T(8,128)(2,1)S(1)}, u32[]{:S(2)}, u32[]{:S(2)}) collective-permute-start(bf16[64,1024]{1,0:T(8,128)(2,1)} %get-tuple-element.51), channel_id=1, source_target_pairs={{0,5},{1,6},{2,7},{3,0},{4,1},{5,2},{6,3},{7,4},{8,13},{9,14},{10,... | collective-permute-start | bytes 393224 | tf_op jit(solution)/shard_map/ppermute | solution.py:650
  53.9 14.7 %collective-permute-start.21 = (bf16[2,8,32,128]{3,2,1,0:T(8,128)(2,1)}, bf16[2,8,32,128]{3,2,1,0:T(8,128)(2,1)S(1)}, u32[]{:S(2)}, u32[]{:S(2)}) collective-permute-start(bf16[2,8,32,128]{3,2,1,0:T(8,128)(2,1)} %get-tuple-element.72), channel_id=1, source_target_pairs={{0,1},{1,2},{2,3},{3,4},{4,5},{5,6},{6,7},{7,0},{8,9},{9,10},{10,1... | collective-permute-start | bytes 393224 | tf_op jit(solution)/shard_map/ppermute | solution.py:650
  55.9 14.6 %collective-permute-start.22 = (bf16[2,8,32,128]{3,2,1,0:T(8,128)(2,1)}, bf16[2,8,32,128]{3,2,1,0:T(8,128)(2,1)S(1)}, u32[]{:S(2)}, u32[]{:S(2)}) collective-permute-start(bf16[2,8,32,128]{3,2,1,0:T(8,128)(2,1)} %get-tuple-element.73), channel_id=1, source_target_pairs={{0,2},{1,3},{2,4},{3,5},{4,6},{5,7},{6,0},{7,1},{8,10},{9,11},{10,... | collective-permute-start | bytes 393224 | tf_op jit(solution)/shard_map/ppermute | solution.py:650
  67.5 14.8 %collective-permute-start.9 = (bf16[2,8,32,128]{3,2,1,0:T(8,128)(2,1)}, bf16[2,8,32,128]{3,2,1,0:T(8,128)(2,1)S(1)}, u32[]{:S(2)}, u32[]{:S(2)}) collective-permute-start(bf16[2,8,32,128]{3,2,1,0:T(8,128)(2,1)} %get-tuple-element.57), channel_id=1, source_target_pairs={{0,3},{1,4},{2,5},{3,6},{4,7},{5,0},{6,1},{7,2},{8,11},{9,12},{10,... | collective-permute-start | bytes 393224 | tf_op jit(solution)/shard_map/ppermute | solution.py:650
  68.5 22.1 %collective-permute-start.10 = (bf16[2,8,32,128]{3,2,1,0:T(8,128)(2,1)}, bf16[2,8,32,128]{3,2,1,0:T(8,128)(2,1)S(1)}, u32[]{:S(2)}, u32[]{:S(2)}) collective-permute-start(bf16[2,8,32,128]{3,2,1,0:T(8,128)(2,1)} %get-tuple-element.58), channel_id=1, source_target_pairs={{0,4},{1,5},{2,6},{3,7},{4,0},{5,1},{6,2},{7,3},{8,12},{9,13},{10,... | collective-permute-start | bytes 393224 | tf_op jit(solution)/shard_map/ppermute | solution.py:650
  70.5 20.2 %collective-permute-start.11 = (bf16[2,8,32,128]{3,2,1,0:T(8,128)(2,1)}, bf16[2,8,32,128]{3,2,1,0:T(8,128)(2,1)S(1)}, u32[]{:S(2)}, u32[]{:S(2)}) collective-permute-start(bf16[2,8,32,128]{3,2,1,0:T(8,128)(2,1)} %get-tuple-element.59), channel_id=1, source_target_pairs={{0,5},{1,6},{2,7},{3,0},{4,1},{5,2},{6,3},{7,4},{8,13},{9,14},{10,... | collective-permute-start | bytes 393224 | tf_op jit(solution)/shard_map/ppermute | solution.py:650
  72.7 19.3 %collective-permute-start.12 = (bf16[2,8,32,128]{3,2,1,0:T(8,128)(2,1)}, bf16[2,8,32,128]{3,2,1,0:T(8,128)(2,1)S(1)}, u32[]{:S(2)}, u32[]{:S(2)}) collective-permute-start(bf16[2,8,32,128]{3,2,1,0:T(8,128)(2,1)} %get-tuple-element.60), channel_id=1, source_target_pairs={{0,6},{1,7},{2,0},{3,1},{4,2},{5,3},{6,4},{7,5},{8,14},{9,15},{10,... | collective-permute-start | bytes 393224 | tf_op jit(solution)/shard_map/ppermute | solution.py:650
  74.3 31.9 %collective-permute-start.13 = (bf16[2,8,32,128]{3,2,1,0:T(8,128)(2,1)}, bf16[2,8,32,128]{3,2,1,0:T(8,128)(2,1)S(1)}, u32[]{:S(2)}, u32[]{:S(2)}) collective-permute-start(bf16[2,8,32,128]{3,2,1,0:T(8,128)(2,1)} %get-tuple-element.61), channel_id=1, source_target_pairs={{0,7},{1,0},{2,1},{3,2},{4,3},{5,4},{6,5},{7,6},{8,15},{9,8},{10,9... | collective-permute-start | bytes 393224 | tf_op jit(solution)/shard_map/ppermute | solution.py:650
  82.4 27.3 %collective-permute-start.23 = (bf16[2,8,32,128]{3,2,1,0:T(8,128)(2,1)}, bf16[2,8,32,128]{3,2,1,0:T(8,128)(2,1)S(1)}, u32[]{:S(2)}, u32[]{:S(2)}) collective-permute-start(bf16[2,8,32,128]{3,2,1,0:T(8,128)(2,1)} %get-tuple-element.74), channel_id=1, source_target_pairs={{0,3},{1,4},{2,5},{3,6},{4,7},{5,0},{6,1},{7,2},{8,11},{9,12},{10,... | collective-permute-start | bytes 393224 | tf_op jit(solution)/shard_map/ppermute | solution.py:650
  90.7 19.1 %collective-permute-start.24 = (bf16[2,8,32,128]{3,2,1,0:T(8,128)(2,1)}, bf16[2,8,32,128]{3,2,1,0:T(8,128)(2,1)S(1)}, u32[]{:S(2)}, u32[]{:S(2)}) collective-permute-start(bf16[2,8,32,128]{3,2,1,0:T(8,128)(2,1)} %get-tuple-element.75), channel_id=1, source_target_pairs={{0,4},{1,5},{2,6},{3,7},{4,0},{5,1},{6,2},{7,3},{8,12},{9,13},{10,... | collective-permute-start | bytes 393224 | tf_op jit(solution)/shard_map/ppermute | solution.py:650
  90.7 19.1 %collective-permute-start.25 = (bf16[2,8,32,128]{3,2,1,0:T(8,128)(2,1)}, bf16[2,8,32,128]{3,2,1,0:T(8,128)(2,1)S(1)}, u32[]{:S(2)}, u32[]{:S(2)}) collective-permute-start(bf16[2,8,32,128]{3,2,1,0:T(8,128)(2,1)} %get-tuple-element.76), channel_id=1, source_target_pairs={{0,5},{1,6},{2,7},{3,0},{4,1},{5,2},{6,3},{7,4},{8,13},{9,14},{10,... | collective-permute-start | bytes 393224 | tf_op jit(solution)/shard_map/ppermute | solution.py:650
  92.0 17.9 %collective-permute-start.26 = (bf16[2,8,32,128]{3,2,1,0:T(8,128)(2,1)}, bf16[2,8,32,128]{3,2,1,0:T(8,128)(2,1)S(1)}, u32[]{:S(2)}, u32[]{:S(2)}) collective-permute-start(bf16[2,8,32,128]{3,2,1,0:T(8,128)(2,1)} %get-tuple-element.77), channel_id=1, source_target_pairs={{0,6},{1,7},{2,0},{3,1},{4,2},{5,3},{6,4},{7,5},{8,14},{9,15},{10,... | collective-permute-start | bytes 393224 | tf_op jit(solution)/shard_map/ppermute | solution.py:650
  114.9 16.1 %collective-permute-start.28 = (bf16[256,8,128]{2,1,0:T(8,128)(2,1)}, bf16[256,8,128]{2,1,0:T(8,128)(2,1)S(1)}, u32[]{:S(2)}, u32[]{:S(2)}) collective-permute-start(bf16[256,8,128]{2,1,0:T(8,128)(2,1)} %get-tuple-element.80), channel_id=1, source_target_pairs={{0,16},{8,24},{16,0},{24,8},{1,17},{9,25},{17,1},{25,9},{2,18},{10... | collective-permute-start | bytes 1572872 | tf_op jit(solution)/shard_map/ppermute | solution.py:654
  116.5 24.2 %collective-permute-start.29 = (bf16[256,8,128]{2,1,0:T(8,128)(2,1)}, bf16[256,8,128]{2,1,0:T(8,128)(2,1)S(1)}, u32[]{:S(2)}, u32[]{:S(2)}) collective-permute-start(bf16[256,8,128]{2,1,0:T(8,128)(2,1)} %get-tuple-element.81), channel_id=1, source_target_pairs={{0,16},{8,24},{16,0},{24,8},{1,17},{9,25},{17,1},{25,9},{2,18},{10... | collective-permute-start | bytes 1572872 | tf_op jit(solution)/shard_map/ppermute | solution.py:654
  (44 other events, 482.5 us)

commit v7 on v6

--- a/solution.py
+++ b/solution.py
@@ -13,7 +13,8 @@
 TAPS = 16
 LANES = 128
 RADIX = 64
-VMEM_LIMIT = 60 * 1024 * 1024
+EIGHT = 8
+VMEM_LIMIT = 67_000_000
 
 
 def tap_table(fft_len):
@@ -31,18 +32,20 @@
     def one_tile(tile, carry):
         cols = pl.ds(pl.multiple_of(tile * LANES, LANES), LANES)
         coeff = [
-            jnp.broadcast_to(coeff_ref[0, t : t + 1, cols], (sig_tile, LANES)) for t in range(TAPS)
+            jnp.broadcast_to(coeff_ref[0, t : t + 1, cols], (EIGHT, LANES)) for t in range(TAPS)
         ]
-        total = [None] * spec_count
-        for frame in range(frames):
-            sample = volt_ref[frame, :, cols].astype(jnp.float32)
-            for s in range(max(0, frame - TAPS + 1), min(spec_count - 1, frame) + 1):
-                term = coeff[frame - s] * sample
-                total[s] = term if total[s] is None else total[s] + term
-            if frame >= TAPS - 1:
-                s = frame - TAPS + 1
-                out_ref[s, :, cols] = total[s].astype(jnp.bfloat16)
-                total[s] = None
+        for low in range(0, sig_tile, EIGHT):
+            rows = slice(low, low + EIGHT)
+            total = [None] * spec_count
+            for frame in range(frames):
+                sample = volt_ref[frame, rows, cols].astype(jnp.float32)
+                for s in range(max(0, frame - TAPS + 1), min(spec_count - 1, frame) + 1):
+                    term = coeff[frame - s] * sample
+                    total[s] = term if total[s] is None else total[s] + term
+                if frame >= TAPS - 1:
+                    s = frame - TAPS + 1
+                    out_ref[s, rows, cols] = total[s].astype(jnp.bfloat16)
+                    total[s] = None
         return carry
 
     lax.fori_loop(0, block_len // LANES, one_tile, 0)
@@ -53,7 +56,7 @@
     frames = spec_count + TAPS - 1
     table = tap_table(block_len * chan_count).astype(np.float32)
     table = np.ascontiguousarray(table.reshape(TAPS, chan_count, block_len).transpose(1, 0, 2))
-    sig_tile = 16
+    sig_tile = 32
     return pl.pallas_call(
         filter_kernel,
         out_shape=jax.ShapeDtypeStruct((spec_count, sig_count, block_len), jnp.bfloat16),
@@ -74,38 +77,42 @@
     )(chan_id, frames_first, jnp.asarray(table))
 
 
-def filter_by_shift_kernel(chan_ref, volt_ref, coeff_ref, *refs):
+def filter_by_pair_kernel(pairs, chan_ref, volt_ref, coeff_ref, *refs):
     out_refs, block_ref = refs[:-1], refs[-1]
     filter_kernel(chan_ref, volt_ref, coeff_ref, block_ref)
-    count = len(out_refs)
-    for shift, out_ref in enumerate(out_refs):
-        out_ref[...] = block_ref[lax.rem(chan_ref[0] + shift, count)]
-
-
-def filter_by_shift(frames_first, chan_id, chan_count, first):
+    for pair, out_ref in zip(pairs, out_refs):
+        out_ref[...] = block_ref[(chan_ref[0] ^ pair) % len(pairs)]
+
+
+def filter_by_pair(frames_first, chan_id, chan_count, first, pairs):
     _, sig_count, block_len = frames_first.shape
-    frames = chan_count + TAPS - 1
+    count = len(pairs)
+    frames = count + TAPS - 1
     table = tap_table(block_len * chan_count).astype(np.float32)
     table = np.ascontiguousarray(table.reshape(TAPS, chan_count, block_len).transpose(1, 0, 2))
-    sig_tile = 16
+    sig_tile = 32
+
+    def frames_at(i, chan):
+        lowest = (chan[0] ^ pairs[0]) // count * count
+        return first + lowest, i * sig_tile, 0
+
     return pl.pallas_call(
-        filter_by_shift_kernel,
-        out_shape=[jax.ShapeDtypeStruct((sig_count, block_len), jnp.bfloat16)] * chan_count,
+        functools.partial(filter_by_pair_kernel, pairs),
+        out_shape=[jax.ShapeDtypeStruct((sig_count, block_len), jnp.bfloat16)] * count,
         grid_spec=pltpu.PrefetchScalarGridSpec(
             num_scalar_prefetch=1,
             grid=(sig_count // sig_tile,),
             in_specs=[
                 pl.BlockSpec(
-                    (pl.Element(frames), pl.Element(sig_tile), pl.Element(block_len)),
-                    lambda i, c: (first, i * sig_tile, 0),
+                    (pl.Element(frames), pl.Element(sig_tile), pl.Element(block_len)), frames_at
                 ),
                 pl.BlockSpec((1, TAPS, block_len), lambda i, c: (c[0], 0, 0)),
             ],
-            out_specs=[pl.BlockSpec((sig_tile, block_len), lambda i, c: (i, 0))] * chan_count,
-            scratch_shapes=[pltpu.VMEM((chan_count, sig_tile, block_len), jnp.bfloat16)],
+            out_specs=[pl.BlockSpec((sig_tile, block_len), lambda i, c: (i, 0))] * count,
+            scratch_shapes=[pltpu.VMEM((count, sig_tile, block_len), jnp.bfloat16)],
         ),
         compiler_params=pltpu.CompilerParams(vmem_limit_bytes=VMEM_LIMIT),
-        name="filter_by_shift",
+        name="filter_by_pair",
     )(chan_id, frames_first, jnp.asarray(table))
 
 
@@ -341,15 +348,15 @@
     )(samples, *transform_tables(chan_count * block_len))
 
 
-def transform_by_shift_kernel(chan_count, *refs):
+def transform_by_pair_kernel(chan_count, *refs):
     chan_ref, tables = refs[0], refs[1:5]
     in_refs, out_refs = refs[5 : 5 + chan_count], refs[5 + chan_count : 5 + 2 * chan_count]
     block_ref, result_ref, mid_ref, high_ref, low_ref, in_sem, out_sem = refs[5 + 2 * chan_count :]
     chan = chan_ref[0]
     fetches = []
-    for shift, in_ref in enumerate(in_refs):
-        source = lax.rem(chan + chan_count - shift, chan_count)
-        fetches.append(pltpu.make_async_copy(in_ref, block_ref.at[source], in_sem.at[shift]))
+    for pair, in_ref in enumerate(in_refs):
+        source = chan ^ pair
+        fetches.append(pltpu.make_async_copy(in_ref, block_ref.at[source], in_sem.at[pair]))
         fetches[-1].start()
     for fetch in fetches:
         fetch.wait()
@@ -357,22 +364,22 @@
         chan_count, True, block_ref, *tables, result_ref, mid_ref, high_ref, low_ref
     )
     sends = []
-    for shift, out_ref in enumerate(out_refs):
-        target = lax.rem(chan + shift, chan_count)
-        sends.append(pltpu.make_async_copy(result_ref.at[target], out_ref, out_sem.at[shift]))
+    for pair, out_ref in enumerate(out_refs):
+        target = chan ^ pair
+        sends.append(pltpu.make_async_copy(result_ref.at[target], out_ref, out_sem.at[pair]))
         sends[-1].start()
     for send in sends:
         send.wait()
 
 
-def transform_by_shift(blocks, chan_id):
+def transform_by_pair(blocks, chan_id):
     chan_count = len(blocks)
     rows, block_len = blocks[0].shape
     whole = pl.BlockSpec(memory_space=pltpu.VMEM)
     apart = pl.BlockSpec(memory_space=pltpu.HBM)
     shape = (2, RADIX // chan_count, LANES // 4, 2 * rows)
     return pl.pallas_call(
-        functools.partial(transform_by_shift_kernel, chan_count),
+        functools.partial(transform_by_pair_kernel, chan_count),
         out_shape=[jax.ShapeDtypeStruct(shape, jnp.bfloat16)] * chan_count,
         in_specs=[pl.BlockSpec(memory_space=pltpu.SMEM)] + [whole] * 4 + [apart] * chan_count,
         out_specs=[apart] * chan_count,
@@ -383,11 +390,8 @@
         + transform_scratch(rows)
         + [pltpu.SemaphoreType.DMA((chan_count,)), pltpu.SemaphoreType.DMA((chan_count,))],
         compiler_params=pltpu.CompilerParams(vmem_limit_bytes=VMEM_LIMIT),
-        name="transform_by_shift",
+        name="transform_by_pair",
     )(chan_id, *transform_tables(chan_count * block_len), *blocks)
-
-
-EIGHT = 8
 
 
 def turn_kernel(group_ref, *refs):
@@ -458,30 +462,43 @@
     chunk_refs, out_ref = refs[:-1], refs[-1]
     _, channels, _, lanes = chunk_refs[0].shape
     sig_count = lanes // 2
-
-    def pair(step, carry):
+    together = 2 * lanes // out_ref.shape[3]
+    width = out_ref.shape[3]
+    count = channels // out_ref.shape[1]
+    row = lax.broadcasted_iota(jnp.int32, (sig_count, lanes), 0)
+    column = lax.broadcasted_iota(jnp.int32, (sig_count, lanes), 1)
+    identity = (row == column).astype(jnp.bfloat16)
+
+    def some_pairs(step, carry):
         rows = []
-        for i in range(2):
-            values = [ref[0, 2 * step + i].astype(jnp.float32) for ref in chunk_refs]
+        for i in range(count * together):
+            values = [ref[0, count * together * step + i].astype(jnp.float32) for ref in chunk_refs]
             rows += values + [pltpu.roll(value, sig_count, 1) for value in values]
-        stacked = jnp.concatenate(rows, axis=0)
-        out_ref[0, step] = stacked.T[:sig_count].astype(jnp.bfloat16)
+        stacked = jnp.concatenate(rows, axis=0).astype(jnp.bfloat16)
+        turned = lax.dot_general(
+            identity, stacked, (((1,), (1,)), ((), ())), preferred_element_type=jnp.float32
+        )
+        for i in range(together):
+            out_ref[0, together * step + i] = turned[:, i * width : (i + 1) * width].astype(
+                jnp.bfloat16
+            )
         return carry
 
-    lax.fori_loop(0, channels // 2, pair, 0, unroll=32)
+    lax.fori_loop(0, channels // (count * together), some_pairs, 0, unroll=16)
 
 
 def left_operand(chunks):
     halves, channels, chan_count, lanes = chunks[0].shape
-    depth = 2 * 2 * len(chunks) * chan_count
+    depth = 2 * len(chunks) * chan_count
+    count = lanes // depth
     tile = 128
     return pl.pallas_call(
         left_kernel,
-        out_shape=jax.ShapeDtypeStruct((halves, channels // 2, lanes // 2, depth), jnp.bfloat16),
+        out_shape=jax.ShapeDtypeStruct((halves, channels // count, lanes // 2, lanes), jnp.bfloat16),
         grid=(halves, channels // tile),
         in_specs=[pl.BlockSpec((1, tile, chan_count, lanes), lambda u, i: (u, i, 0, 0))]
         * len(chunks),
-        out_specs=pl.BlockSpec((1, tile // 2, lanes // 2, depth), lambda u, i: (u, i, 0, 0)),
+        out_specs=pl.BlockSpec((1, tile // count, lanes // 2, lanes), lambda u, i: (u, i, 0, 0)),
         compiler_params=pltpu.CompilerParams(vmem_limit_bytes=VMEM_LIMIT),
         name="left_operand",
     )(*chunks)
@@ -498,7 +515,13 @@
         lax.broadcasted_iota(jnp.int32, (chan_count, lanes), 1) < sig_count, 1.0, -1.0
     ).astype(jnp.float32)
 
-    def pair(step, carry):
+    def pairs(step, carry):
+        left = left_ref[0, step]
+        for i in range(2):
+            pair(2 * step + i, left[:, i * sig_count : (i + 1) * sig_count])
+        return carry
+
+    def pair(step, left):
         blocks = []
         for i in range(2):
             values = [ref[2 * step + i].astype(jnp.float32) for ref in chunk_refs]
@@ -513,16 +536,15 @@
             ],
             axis=0,
         )
-        both = jnp.dot(left_ref[0, step], weights, preferred_element_type=jnp.float32)
+        both = jnp.dot(left, weights, preferred_element_type=jnp.float32)
         for i in range(2):
             q = 2 * step + i
             for a in range(0, sig_count, EIGHT):
                 sum_ref[pl.ds(a * pitch + q, EIGHT, stride=pitch), :] = both[
                     a : a + EIGHT, i * lanes : (i + 1) * lanes
                 ]
-        return carry
-
-    lax.fori_loop(0, channels // 2, pair, 0, unroll=32)
+
+    lax.fori_loop(0, channels // 4, pairs, 0, unroll=32)
 
     def finish(a, carry):
         rows = pl.ds(a * pitch, channels)
@@ -534,6 +556,7 @@
 
 def correlate(left, chunks, group_id, plan, distance, spec_count, so_far):
     channels, chan_count, lanes = chunks[0].shape
+    per_left = channels // left.shape[1]
     sig_count, depth = left.shape[2:]
     rounds = plan.shape[0]
     tile = 128
@@ -549,7 +572,7 @@
         return found
 
     in_specs = [
-        pl.BlockSpec((1, tile // 2, sig_count, depth), lambda i, g, p: (half_of(g), i, 0, 0)),
+        pl.BlockSpec((1, tile // per_left, sig_count, depth), lambda i, g, p: (half_of(g), i, 0, 0)),
     ] + [pl.BlockSpec((tile, chan_count, lanes), lambda i, g, p: (i, 0, 0))] * len(chunks)
     operands = [left, *chunks]
     aliases = {}
@@ -645,9 +668,10 @@
 
     def over_chan(blocks):
         moved = list(blocks)
-        for shift in farthest_first(chan_count):
-            pairs = [(c, (c + shift) % chan_count) for c in range(chan_count)]
-            moved[shift] = lax.ppermute(blocks[shift], "chan", pairs)
+        for pair in farthest_first(chan_count):
+            moved[pair] = lax.ppermute(
+                blocks[pair], "chan", [(c, c ^ pair) for c in range(chan_count)]
+            )
         return moved
 
     def to_mate(value, distance):
@@ -657,9 +681,17 @@
     channels = []
     chunks = spec_count // chan_count
     for chunk in range(chunks):
-        blocks = filter_by_shift(frames_first, chan_id, chan_count, chunk * chan_count)
+        if chunk:
+            parts = (range(chan_count),)
+        else:
+            parts = (range(chan_count // 2, chan_count), range(chan_count // 2))
+        blocks = [None] * chan_count
+        for pairs in parts:
+            blocks[pairs.start : pairs.stop] = filter_by_pair(
+                frames_first, chan_id, chan_count, chunk * chan_count, pairs
+            )
         blocks = over_chan(blocks)
-        blocks = transform_by_shift(blocks, chan_id)
+        blocks = transform_by_pair(blocks, chan_id)
         channels.append(over_chan(blocks))
     for channel in channels:
         halves, for_near, for_across = turn(channel, group_id)
@@ -675,7 +707,8 @@
 
 
 def farthest_first(chan_count):
-    return sorted(range(1, chan_count), key=lambda shift: abs(shift - chan_count // 2))
+    half = chan_count // 2
+    return list(range(half, chan_count)) + list(range(1, half))
 
 
 def overlaps(group_count, chan_count):

time: 156 us -> 159 us (1.019); the launches traced: 155 us -> 156 us
  waiting for transfers between devices: 19.9 us -> 50.6 us
  starting transfers between devices: 75.1 us -> 53.6 us
  local copies, waits for them, and re-layouts: 5.45 us -> 0 us
  Pallas kernels: 54.2 us -> 51.8 us
    ppermute x28, waiting for transfers between devices: 10.2 us -> 37 us  [over_chan(): lax.ppermute(blocks[pair], 'chan', [(c, c ^ pair) for c in range(chan_cou...]
    ppermute x28, starting transfers between devices: 72.4 us -> 50.9 us  [over_chan(): lax.ppermute(blocks[pair], 'chan', [(c, c ^ pair) for c in range(chan_cou...]
    unnamed x68 -> x0, local copies, waits for them, and re-layouts: 5.45 us -> none
    ppermute x6, waiting for transfers between devices: 9.66 us -> 13.6 us  [to_mate(): lax.ppermute(value, 'grp', [(g, g ^ distance) for g in range(group_count)])]
    pallas_call x3, Pallas kernels: 17.9 us -> 16 us  [correlate(): pl.pallas_call(functools.partial(correlate_kernel, len(chunks), spec_coun...]
    pallas_call x1, Pallas kernels: 6.45 us -> 4.81 us  [left_operand(): pl.pallas_call(left_kernel, out_shape=jax.ShapeDtypeStruct((halves, chann...]
    pallas_call x4 -> x5, Pallas kernels: 24.1 us -> 25.3 us  [the longest x3 13.3 us: filter_by_pair(): pl.pallas_call(functools.partial(filter_by_pair_kernel, pairs), out_shape...]
  transfers between devices with their start and end apart: 34 -> 34, of which waited for: 5 -> 10; matrix products, arithmetic and copies ran while one was open for 0% -> 0% of each run, Pallas kernels for 27% -> 27%
where the time goes in v7:
time: 159 us; the launch traced here: 156 us
  starting transfers between devices  53.6 us (34%)
  Pallas kernels  51.8 us (33%)
  waiting for transfers between devices  50.6 us (32%)
    ppermute x28, starting transfers between devices, over_chan(): lax.ppermute(blocks[pair], 'chan', [(c, c ^ pair) for c in range(chan_cou...  50.9 us
    ppermute x28, waiting for transfers between devices, over_chan(): lax.ppermute(blocks[pair], 'chan', [(c, c ^ pair) for c in range(chan_cou...  37 us
    pallas_call x3, Pallas kernels, correlate(): pl.pallas_call(functools.partial(correlate_kernel, len(chunks), spec_coun...  16 us
    ppermute x6, waiting for transfers between devices, to_mate(): lax.ppermute(value, 'grp', [(g, g ^ distance) for g in range(group_count)])  13.6 us
    pallas_call x3, Pallas kernels, filter_by_pair(): pl.pallas_call(functools.partial(filter_by_pair_kernel, pairs), out_shape...  13.3 us
    pallas_call x2, Pallas kernels, transform_by_pair(): pl.pallas_call(functools.partial(transform_by_pair_kernel, chan_count), o...  12 us
    pallas_call x2, Pallas kernels, turn(): pl.pallas_call(turn_kernel, out_shape=[jax.ShapeDtypeStruct((halves,) + o...  5.74 us
    pallas_call x1, Pallas kernels, left_operand(): pl.pallas_call(left_kernel, out_shape=jax.ShapeDtypeStruct((halves, chann...  4.81 us
  transfers between devices with their start and end apart: 34, of which 10 were waited for; matrix products, arithmetic and copies ran while one was open for 0% of the time, Pallas kernels for 27%

profile of v7, /device:TPU:0, one launch (start us, length us, event | category | flops | bytes accessed | tf_op | source)
XLA Modules:
  0.0 156.2 jit_solution(4304626308171895407)
XLA Ops:
  0.0 4.0 %filter_by_pair.4 = (bf16[64,1024]{1,0:T(8,128)(2,1)}, bf16[64,1024]{1,0:T(8,128)(2,1)}, bf16[64,1024]{1,0:T(8,128)(2,1)}, bf16[64,1024]{1,0:T(8,128)(2,1)}) custom-call(s32[1]{0:T(128)} %bitcast.1.chan_ref.refs_0_, s32[31,64,1024]{2,1,0:T(8,128)} %bitcast.3, f32[8,16,1024]{2,1,0:T(8,128)} %constant.18.clone.coeff_ref), custom_call_target="tpu_custom_call" | custom-call | tf_op jit(solution)/shard_map/filter_by_pair/pallas_call | solution.py:99
  4.0 4.1 %collective-permute-start.3 = (bf16[64,1024]{1,0:T(8,128)(2,1)}, bf16[64,1024]{1,0:T(8,128)(2,1)}, u32[]{:S(2)}, u32[]{:S(2)}) collective-permute-start(bf16[64,1024]{1,0:T(8,128)(2,1)} %get-tuple-element.50), channel_id=1, source_target_pairs={{0,4},{1,5},{2,6},{3,7},{4,0},{5,1},{6,2},{7,3},{8,12},{9,13},{10,... | collective-permute-start | bytes 393224 | tf_op jit(solution)/shard_map/ppermute | solution.py:672
  9.3 3.6 %collective-permute-start.5 = (bf16[64,1024]{1,0:T(8,128)(2,1)}, bf16[64,1024]{1,0:T(8,128)(2,1)}, u32[]{:S(2)}, u32[]{:S(2)}) collective-permute-start(bf16[64,1024]{1,0:T(8,128)(2,1)} %get-tuple-element.52), channel_id=1, source_target_pairs={{0,6},{1,7},{2,4},{3,5},{4,2},{5,3},{6,0},{7,1},{8,14},{9,15},{10,... | collective-permute-start | bytes 393224 | tf_op jit(solution)/shard_map/ppermute | solution.py:672
  12.9 4.0 %filter_by_pair.3 = (bf16[64,1024]{1,0:T(8,128)(2,1)}, bf16[64,1024]{1,0:T(8,128)(2,1)}, bf16[64,1024]{1,0:T(8,128)(2,1)}, bf16[64,1024]{1,0:T(8,128)(2,1)}) custom-call(s32[1]{0:T(128)} %bitcast.1.chan_ref.refs_0_, s32[31,64,1024]{2,1,0:T(8,128)} %bitcast.4, f32[8,16,1024]{2,1,0:T(8,128)} %constant.18.clone.coeff_ref), custom_call_target="tpu_custom_call" | custom-call | tf_op jit(solution)/shard_map/filter_by_pair/pallas_call | solution.py:99
  18.5 5.4 %filter_by_pair.5 = (bf16[64,1024]{1,0:T(8,128)(2,1)}, bf16[64,1024]{1,0:T(8,128)(2,1)}, bf16[64,1024]{1,0:T(8,128)(2,1)}, bf16[64,1024]{1,0:T(8,128)(2,1)}, bf1...) custom-call(s32[1]{0:T(128)} %bitcast.1.chan_ref.refs_0_, ...), custom_call_target="tpu_custom_call" | custom-call | tf_op jit(solution)/shard_map/filter_by_pair/pallas_call | solution.py:99
  24.0 4.0 %collective-permute-done.4.refs_10_ = bf16[64,1024]{1,0:T(8,128)(2,1)} collective-permute-done((bf16[64,1024]{1,0:T(8,128)(2,1)}, bf16[64,1024]{1,0:T(8,128)(2,1)}, u32[]{:S(2)}, u32[]{:S(2)}) %collective-permute-start.4) | collective-permute-done | bytes 131104 | tf_op jit(solution)/shard_map/ppermute | solution.py:672
  28.2 6.9 %collective-permute-start.15 = (bf16[64,1024]{1,0:T(8,128)(2,1)}, bf16[64,1024]{1,0:T(8,128)(2,1)}, u32[]{:S(2)}, u32[]{:S(2)}) collective-permute-start(bf16[64,1024]{1,0:T(8,128)(2,1)} %get-tuple-element.65), channel_id=1, source_target_pairs={{0,2},{1,3},{2,0},{3,1},{4,6},{5,7},{6,4},{7,5},{8,10},{9,11},{10,... | collective-permute-start | bytes 393224 | tf_op jit(solution)/shard_map/ppermute | solution.py:672
  35.1 4.1 %collective-permute-start.17 = (bf16[64,1024]{1,0:T(8,128)(2,1)}, bf16[64,1024]{1,0:T(8,128)(2,1)}, u32[]{:S(2)}, u32[]{:S(2)}) collective-permute-start(bf16[64,1024]{1,0:T(8,128)(2,1)} %get-tuple-element.67), channel_id=1, source_target_pairs={{0,4},{1,5},{2,6},{3,7},{4,0},{5,1},{6,2},{7,3},{8,12},{9,13},{10,... | collective-permute-start | bytes 393224 | tf_op jit(solution)/shard_map/ppermute | solution.py:672
  44.7 6.0 %transform_by_pair.2 = (bf16[2,8,32,128]{3,2,1,0:T(8,128)(2,1)}, bf16[2,8,32,128]{3,2,1,0:T(8,128)(2,1)}, bf16[2,8,32,128]{3,2,1,0:T(8,128)(2,1)}, bf16[2,8,32,1...) custom-call(s32[1]{0:T(128)} %bitcast.1.chan_ref.refs_0_, ...), custom_call_target="tpu_custom_call" | custom-call | tf_op jit(solution)/shard_map/transform_by_pair/pallas_call | solution.py:381
  54.8 4.7 %collective-permute-done.18.refs_10_ = bf16[64,1024]{1,0:T(8,128)(2,1)} collective-permute-done((bf16[64,1024]{1,0:T(8,128)(2,1)}, bf16[64,1024]{1,0:T(8,128)(2,1)}, u32[]{:S(2)}, u32[]{:S(2)}) %collective-permute-start.18) | collective-permute-done | bytes 131104 | tf_op jit(solution)/shard_map/ppermute | solution.py:672
  59.5 6.0 %transform_by_pair.3 = (bf16[2,8,32,128]{3,2,1,0:T(8,128)(2,1)}, bf16[2,8,32,128]{3,2,1,0:T(8,128)(2,1)}, bf16[2,8,32,128]{3,2,1,0:T(8,128)(2,1)}, bf16[2,8,32,1...) custom-call(s32[1]{0:T(128)} %bitcast.1.chan_ref.refs_0_, ...), custom_call_target="tpu_custom_call" | custom-call | tf_op jit(solution)/shard_map/transform_by_pair/pallas_call | solution.py:381
  66.5 4.7 %collective-permute-start.22 = (bf16[2,8,32,128]{3,2,1,0:T(8,128)(2,1)}, bf16[2,8,32,128]{3,2,1,0:T(8,128)(2,1)}, u32[]{:S(2)}, u32[]{:S(2)}) collective-permute-start(bf16[2,8,32,128]{3,2,1,0:T(8,128)(2,1)} %get-tuple-element.73), channel_id=1, source_target_pairs={{0,2},{1,3},{2,0},{3,1},{4,6},{5,7},{6,4},{7,5},{8,10},{9,11},{10,... | collective-permute-start | bytes 393224 | tf_op jit(solution)/shard_map/ppermute | solution.py:672
  77.7 3.3 %collective-permute-start.27 = (bf16[2,8,32,128]{3,2,1,0:T(8,128)(2,1)}, bf16[2,8,32,128]{3,2,1,0:T(8,128)(2,1)}, u32[]{:S(2)}, u32[]{:S(2)}) collective-permute-start(bf16[2,8,32,128]{3,2,1,0:T(8,128)(2,1)} %get-tuple-element.78), channel_id=1, source_target_pairs={{0,7},{1,6},{2,5},{3,4},{4,3},{5,2},{6,1},{7,0},{8,15},{9,14},{10,... | collective-permute-start | bytes 393224 | tf_op jit(solution)/shard_map/ppermute | solution.py:672
  81.2 8.2 %collective-permute-done.24.refs_4_ = bf16[2,8,32,128]{3,2,1,0:T(8,128)(2,1)} collective-permute-done((bf16[2,8,32,128]{3,2,1,0:T(8,128)(2,1)}, bf16[2,8,32,128]{3,2,1,0:T(8,128)(2,1)}, u32[]{:S(2)}, u32[]{:S(2)}) %collective-permute-start.24) | collective-permute-done | bytes 131104 | tf_op jit(solution)/shard_map/ppermute | solution.py:672
  89.4 11.3 %collective-permute-done.25.refs_5_ = bf16[2,8,32,128]{3,2,1,0:T(8,128)(2,1)} collective-permute-done((bf16[2,8,32,128]{3,2,1,0:T(8,128)(2,1)}, bf16[2,8,32,128]{3,2,1,0:T(8,128)(2,1)}, u32[]{:S(2)}, u32[]{:S(2)}) %collective-permute-start.25) | collective-permute-done | bytes 131104 | tf_op jit(solution)/shard_map/ppermute | solution.py:672
  108.2 5.0 %collective-permute-done.10.refs_4_ = bf16[2,8,32,128]{3,2,1,0:T(8,128)(2,1)} collective-permute-done((bf16[2,8,32,128]{3,2,1,0:T(8,128)(2,1)}, bf16[2,8,32,128]{3,2,1,0:T(8,128)(2,1)}, u32[]{:S(2)}, u32[]{:S(2)}) %collective-permute-start.10) | collective-permute-done | bytes 131104 | tf_op jit(solution)/shard_map/ppermute | solution.py:672
  113.1 3.0 %collective-permute-done.11.refs_5_ = bf16[2,8,32,128]{3,2,1,0:T(8,128)(2,1)} collective-permute-done((bf16[2,8,32,128]{3,2,1,0:T(8,128)(2,1)}, bf16[2,8,32,128]{3,2,1,0:T(8,128)(2,1)}, u32[]{:S(2)}, u32[]{:S(2)}) %collective-permute-start.11) | collective-permute-done | bytes 131104 | tf_op jit(solution)/shard_map/ppermute | solution.py:672
  116.1 2.9 %turn.2 = (bf16[2,256,8,128]{3,2,1,0:T(8,128)(2,1)}, bf16[256,8,128]{2,1,0:T(8,128)(2,1)}, bf16[256,8,128]{2,1,0:T(8,128)(2,1)}) custom-call(s32[1]{0:T(128)} %bitcast.group_ref, bf16[2,8,32,128]{3,2,1,0:T(8,128)(2,1)} %get-tuple-element.54.refs_0_, bf16[2,8,32,128]{3,2,1,0:T(8,128)(2,1)} %collective-permute-done.7.refs_1_, ...), custom_call_target="tpu_custom_call" | custom-call | tf_op jit(solution)/shard_map/turn/pallas_call | solution.py:437
  121.2 4.8 %left_operand.1.left_ref = bf16[2,64,64,128]{3,2,1,0:T(8,128)(2,1)} custom-call(bf16[2,256,8,128]{3,2,1,0:T(8,128)(2,1)} %get-tuple-element.62.refs_0_, bf16[2,256,8,128]{3,2,1,0:T(8,128)(2,1)} %get-tuple-element.79.refs_1_), custom_call_target="tpu_custom_call" | custom-call | tf_op jit(solution)/shard_map/left_operand/pallas_call | solution.py:495
  126.0 5.3 %correlate.3.refs_2_ = bf16[3,64,256,128]{3,2,1,0:T(8,128)(2,1)} custom-call(s32[1]{0:T(128)} %bitcast.group_ref, s32[3,4]{1,0:T(4,128)} %plan_ref.5, bf16[2,64,64,128]{3,2,1,0:T(8,128)(2,1)} %left_operand.1.left_ref, bf16[256,8,128]{2,1,0:T(8,128)(2,1)} %collective-permute-done.30.refs_0_, bf16[256,8,128]{2,1,0:T(8,128)(2,1)} %collective-permute-done.31.refs_1_), custom_call_target="tpu_custom_call" | custom-call | flops 536870912 | bytes 16777216 | tf_op jit(solution)/shard_map/correlate/pallas_call | solution.py:583
  131.3 2.9 %collective-permute-done.29.refs_1_ = bf16[256,8,128]{2,1,0:T(8,128)(2,1)} collective-permute-done((bf16[256,8,128]{2,1,0:T(8,128)(2,1)}, bf16[256,8,128]{2,1,0:T(8,128)(2,1)}, u32[]{:S(2)}, u32[]{:S(2)}) %collective-permute-start.29) | collective-permute-done | bytes 524320 | tf_op jit(solution)/shard_map/ppermute | solution.py:678
  134.3 10.7 %collective-permute-done.28.refs_0_ = bf16[256,8,128]{2,1,0:T(8,128)(2,1)} collective-permute-done((bf16[256,8,128]{2,1,0:T(8,128)(2,1)}, bf16[256,8,128]{2,1,0:T(8,128)(2,1)}, u32[]{:S(2)}, u32[]{:S(2)}) %collective-permute-start.28) | collective-permute-done | bytes 524320 | tf_op jit(solution)/shard_map/ppermute | solution.py:678
  145.5 5.3 %correlate.4.refs_2_ = bf16[3,64,256,128]{3,2,1,0:T(8,128)(2,1)} custom-call(s32[1]{0:T(128)} %bitcast.group_ref, s32[3,4]{1,0:T(4,128)} %plan_ref.5, bf16[2,64,64,128]{3,2,1,0:T(8,128)(2,1)} %left_operand.1.left_ref, bf16[256,8,128]{2,1,0:T(8,128)(2,1)} %collective-permute-done.28.refs_0_, ...), custom_call_target="tpu_custom_call", output_to_operand_aliasing={{}: (5, {})} | custom-call | flops 536870912 | bytes 16777216 | tf_op jit(solution)/shard_map/correlate/pallas_call | solution.py:583
  150.8 5.3 %correlate.5 = bf16[3,64,256,128]{3,2,1,0:T(8,128)(2,1)} custom-call(s32[1]{0:T(128)} %bitcast.group_ref, s32[3,4]{1,0:T(4,128)} %plan_ref.5, bf16[2,64,64,128]{3,2,1,0:T(8,128)(2,1)} %left_operand.1.left_ref, bf16[256,8,128]{2,1,0:T(8,128)(2,1)} %collective-permute-done.32.refs_0_, ...), custom_call_target="tpu_custom_call", output_to_operand_aliasing={{}: (5, {})} | custom-call | flops 536870912 | bytes 16777216 | tf_op jit(solution)/shard_map/correlate/pallas_call | solution.py:583
  (55 shorter events, 30.6 us)
Async XLA Ops:
  4.0 20.0 %collective-permute-start.3 = (bf16[64,1024]{1,0:T(8,128)(2,1)}, bf16[64,1024]{1,0:T(8,128)(2,1)}, u32[]{:S(2)}, u32[]{:S(2)}) collective-permute-start(bf16[64,1024]{1,0:T(8,128)(2,1)} %get-tuple-element.50), channel_id=1, source_target_pairs={{0,4},{1,5},{2,6},{3,7},{4,0},{5,1},{6,2},{7,3},{8,12},{9,13},{10,... | collective-permute-start | bytes 393224 | tf_op jit(solution)/shard_map/ppermute | solution.py:672
  8.0 20.0 %collective-permute-start.4 = (bf16[64,1024]{1,0:T(8,128)(2,1)}, bf16[64,1024]{1,0:T(8,128)(2,1)}, u32[]{:S(2)}, u32[]{:S(2)}) collective-permute-start(bf16[64,1024]{1,0:T(8,128)(2,1)} %get-tuple-element.51), channel_id=1, source_target_pairs={{0,5},{1,4},{2,7},{3,6},{4,1},{5,0},{6,3},{7,2},{8,13},{9,12},{10,... | collective-permute-start | bytes 393224 | tf_op jit(solution)/shard_map/ppermute | solution.py:672
  9.3 18.7 %collective-permute-start.5 = (bf16[64,1024]{1,0:T(8,128)(2,1)}, bf16[64,1024]{1,0:T(8,128)(2,1)}, u32[]{:S(2)}, u32[]{:S(2)}) collective-permute-start(bf16[64,1024]{1,0:T(8,128)(2,1)} %get-tuple-element.52), channel_id=1, source_target_pairs={{0,6},{1,7},{2,4},{3,5},{4,2},{5,3},{6,0},{7,1},{8,14},{9,15},{10,... | collective-permute-start | bytes 393224 | tf_op jit(solution)/shard_map/ppermute | solution.py:672
  12.9 15.3 %collective-permute-start.6 = (bf16[64,1024]{1,0:T(8,128)(2,1)}, bf16[64,1024]{1,0:T(8,128)(2,1)}, u32[]{:S(2)}, u32[]{:S(2)}) collective-permute-start(bf16[64,1024]{1,0:T(8,128)(2,1)} %get-tuple-element.53), channel_id=1, source_target_pairs={{0,7},{1,6},{2,5},{3,4},{4,3},{5,2},{6,1},{7,0},{8,15},{9,14},{10,... | collective-permute-start | bytes 393224 | tf_op jit(solution)/shard_map/ppermute | solution.py:672
  16.9 18.2 %collective-permute-start = (bf16[64,1024]{1,0:T(8,128)(2,1)}, bf16[64,1024]{1,0:T(8,128)(2,1)}, u32[]{:S(2)}, u32[]{:S(2)}) collective-permute-start(bf16[64,1024]{1,0:T(8,128)(2,1)} %get-tuple-element.47), channel_id=1, source_target_pairs={{0,1},{1,0},{2,3},{3,2},{4,5},{5,4},{6,7},{7,6},{8,9},{9,8},{10,11... | collective-permute-start | bytes 393224 | tf_op jit(solution)/shard_map/ppermute | solution.py:672
  28.2 14.9 %collective-permute-start.15 = (bf16[64,1024]{1,0:T(8,128)(2,1)}, bf16[64,1024]{1,0:T(8,128)(2,1)}, u32[]{:S(2)}, u32[]{:S(2)}) collective-permute-start(bf16[64,1024]{1,0:T(8,128)(2,1)} %get-tuple-element.65), channel_id=1, source_target_pairs={{0,2},{1,3},{2,0},{3,1},{4,6},{5,7},{6,4},{7,5},{8,10},{9,11},{10,... | collective-permute-start | bytes 393224 | tf_op jit(solution)/shard_map/ppermute | solution.py:672
  35.1 15.6 %collective-permute-start.16 = (bf16[64,1024]{1,0:T(8,128)(2,1)}, bf16[64,1024]{1,0:T(8,128)(2,1)}, u32[]{:S(2)}, u32[]{:S(2)}) collective-permute-start(bf16[64,1024]{1,0:T(8,128)(2,1)} %get-tuple-element.66), channel_id=1, source_target_pairs={{0,3},{1,2},{2,1},{3,0},{4,7},{5,6},{6,5},{7,4},{8,11},{9,10},{10,... | collective-permute-start | bytes 393224 | tf_op jit(solution)/shard_map/ppermute | solution.py:672
  35.1 17.8 %collective-permute-start.17 = (bf16[64,1024]{1,0:T(8,128)(2,1)}, bf16[64,1024]{1,0:T(8,128)(2,1)}, u32[]{:S(2)}, u32[]{:S(2)}) collective-permute-start(bf16[64,1024]{1,0:T(8,128)(2,1)} %get-tuple-element.67), channel_id=1, source_target_pairs={{0,4},{1,5},{2,6},{3,7},{4,0},{5,1},{6,2},{7,3},{8,12},{9,13},{10,... | collective-permute-start | bytes 393224 | tf_op jit(solution)/shard_map/ppermute | solution.py:672
  39.2 20.3 %collective-permute-start.18 = (bf16[64,1024]{1,0:T(8,128)(2,1)}, bf16[64,1024]{1,0:T(8,128)(2,1)}, u32[]{:S(2)}, u32[]{:S(2)}) collective-permute-start(bf16[64,1024]{1,0:T(8,128)(2,1)} %get-tuple-element.68), channel_id=1, source_target_pairs={{0,5},{1,4},{2,7},{3,6},{4,1},{5,0},{6,3},{7,2},{8,13},{9,12},{10,... | collective-permute-start | bytes 393224 | tf_op jit(solution)/shard_map/ppermute | solution.py:672
  40.9 18.6 %collective-permute-start.19 = (bf16[64,1024]{1,0:T(8,128)(2,1)}, bf16[64,1024]{1,0:T(8,128)(2,1)}, u32[]{:S(2)}, u32[]{:S(2)}) collective-permute-start(bf16[64,1024]{1,0:T(8,128)(2,1)} %get-tuple-element.69), channel_id=1, source_target_pairs={{0,6},{1,7},{2,4},{3,5},{4,2},{5,3},{6,0},{7,1},{8,14},{9,15},{10,... | collective-permute-start | bytes 393224 | tf_op jit(solution)/shard_map/ppermute | solution.py:672
  43.2 16.3 %collective-permute-start.20 = (bf16[64,1024]{1,0:T(8,128)(2,1)}, bf16[64,1024]{1,0:T(8,128)(2,1)}, u32[]{:S(2)}, u32[]{:S(2)}) collective-permute-start(bf16[64,1024]{1,0:T(8,128)(2,1)} %get-tuple-element.70), channel_id=1, source_target_pairs={{0,7},{1,6},{2,5},{3,4},{4,3},{5,2},{6,1},{7,0},{8,15},{9,14},{10,... | collective-permute-start | bytes 393224 | tf_op jit(solution)/shard_map/ppermute | solution.py:672
  50.7 21.1 %collective-permute-start.7 = (bf16[2,8,32,128]{3,2,1,0:T(8,128)(2,1)}, bf16[2,8,32,128]{3,2,1,0:T(8,128)(2,1)}, u32[]{:S(2)}, u32[]{:S(2)}) collective-permute-start(bf16[2,8,32,128]{3,2,1,0:T(8,128)(2,1)} %get-tuple-element.55), channel_id=1, source_target_pairs={{0,1},{1,0},{2,3},{3,2},{4,5},{5,4},{6,7},{7,6},{8,9},{9,8},{10,11... | collective-permute-start | bytes 393224 | tf_op jit(solution)/shard_map/ppermute | solution.py:672
  52.9 21.7 %collective-permute-start.8 = (bf16[2,8,32,128]{3,2,1,0:T(8,128)(2,1)}, bf16[2,8,32,128]{3,2,1,0:T(8,128)(2,1)}, u32[]{:S(2)}, u32[]{:S(2)}) collective-permute-start(bf16[2,8,32,128]{3,2,1,0:T(8,128)(2,1)} %get-tuple-element.56), channel_id=1, source_target_pairs={{0,2},{1,3},{2,0},{3,1},{4,6},{5,7},{6,4},{7,5},{8,10},{9,11},{10,... | collective-permute-start | bytes 393224 | tf_op jit(solution)/shard_map/ppermute | solution.py:672
  71.8 17.6 %collective-permute-start.24 = (bf16[2,8,32,128]{3,2,1,0:T(8,128)(2,1)}, bf16[2,8,32,128]{3,2,1,0:T(8,128)(2,1)}, u32[]{:S(2)}, u32[]{:S(2)}) collective-permute-start(bf16[2,8,32,128]{3,2,1,0:T(8,128)(2,1)} %get-tuple-element.75), channel_id=1, source_target_pairs={{0,4},{1,5},{2,6},{3,7},{4,0},{5,1},{6,2},{7,3},{8,12},{9,13},{10,... | collective-permute-start | bytes 393224 | tf_op jit(solution)/shard_map/ppermute | solution.py:672
  74.7 26.0 %collective-permute-start.25 = (bf16[2,8,32,128]{3,2,1,0:T(8,128)(2,1)}, bf16[2,8,32,128]{3,2,1,0:T(8,128)(2,1)}, u32[]{:S(2)}, u32[]{:S(2)}) collective-permute-start(bf16[2,8,32,128]{3,2,1,0:T(8,128)(2,1)} %get-tuple-element.76), channel_id=1, source_target_pairs={{0,5},{1,4},{2,7},{3,6},{4,1},{5,0},{6,3},{7,2},{8,13},{9,12},{10,... | collective-permute-start | bytes 393224 | tf_op jit(solution)/shard_map/ppermute | solution.py:672
  75.1 25.6 %collective-permute-start.26 = (bf16[2,8,32,128]{3,2,1,0:T(8,128)(2,1)}, bf16[2,8,32,128]{3,2,1,0:T(8,128)(2,1)}, u32[]{:S(2)}, u32[]{:S(2)}) collective-permute-start(bf16[2,8,32,128]{3,2,1,0:T(8,128)(2,1)} %get-tuple-element.77), channel_id=1, source_target_pairs={{0,6},{1,7},{2,4},{3,5},{4,2},{5,3},{6,0},{7,1},{8,14},{9,15},{10,... | collective-permute-start | bytes 393224 | tf_op jit(solution)/shard_map/ppermute | solution.py:672
  77.7 24.7 %collective-permute-start.27 = (bf16[2,8,32,128]{3,2,1,0:T(8,128)(2,1)}, bf16[2,8,32,128]{3,2,1,0:T(8,128)(2,1)}, u32[]{:S(2)}, u32[]{:S(2)}) collective-permute-start(bf16[2,8,32,128]{3,2,1,0:T(8,128)(2,1)} %get-tuple-element.78), channel_id=1, source_target_pairs={{0,7},{1,6},{2,5},{3,4},{4,3},{5,2},{6,1},{7,0},{8,15},{9,14},{10,... | collective-permute-start | bytes 393224 | tf_op jit(solution)/shard_map/ppermute | solution.py:672
  81.1 27.0 %collective-permute-start.9 = (bf16[2,8,32,128]{3,2,1,0:T(8,128)(2,1)}, bf16[2,8,32,128]{3,2,1,0:T(8,128)(2,1)}, u32[]{:S(2)}, u32[]{:S(2)}) collective-permute-start(bf16[2,8,32,128]{3,2,1,0:T(8,128)(2,1)} %get-tuple-element.57), channel_id=1, source_target_pairs={{0,3},{1,2},{2,1},{3,0},{4,7},{5,6},{6,5},{7,4},{8,11},{9,10},{10,... | collective-permute-start | bytes 393224 | tf_op jit(solution)/shard_map/ppermute | solution.py:672
  89.4 23.7 %collective-permute-start.10 = (bf16[2,8,32,128]{3,2,1,0:T(8,128)(2,1)}, bf16[2,8,32,128]{3,2,1,0:T(8,128)(2,1)}, u32[]{:S(2)}, u32[]{:S(2)}) collective-permute-start(bf16[2,8,32,128]{3,2,1,0:T(8,128)(2,1)} %get-tuple-element.58), channel_id=1, source_target_pairs={{0,4},{1,5},{2,6},{3,7},{4,0},{5,1},{6,2},{7,3},{8,12},{9,13},{10,... | collective-permute-start | bytes 393224 | tf_op jit(solution)/shard_map/ppermute | solution.py:672
  100.7 15.4 %collective-permute-start.11 = (bf16[2,8,32,128]{3,2,1,0:T(8,128)(2,1)}, bf16[2,8,32,128]{3,2,1,0:T(8,128)(2,1)}, u32[]{:S(2)}, u32[]{:S(2)}) collective-permute-start(bf16[2,8,32,128]{3,2,1,0:T(8,128)(2,1)} %get-tuple-element.59), channel_id=1, source_target_pairs={{0,5},{1,4},{2,7},{3,6},{4,1},{5,0},{6,3},{7,2},{8,13},{9,12},{10,... | collective-permute-start | bytes 393224 | tf_op jit(solution)/shard_map/ppermute | solution.py:672
  100.7 15.4 %collective-permute-start.12 = (bf16[2,8,32,128]{3,2,1,0:T(8,128)(2,1)}, bf16[2,8,32,128]{3,2,1,0:T(8,128)(2,1)}, u32[]{:S(2)}, u32[]{:S(2)}) collective-permute-start(bf16[2,8,32,128]{3,2,1,0:T(8,128)(2,1)} %get-tuple-element.60), channel_id=1, source_target_pairs={{0,6},{1,7},{2,4},{3,5},{4,2},{5,3},{6,0},{7,1},{8,14},{9,15},{10,... | collective-permute-start | bytes 393224 | tf_op jit(solution)/shard_map/ppermute | solution.py:672
  108.1 17.9 %collective-permute-start.31 = (bf16[256,8,128]{2,1,0:T(8,128)(2,1)}, bf16[256,8,128]{2,1,0:T(8,128)(2,1)}, u32[]{:S(2)}, u32[]{:S(2)}) collective-permute-start(bf16[256,8,128]{2,1,0:T(8,128)(2,1)} %get-tuple-element.83), channel_id=1, source_target_pairs={{0,8},{8,0},{16,24},{24,16},{1,9},{9,1},{17,25},{25,17},{2,10},{10... | collective-permute-start | bytes 1572872 | tf_op jit(solution)/shard_map/ppermute | solution.py:678
  119.1 15.2 %collective-permute-start.29 = (bf16[256,8,128]{2,1,0:T(8,128)(2,1)}, bf16[256,8,128]{2,1,0:T(8,128)(2,1)}, u32[]{:S(2)}, u32[]{:S(2)}) collective-permute-start(bf16[256,8,128]{2,1,0:T(8,128)(2,1)} %get-tuple-element.81), channel_id=1, source_target_pairs={{0,16},{8,24},{16,0},{24,8},{1,17},{9,25},{17,1},{25,9},{2,18},{10... | collective-permute-start | bytes 1572872 | tf_op jit(solution)/shard_map/ppermute | solution.py:678
  120.7 24.3 %collective-permute-start.28 = (bf16[256,8,128]{2,1,0:T(8,128)(2,1)}, bf16[256,8,128]{2,1,0:T(8,128)(2,1)}, u32[]{:S(2)}, u32[]{:S(2)}) collective-permute-start(bf16[256,8,128]{2,1,0:T(8,128)(2,1)} %get-tuple-element.80), channel_id=1, source_target_pairs={{0,16},{8,24},{16,0},{24,8},{1,17},{9,25},{17,1},{25,9},{2,18},{10... | collective-permute-start | bytes 1572872 | tf_op jit(solution)/shard_map/ppermute | solution.py:678
  (10 other events, 98.2 us)

commit v8 on v7

--- a/solution.py
+++ b/solution.py
@@ -394,8 +394,12 @@
     )(chan_id, *transform_tables(chan_count * block_len), *blocks)
 
 
-def turn_kernel(group_ref, *refs):
-    in_refs, (out_ref, near_ref, across_ref, wide_ref) = refs[:-4], refs[-4:]
+def turn_kernel(other, group_ref, *refs):
+    wide_ref = refs[-1]
+    if other:
+        in_refs, (across_ref, out_ref, near_ref) = refs[:-4], refs[-4:-1]
+    else:
+        in_refs, out_ref = refs[:-2], refs[-2]
     chan_count = len(in_refs)
     _, per, k2_count, _ = in_refs[0].shape
     pitch = per * chan_count + 1
@@ -414,65 +418,67 @@
         base = pl.multiple_of(k2 * per, per)
         for e in range(per):
             rows = pl.ds(k2 * pitch + e * chan_count, chan_count)
-            out_ref[0, base + e] = wide_ref[rows, :].astype(jnp.bfloat16)
+            out_ref[base + e] = wide_ref[rows, :].astype(jnp.bfloat16)
         return carry
 
-    lax.fori_loop(0, k2_count, narrow, 0, unroll=2)
-
-    half, group = pl.program_id(0), group_ref[0]
-
-    @pl.when(half == 1 - group % 2)
-    def _():
-        near_ref[...] = out_ref[0]
-
-    @pl.when(half == 1 - group // 2)
-    def _():
-        across_ref[...] = out_ref[0]
-
-
-def turn(blocks, group_id):
+    lax.fori_loop(0, k2_count, narrow, 0, unroll=4)
+
+    if other:
+        group = group_ref[0]
+        same = group % 2 == group // 2
+
+        @pl.when(same)
+        def _():
+            near_ref[...] = across_ref[...]
+
+        @pl.when(jnp.logical_not(same))
+        def _():
+            near_ref[...] = out_ref[...]
+
+
+def turn(blocks, group_id, across=None):
     chan_count = len(blocks)
-    halves, per, k2_count, lanes = blocks[0].shape
+    _, per, k2_count, lanes = blocks[0].shape
     one_half = (per * k2_count, chan_count, lanes)
-    return pl.pallas_call(
-        turn_kernel,
-        out_shape=[
-            jax.ShapeDtypeStruct((halves,) + one_half, jnp.bfloat16),
-            jax.ShapeDtypeStruct(one_half, jnp.bfloat16),
-            jax.ShapeDtypeStruct(one_half, jnp.bfloat16),
-        ],
+    other = across is not None
+    whole = pl.BlockSpec(one_half, lambda u, g: (0, 0, 0))
+
+    def half_at(u, group):
+        upper = group[0] // 2
+        return upper if other else 1 - upper, 0, 0, 0
+
+    results = pl.pallas_call(
+        functools.partial(turn_kernel, other),
+        out_shape=[jax.ShapeDtypeStruct(one_half, jnp.bfloat16)] * (1 + other),
         grid_spec=pltpu.PrefetchScalarGridSpec(
             num_scalar_prefetch=1,
-            grid=(halves,),
-            in_specs=[pl.BlockSpec((1, per, k2_count, lanes), lambda u, g: (u, 0, 0, 0))]
-            * chan_count,
-            out_specs=[
-                pl.BlockSpec((1,) + one_half, lambda u, g: (u, 0, 0, 0)),
-                pl.BlockSpec(one_half, lambda u, g: (0, 0, 0)),
-                pl.BlockSpec(one_half, lambda u, g: (0, 0, 0)),
-            ],
+            grid=(1,),
+            in_specs=[pl.BlockSpec((1, per, k2_count, lanes), half_at)] * chan_count
+            + [whole] * other,
+            out_specs=[whole] * (1 + other),
             scratch_shapes=[pltpu.VMEM((k2_count * (per * chan_count + 1), lanes), jnp.float32)],
         ),
         compiler_params=pltpu.CompilerParams(vmem_limit_bytes=VMEM_LIMIT),
         name="turn",
-    )(group_id, *blocks)
-
-
-def left_kernel(*refs):
-    chunk_refs, out_ref = refs[:-1], refs[-1]
-    _, channels, _, lanes = chunk_refs[0].shape
+    )(group_id, *blocks, *([across] if other else []))
+    return results if other else results[0]
+
+
+def left_kernel(chunk_count, *refs):
+    out_ref = refs[-1]
+    channels, _, lanes = refs[0].shape
     sig_count = lanes // 2
-    together = 2 * lanes // out_ref.shape[3]
     width = out_ref.shape[3]
+    together = 2 * lanes // width
     count = channels // out_ref.shape[1]
     row = lax.broadcasted_iota(jnp.int32, (sig_count, lanes), 0)
     column = lax.broadcasted_iota(jnp.int32, (sig_count, lanes), 1)
     identity = (row == column).astype(jnp.bfloat16)
 
-    def some_pairs(step, carry):
+    def some_entries(chunk_refs, step, carry):
         rows = []
         for i in range(count * together):
-            values = [ref[0, count * together * step + i].astype(jnp.float32) for ref in chunk_refs]
+            values = [ref[count * together * step + i].astype(jnp.float32) for ref in chunk_refs]
             rows += values + [pltpu.roll(value, sig_count, 1) for value in values]
         stacked = jnp.concatenate(rows, axis=0).astype(jnp.bfloat16)
         turned = lax.dot_general(
@@ -484,24 +490,40 @@
             )
         return carry
 
-    lax.fori_loop(0, channels // (count * together), some_pairs, 0, unroll=16)
-
-
-def left_operand(chunks):
-    halves, channels, chan_count, lanes = chunks[0].shape
-    depth = 2 * len(chunks) * chan_count
+    for half in range((len(refs) - 1) // chunk_count):
+
+        @pl.when(pl.program_id(0) == half)
+        def _():
+            chunk_refs = refs[half * chunk_count : (half + 1) * chunk_count]
+            steps = channels // (count * together)
+            lax.fori_loop(0, steps, functools.partial(some_entries, chunk_refs), 0, unroll=16)
+
+
+def left_operand(halves):
+    chunk_count = len(halves[0])
+    channels, chan_count, lanes = halves[0][0].shape
+    depth = 2 * chunk_count * chan_count
     count = lanes // depth
     tile = 128
+    last = channels // tile - 1
+
+    def spec(half):
+        def index(u, i):
+            return jnp.where(u == half, i, jnp.where(u < half, 0, last)), 0, 0
+
+        return pl.BlockSpec((tile, chan_count, lanes), index)
+
     return pl.pallas_call(
-        left_kernel,
-        out_shape=jax.ShapeDtypeStruct((halves, channels // count, lanes // 2, lanes), jnp.bfloat16),
-        grid=(halves, channels // tile),
-        in_specs=[pl.BlockSpec((1, tile, chan_count, lanes), lambda u, i: (u, i, 0, 0))]
-        * len(chunks),
+        functools.partial(left_kernel, chunk_count),
+        out_shape=jax.ShapeDtypeStruct(
+            (len(halves), channels // count, lanes // 2, lanes), jnp.bfloat16
+        ),
+        grid=(len(halves), channels // tile),
+        in_specs=[spec(half) for half, chunks in enumerate(halves) for _ in chunks],
         out_specs=pl.BlockSpec((1, tile // count, lanes // 2, lanes), lambda u, i: (u, i, 0, 0)),
         compiler_params=pltpu.CompilerParams(vmem_limit_bytes=VMEM_LIMIT),
         name="left_operand",
-    )(*chunks)
+    )(*[chunk for chunks in halves for chunk in chunks])
 
 
 def correlate_kernel(chunk_count, spec_count, group_ref, plan_ref, left_ref, *refs):
@@ -562,7 +584,9 @@
     tile = 128
 
     def half_of(group):
-        return (group[0] > (group[0] ^ distance)).astype(jnp.int32)
+        if distance > 1:
+            return 0
+        return jnp.where(group[0] % 2 == group[0] // 2, 0, 1)
 
     def round_of(group, plan):
         mate = group[0] ^ distance
@@ -677,7 +701,7 @@
     def to_mate(value, distance):
         return lax.ppermute(value, "grp", [(g, g ^ distance) for g in range(group_count)])
 
-    turned, near, across = [], [], []
+    own, near, across, across_own = [], [], [], []
     channels = []
     chunks = spec_count // chan_count
     for chunk in range(chunks):
@@ -694,11 +718,13 @@
         blocks = transform_by_pair(blocks, chan_id)
         channels.append(over_chan(blocks))
     for channel in channels:
-        halves, for_near, for_across = turn(channel, group_id)
-        turned.append(halves)
-        near = near + [to_mate(for_near, 1)]
-        across = across + [to_mate(for_across, 2)]
-    left = left_operand(turned)
+        for_across = turn(channel, group_id)
+        across.append(to_mate(for_across, 2))
+        kept, for_near = turn(channel, group_id, for_across)
+        near.append(to_mate(for_near, 1))
+        across_own.append(for_across)
+        own.append(kept)
+    left = left_operand([own, across_own])
     result = correlate(left, near, group_id, plan, 1, spec_count, None)
     across, result = lax.optimization_barrier((across, result))
     relayed = [to_mate(value, 1) for value in across]

time: 159 us -> 149 us (0.937)
  waiting for transfers between devices: 50.6 us -> 27.5 us
  starting transfers between devices: 53.6 us -> 62.9 us
  Pallas kernels: 51.8 us -> 55.4 us
    ppermute x28, waiting for transfers between devices: 37 us -> 13.9 us  [over_chan(): lax.ppermute(blocks[pair], 'chan', [(c, c ^ pair) for c in range(chan_cou...]
    ppermute x28, starting transfers between devices: 50.9 us -> 60.4 us  [over_chan(): lax.ppermute(blocks[pair], 'chan', [(c, c ^ pair) for c in range(chan_cou...]
    pallas_call x3 -> x5, Pallas kernels: 10.5 us -> 14.2 us  [the longest x4 9.23 us: turn(): pl.pallas_call(functools.partial(turn_kernel, other), out_shape=[jax.Shap...]
  transfers between devices with their start and end apart: 34 -> 34, of which waited for: 10 -> 8; matrix products, arithmetic and copies ran while one was open for 0% -> 0% of each run, Pallas kernels for 27% -> 32%
where the time goes in v8:
time: 149 us; the launch traced here: 146 us
  starting transfers between devices  62.9 us (42%)
  Pallas kernels  55.4 us (37%)
  waiting for transfers between devices  27.5 us (18%)
    ppermute x28, starting transfers between devices, over_chan(): lax.ppermute(blocks[pair], 'chan', [(c, c ^ pair) for c in range(chan_cou...  60.4 us
    pallas_call x3, Pallas kernels, correlate(): pl.pallas_call(functools.partial(correlate_kernel, len(chunks), spec_coun...  15.9 us
    ppermute x28, waiting for transfers between devices, over_chan(): lax.ppermute(blocks[pair], 'chan', [(c, c ^ pair) for c in range(chan_cou...  13.9 us
    ppermute x6, waiting for transfers between devices, to_mate(): lax.ppermute(value, 'grp', [(g, g ^ distance) for g in range(group_count)])  13.6 us
    pallas_call x3, Pallas kernels, filter_by_pair(): pl.pallas_call(functools.partial(filter_by_pair_kernel, pairs), out_shape...  13.3 us
    pallas_call x2, Pallas kernels, transform_by_pair(): pl.pallas_call(functools.partial(transform_by_pair_kernel, chan_count), o...  12 us
    pallas_call x4, Pallas kernels, turn(): pl.pallas_call(functools.partial(turn_kernel, other), out_shape=[jax.Shap...  9.23 us
    pallas_call x1, Pallas kernels, left_operand(): pl.pallas_call(functools.partial(left_kernel, chunk_count), out_shape=jax...  4.96 us
  transfers between devices with their start and end apart: 34, of which 8 were waited for; matrix products, arithmetic and copies ran while one was open for 0% of the time, Pallas kernels for 32%

profile of v8, /device:TPU:0, one launch (start us, length us, event | category | flops | bytes accessed | tf_op | source)
XLA Modules:
  0.0 145.9 jit_solution(14490474866644067615)
XLA Ops:
  0.0 4.0 %filter_by_pair.4 = (bf16[64,1024]{1,0:T(8,128)(2,1)}, bf16[64,1024]{1,0:T(8,128)(2,1)}, bf16[64,1024]{1,0:T(8,128)(2,1)}, bf16[64,1024]{1,0:T(8,128)(2,1)}) custom-call(s32[1]{0:T(128)} %bitcast.1.chan_ref.refs_0_, s32[31,64,1024]{2,1,0:T(8,128)} %bitcast.3, f32[8,16,1024]{2,1,0:T(8,128)} %constant.18.clone.coeff_ref), custom_call_target="tpu_custom_call" | custom-call | tf_op jit(solution)/shard_map/filter_by_pair/pallas_call | solution.py:99
  4.0 4.1 %collective-permute-start.3 = (bf16[64,1024]{1,0:T(8,128)(2,1)}, bf16[64,1024]{1,0:T(8,128)(2,1)}, u32[]{:S(2)}, u32[]{:S(2)}) collective-permute-start(bf16[64,1024]{1,0:T(8,128)(2,1)} %get-tuple-element.48), channel_id=1, source_target_pairs={{0,4},{1,5},{2,6},{3,7},{4,0},{5,1},{6,2},{7,3},{8,12},{9,13},{10,... | collective-permute-start | bytes 393224 | tf_op jit(solution)/shard_map/ppermute | solution.py:696
  9.3 3.6 %collective-permute-start.5 = (bf16[64,1024]{1,0:T(8,128)(2,1)}, bf16[64,1024]{1,0:T(8,128)(2,1)}, u32[]{:S(2)}, u32[]{:S(2)}) collective-permute-start(bf16[64,1024]{1,0:T(8,128)(2,1)} %get-tuple-element.50), channel_id=1, source_target_pairs={{0,6},{1,7},{2,4},{3,5},{4,2},{5,3},{6,0},{7,1},{8,14},{9,15},{10,... | collective-permute-start | bytes 393224 | tf_op jit(solution)/shard_map/ppermute | solution.py:696
  12.9 4.0 %filter_by_pair.3 = (bf16[64,1024]{1,0:T(8,128)(2,1)}, bf16[64,1024]{1,0:T(8,128)(2,1)}, bf16[64,1024]{1,0:T(8,128)(2,1)}, bf16[64,1024]{1,0:T(8,128)(2,1)}) custom-call(s32[1]{0:T(128)} %bitcast.1.chan_ref.refs_0_, s32[31,64,1024]{2,1,0:T(8,128)} %bitcast.4, f32[8,16,1024]{2,1,0:T(8,128)} %constant.18.clone.coeff_ref), custom_call_target="tpu_custom_call" | custom-call | tf_op jit(solution)/shard_map/filter_by_pair/pallas_call | solution.py:99
  18.5 5.3 %filter_by_pair.5 = (bf16[64,1024]{1,0:T(8,128)(2,1)}, bf16[64,1024]{1,0:T(8,128)(2,1)}, bf16[64,1024]{1,0:T(8,128)(2,1)}, bf16[64,1024]{1,0:T(8,128)(2,1)}, bf1...) custom-call(s32[1]{0:T(128)} %bitcast.1.chan_ref.refs_0_, ...), custom_call_target="tpu_custom_call" | custom-call | tf_op jit(solution)/shard_map/filter_by_pair/pallas_call | solution.py:99
  24.0 4.0 %collective-permute-done.4.refs_10_ = bf16[64,1024]{1,0:T(8,128)(2,1)} collective-permute-done((bf16[64,1024]{1,0:T(8,128)(2,1)}, bf16[64,1024]{1,0:T(8,128)(2,1)}, u32[]{:S(2)}, u32[]{:S(2)}) %collective-permute-start.4) | collective-permute-done | bytes 131104 | tf_op jit(solution)/shard_map/ppermute | solution.py:696
  28.2 6.9 %collective-permute-start.15 = (bf16[64,1024]{1,0:T(8,128)(2,1)}, bf16[64,1024]{1,0:T(8,128)(2,1)}, u32[]{:S(2)}, u32[]{:S(2)}) collective-permute-start(bf16[64,1024]{1,0:T(8,128)(2,1)} %get-tuple-element.63), channel_id=1, source_target_pairs={{0,2},{1,3},{2,0},{3,1},{4,6},{5,7},{6,4},{7,5},{8,10},{9,11},{10,... | collective-permute-start | bytes 393224 | tf_op jit(solution)/shard_map/ppermute | solution.py:696
  35.1 4.1 %collective-permute-start.17 = (bf16[64,1024]{1,0:T(8,128)(2,1)}, bf16[64,1024]{1,0:T(8,128)(2,1)}, u32[]{:S(2)}, u32[]{:S(2)}) collective-permute-start(bf16[64,1024]{1,0:T(8,128)(2,1)} %get-tuple-element.65), channel_id=1, source_target_pairs={{0,4},{1,5},{2,6},{3,7},{4,0},{5,1},{6,2},{7,3},{8,12},{9,13},{10,... | collective-permute-start | bytes 393224 | tf_op jit(solution)/shard_map/ppermute | solution.py:696
  44.7 6.1 %transform_by_pair.2 = (bf16[2,8,32,128]{3,2,1,0:T(8,128)(2,1)}, bf16[2,8,32,128]{3,2,1,0:T(8,128)(2,1)}, bf16[2,8,32,128]{3,2,1,0:T(8,128)(2,1)}, bf16[2,8,32,1...) custom-call(s32[1]{0:T(128)} %bitcast.1.chan_ref.refs_0_, ...), custom_call_target="tpu_custom_call" | custom-call | tf_op jit(solution)/shard_map/transform_by_pair/pallas_call | solution.py:381
  54.8 4.7 %collective-permute-done.18.refs_10_ = bf16[64,1024]{1,0:T(8,128)(2,1)} collective-permute-done((bf16[64,1024]{1,0:T(8,128)(2,1)}, bf16[64,1024]{1,0:T(8,128)(2,1)}, u32[]{:S(2)}, u32[]{:S(2)}) %collective-permute-start.18) | collective-permute-done | bytes 131104 | tf_op jit(solution)/shard_map/ppermute | solution.py:696
  59.5 2.8 %collective-permute-start.10 = (bf16[2,8,32,128]{3,2,1,0:T(8,128)(2,1)}, bf16[2,8,32,128]{3,2,1,0:T(8,128)(2,1)}, u32[]{:S(2)}, u32[]{:S(2)}) collective-permute-start(bf16[2,8,32,128]{3,2,1,0:T(8,128)(2,1)} %get-tuple-element.56), channel_id=1, source_target_pairs={{0,4},{1,5},{2,6},{3,7},{4,0},{5,1},{6,2},{7,3},{8,12},{9,13},{10,... | collective-permute-start | bytes 393224 | tf_op jit(solution)/shard_map/ppermute | solution.py:696
  62.3 4.9 %collective-permute-start.11 = (bf16[2,8,32,128]{3,2,1,0:T(8,128)(2,1)}, bf16[2,8,32,128]{3,2,1,0:T(8,128)(2,1)}, u32[]{:S(2)}, u32[]{:S(2)}) collective-permute-start(bf16[2,8,32,128]{3,2,1,0:T(8,128)(2,1)} %get-tuple-element.57), channel_id=1, source_target_pairs={{0,5},{1,4},{2,7},{3,6},{4,1},{5,0},{6,3},{7,2},{8,13},{9,12},{10,... | collective-permute-start | bytes 393224 | tf_op jit(solution)/shard_map/ppermute | solution.py:696
  67.2 6.0 %transform_by_pair.3 = (bf16[2,8,32,128]{3,2,1,0:T(8,128)(2,1)}, bf16[2,8,32,128]{3,2,1,0:T(8,128)(2,1)}, bf16[2,8,32,128]{3,2,1,0:T(8,128)(2,1)}, bf16[2,8,32,1...) custom-call(s32[1]{0:T(128)} %bitcast.1.chan_ref.refs_0_, ...), custom_call_target="tpu_custom_call" | custom-call | tf_op jit(solution)/shard_map/transform_by_pair/pallas_call | solution.py:381
  75.9 2.7 %collective-permute-start.13 = (bf16[2,8,32,128]{3,2,1,0:T(8,128)(2,1)}, bf16[2,8,32,128]{3,2,1,0:T(8,128)(2,1)}, u32[]{:S(2)}, u32[]{:S(2)}) collective-permute-start(bf16[2,8,32,128]{3,2,1,0:T(8,128)(2,1)} %get-tuple-element.59), channel_id=1, source_target_pairs={{0,7},{1,6},{2,5},{3,4},{4,3},{5,2},{6,1},{7,0},{8,15},{9,14},{10,... | collective-permute-start | bytes 393224 | tf_op jit(solution)/shard_map/ppermute | solution.py:696
  79.1 3.0 %collective-permute-start.23 = (bf16[2,8,32,128]{3,2,1,0:T(8,128)(2,1)}, bf16[2,8,32,128]{3,2,1,0:T(8,128)(2,1)}, u32[]{:S(2)}, u32[]{:S(2)}) collective-permute-start(bf16[2,8,32,128]{3,2,1,0:T(8,128)(2,1)} %get-tuple-element.72), channel_id=1, source_target_pairs={{0,3},{1,2},{2,1},{3,0},{4,7},{5,6},{6,5},{7,4},{8,11},{9,10},{10,... | collective-permute-start | bytes 393224 | tf_op jit(solution)/shard_map/ppermute | solution.py:696
  82.1 3.1 %collective-permute-start.24 = (bf16[2,8,32,128]{3,2,1,0:T(8,128)(2,1)}, bf16[2,8,32,128]{3,2,1,0:T(8,128)(2,1)}, u32[]{:S(2)}, u32[]{:S(2)}) collective-permute-start(bf16[2,8,32,128]{3,2,1,0:T(8,128)(2,1)} %get-tuple-element.73), channel_id=1, source_target_pairs={{0,4},{1,5},{2,6},{3,7},{4,0},{5,1},{6,2},{7,3},{8,12},{9,13},{10,... | collective-permute-start | bytes 393224 | tf_op jit(solution)/shard_map/ppermute | solution.py:696
  85.2 5.3 %collective-permute-start.25 = (bf16[2,8,32,128]{3,2,1,0:T(8,128)(2,1)}, bf16[2,8,32,128]{3,2,1,0:T(8,128)(2,1)}, u32[]{:S(2)}, u32[]{:S(2)}) collective-permute-start(bf16[2,8,32,128]{3,2,1,0:T(8,128)(2,1)} %get-tuple-element.74), channel_id=1, source_target_pairs={{0,5},{1,4},{2,7},{3,6},{4,1},{5,0},{6,3},{7,2},{8,13},{9,12},{10,... | collective-permute-start | bytes 393224 | tf_op jit(solution)/shard_map/ppermute | solution.py:696
  100.6 3.7 %collective-permute-done.25.refs_5_ = bf16[2,8,32,128]{3,2,1,0:T(8,128)(2,1)} collective-permute-done((bf16[2,8,32,128]{3,2,1,0:T(8,128)(2,1)}, bf16[2,8,32,128]{3,2,1,0:T(8,128)(2,1)}, u32[]{:S(2)}, u32[]{:S(2)}) %collective-permute-start.25) | collective-permute-done | bytes 131104 | tf_op jit(solution)/shard_map/ppermute | solution.py:696
  110.9 5.0 %left_operand.1.left_ref = bf16[2,64,64,128]{3,2,1,0:T(8,128)(2,1)} custom-call(bf16[256,8,128]{2,1,0:T(8,128)(2,1)} %get-tuple-element.60.refs_0_, bf16[256,8,128]{2,1,0:T(8,128)(2,1)} %get-tuple-element.77.refs_1_, bf16[256,8,128]{2,1,0:T(8,128)(2,1)} %turn.4.refs_8_.refs_2_, bf16[256,8,128]{2,1,0:T(8,128)(2,1)} %turn.6.refs_8_.refs_3_), custom_call_target="tpu_custom_call" | custom-call | tf_op jit(solution)/shard_map/left_operand/pallas_call | solution.py:516
  115.9 5.3 %correlate.3.refs_2_ = bf16[3,64,256,128]{3,2,1,0:T(8,128)(2,1)} custom-call(s32[1]{0:T(128)} %bitcast.group_ref, s32[3,4]{1,0:T(4,128)} %plan_ref.5, bf16[2,64,64,128]{3,2,1,0:T(8,128)(2,1)} %left_operand.1.left_ref, bf16[256,8,128]{2,1,0:T(8,128)(2,1)} %collective-permute-done.30.refs_0_, bf16[256,8,128]{2,1,0:T(8,128)(2,1)} %collective-permute-done.31.refs_1_), custom_call_target="tpu_custom_call" | custom-call | flops 536870912 | bytes 16777216 | tf_op jit(solution)/shard_map/correlate/pallas_call | solution.py:607
  121.2 2.8 %collective-permute-done.28.refs_0_ = bf16[256,8,128]{2,1,0:T(8,128)(2,1)} collective-permute-done((bf16[256,8,128]{2,1,0:T(8,128)(2,1)}, bf16[256,8,128]{2,1,0:T(8,128)(2,1)}, u32[]{:S(2)}, u32[]{:S(2)}) %collective-permute-start.28) | collective-permute-done | bytes 524320 | tf_op jit(solution)/shard_map/ppermute | solution.py:702
  124.0 10.8 %collective-permute-done.29.refs_1_ = bf16[256,8,128]{2,1,0:T(8,128)(2,1)} collective-permute-done((bf16[256,8,128]{2,1,0:T(8,128)(2,1)}, bf16[256,8,128]{2,1,0:T(8,128)(2,1)}, u32[]{:S(2)}, u32[]{:S(2)}) %collective-permute-start.29) | collective-permute-done | bytes 524320 | tf_op jit(solution)/shard_map/ppermute | solution.py:702
  135.3 5.3 %correlate.4.refs_2_ = bf16[3,64,256,128]{3,2,1,0:T(8,128)(2,1)} custom-call(s32[1]{0:T(128)} %bitcast.group_ref, s32[3,4]{1,0:T(4,128)} %plan_ref.5, bf16[2,64,64,128]{3,2,1,0:T(8,128)(2,1)} %left_operand.1.left_ref, bf16[256,8,128]{2,1,0:T(8,128)(2,1)} %collective-permute-done.28.refs_0_, ...), custom_call_target="tpu_custom_call", output_to_operand_aliasing={{}: (5, {})} | custom-call | flops 536870912 | bytes 16777216 | tf_op jit(solution)/shard_map/correlate/pallas_call | solution.py:607
  140.6 5.3 %correlate.5 = bf16[3,64,256,128]{3,2,1,0:T(8,128)(2,1)} custom-call(s32[1]{0:T(128)} %bitcast.group_ref, s32[3,4]{1,0:T(4,128)} %plan_ref.5, bf16[2,64,64,128]{3,2,1,0:T(8,128)(2,1)} %left_operand.1.left_ref, bf16[256,8,128]{2,1,0:T(8,128)(2,1)} %collective-permute-done.32.refs_0_, ...), custom_call_target="tpu_custom_call", output_to_operand_aliasing={{}: (5, {})} | custom-call | flops 536870912 | bytes 16777216 | tf_op jit(solution)/shard_map/correlate/pallas_call | solution.py:607
  (57 shorter events, 33.1 us)
Async XLA Ops:
  4.0 20.0 %collective-permute-start.3 = (bf16[64,1024]{1,0:T(8,128)(2,1)}, bf16[64,1024]{1,0:T(8,128)(2,1)}, u32[]{:S(2)}, u32[]{:S(2)}) collective-permute-start(bf16[64,1024]{1,0:T(8,128)(2,1)} %get-tuple-element.48), channel_id=1, source_target_pairs={{0,4},{1,5},{2,6},{3,7},{4,0},{5,1},{6,2},{7,3},{8,12},{9,13},{10,... | collective-permute-start | bytes 393224 | tf_op jit(solution)/shard_map/ppermute | solution.py:696
  8.0 20.0 %collective-permute-start.4 = (bf16[64,1024]{1,0:T(8,128)(2,1)}, bf16[64,1024]{1,0:T(8,128)(2,1)}, u32[]{:S(2)}, u32[]{:S(2)}) collective-permute-start(bf16[64,1024]{1,0:T(8,128)(2,1)} %get-tuple-element.49), channel_id=1, source_target_pairs={{0,5},{1,4},{2,7},{3,6},{4,1},{5,0},{6,3},{7,2},{8,13},{9,12},{10,... | collective-permute-start | bytes 393224 | tf_op jit(solution)/shard_map/ppermute | solution.py:696
  9.3 18.7 %collective-permute-start.5 = (bf16[64,1024]{1,0:T(8,128)(2,1)}, bf16[64,1024]{1,0:T(8,128)(2,1)}, u32[]{:S(2)}, u32[]{:S(2)}) collective-permute-start(bf16[64,1024]{1,0:T(8,128)(2,1)} %get-tuple-element.50), channel_id=1, source_target_pairs={{0,6},{1,7},{2,4},{3,5},{4,2},{5,3},{6,0},{7,1},{8,14},{9,15},{10,... | collective-permute-start | bytes 393224 | tf_op jit(solution)/shard_map/ppermute | solution.py:696
  12.9 15.3 %collective-permute-start.6 = (bf16[64,1024]{1,0:T(8,128)(2,1)}, bf16[64,1024]{1,0:T(8,128)(2,1)}, u32[]{:S(2)}, u32[]{:S(2)}) collective-permute-start(bf16[64,1024]{1,0:T(8,128)(2,1)} %get-tuple-element.51), channel_id=1, source_target_pairs={{0,7},{1,6},{2,5},{3,4},{4,3},{5,2},{6,1},{7,0},{8,15},{9,14},{10,... | collective-permute-start | bytes 393224 | tf_op jit(solution)/shard_map/ppermute | solution.py:696
  16.9 18.2 %collective-permute-start = (bf16[64,1024]{1,0:T(8,128)(2,1)}, bf16[64,1024]{1,0:T(8,128)(2,1)}, u32[]{:S(2)}, u32[]{:S(2)}) collective-permute-start(bf16[64,1024]{1,0:T(8,128)(2,1)} %get-tuple-element.45), channel_id=1, source_target_pairs={{0,1},{1,0},{2,3},{3,2},{4,5},{5,4},{6,7},{7,6},{8,9},{9,8},{10,11... | collective-permute-start | bytes 393224 | tf_op jit(solution)/shard_map/ppermute | solution.py:696
  28.2 14.9 %collective-permute-start.15 = (bf16[64,1024]{1,0:T(8,128)(2,1)}, bf16[64,1024]{1,0:T(8,128)(2,1)}, u32[]{:S(2)}, u32[]{:S(2)}) collective-permute-start(bf16[64,1024]{1,0:T(8,128)(2,1)} %get-tuple-element.63), channel_id=1, source_target_pairs={{0,2},{1,3},{2,0},{3,1},{4,6},{5,7},{6,4},{7,5},{8,10},{9,11},{10,... | collective-permute-start | bytes 393224 | tf_op jit(solution)/shard_map/ppermute | solution.py:696
  35.1 15.6 %collective-permute-start.16 = (bf16[64,1024]{1,0:T(8,128)(2,1)}, bf16[64,1024]{1,0:T(8,128)(2,1)}, u32[]{:S(2)}, u32[]{:S(2)}) collective-permute-start(bf16[64,1024]{1,0:T(8,128)(2,1)} %get-tuple-element.64), channel_id=1, source_target_pairs={{0,3},{1,2},{2,1},{3,0},{4,7},{5,6},{6,5},{7,4},{8,11},{9,10},{10,... | collective-permute-start | bytes 393224 | tf_op jit(solution)/shard_map/ppermute | solution.py:696
  35.1 17.8 %collective-permute-start.17 = (bf16[64,1024]{1,0:T(8,128)(2,1)}, bf16[64,1024]{1,0:T(8,128)(2,1)}, u32[]{:S(2)}, u32[]{:S(2)}) collective-permute-start(bf16[64,1024]{1,0:T(8,128)(2,1)} %get-tuple-element.65), channel_id=1, source_target_pairs={{0,4},{1,5},{2,6},{3,7},{4,0},{5,1},{6,2},{7,3},{8,12},{9,13},{10,... | collective-permute-start | bytes 393224 | tf_op jit(solution)/shard_map/ppermute | solution.py:696
  39.2 20.3 %collective-permute-start.18 = (bf16[64,1024]{1,0:T(8,128)(2,1)}, bf16[64,1024]{1,0:T(8,128)(2,1)}, u32[]{:S(2)}, u32[]{:S(2)}) collective-permute-start(bf16[64,1024]{1,0:T(8,128)(2,1)} %get-tuple-element.66), channel_id=1, source_target_pairs={{0,5},{1,4},{2,7},{3,6},{4,1},{5,0},{6,3},{7,2},{8,13},{9,12},{10,... | collective-permute-start | bytes 393224 | tf_op jit(solution)/shard_map/ppermute | solution.py:696
  40.8 18.6 %collective-permute-start.19 = (bf16[64,1024]{1,0:T(8,128)(2,1)}, bf16[64,1024]{1,0:T(8,128)(2,1)}, u32[]{:S(2)}, u32[]{:S(2)}) collective-permute-start(bf16[64,1024]{1,0:T(8,128)(2,1)} %get-tuple-element.67), channel_id=1, source_target_pairs={{0,6},{1,7},{2,4},{3,5},{4,2},{5,3},{6,0},{7,1},{8,14},{9,15},{10,... | collective-permute-start | bytes 393224 | tf_op jit(solution)/shard_map/ppermute | solution.py:696
  43.1 19.2 %collective-permute-start.20 = (bf16[64,1024]{1,0:T(8,128)(2,1)}, bf16[64,1024]{1,0:T(8,128)(2,1)}, u32[]{:S(2)}, u32[]{:S(2)}) collective-permute-start(bf16[64,1024]{1,0:T(8,128)(2,1)} %get-tuple-element.68), channel_id=1, source_target_pairs={{0,7},{1,6},{2,5},{3,4},{4,3},{5,2},{6,1},{7,0},{8,15},{9,14},{10,... | collective-permute-start | bytes 393224 | tf_op jit(solution)/shard_map/ppermute | solution.py:696
  50.7 22.5 %collective-permute-start.7 = (bf16[2,8,32,128]{3,2,1,0:T(8,128)(2,1)}, bf16[2,8,32,128]{3,2,1,0:T(8,128)(2,1)}, u32[]{:S(2)}, u32[]{:S(2)}) collective-permute-start(bf16[2,8,32,128]{3,2,1,0:T(8,128)(2,1)} %get-tuple-element.53), channel_id=1, source_target_pairs={{0,1},{1,0},{2,3},{3,2},{4,5},{5,4},{6,7},{7,6},{8,9},{9,8},{10,11... | collective-permute-start | bytes 393224 | tf_op jit(solution)/shard_map/ppermute | solution.py:696
  52.9 22.9 %collective-permute-start.8 = (bf16[2,8,32,128]{3,2,1,0:T(8,128)(2,1)}, bf16[2,8,32,128]{3,2,1,0:T(8,128)(2,1)}, u32[]{:S(2)}, u32[]{:S(2)}) collective-permute-start(bf16[2,8,32,128]{3,2,1,0:T(8,128)(2,1)} %get-tuple-element.54), channel_id=1, source_target_pairs={{0,2},{1,3},{2,0},{3,1},{4,6},{5,7},{6,4},{7,5},{8,10},{9,11},{10,... | collective-permute-start | bytes 393224 | tf_op jit(solution)/shard_map/ppermute | solution.py:696
  59.5 19.2 %collective-permute-start.9 = (bf16[2,8,32,128]{3,2,1,0:T(8,128)(2,1)}, bf16[2,8,32,128]{3,2,1,0:T(8,128)(2,1)}, u32[]{:S(2)}, u32[]{:S(2)}) collective-permute-start(bf16[2,8,32,128]{3,2,1,0:T(8,128)(2,1)} %get-tuple-element.55), channel_id=1, source_target_pairs={{0,3},{1,2},{2,1},{3,0},{4,7},{5,6},{6,5},{7,4},{8,11},{9,10},{10,... | collective-permute-start | bytes 393224 | tf_op jit(solution)/shard_map/ppermute | solution.py:696
  59.5 19.2 %collective-permute-start.10 = (bf16[2,8,32,128]{3,2,1,0:T(8,128)(2,1)}, bf16[2,8,32,128]{3,2,1,0:T(8,128)(2,1)}, u32[]{:S(2)}, u32[]{:S(2)}) collective-permute-start(bf16[2,8,32,128]{3,2,1,0:T(8,128)(2,1)} %get-tuple-element.56), channel_id=1, source_target_pairs={{0,4},{1,5},{2,6},{3,7},{4,0},{5,1},{6,2},{7,3},{8,12},{9,13},{10,... | collective-permute-start | bytes 393224 | tf_op jit(solution)/shard_map/ppermute | solution.py:696
  62.3 16.8 %collective-permute-start.11 = (bf16[2,8,32,128]{3,2,1,0:T(8,128)(2,1)}, bf16[2,8,32,128]{3,2,1,0:T(8,128)(2,1)}, u32[]{:S(2)}, u32[]{:S(2)}) collective-permute-start(bf16[2,8,32,128]{3,2,1,0:T(8,128)(2,1)} %get-tuple-element.57), channel_id=1, source_target_pairs={{0,5},{1,4},{2,7},{3,6},{4,1},{5,0},{6,3},{7,2},{8,13},{9,12},{10,... | collective-permute-start | bytes 393224 | tf_op jit(solution)/shard_map/ppermute | solution.py:696
  78.6 14.0 %collective-permute-start.22 = (bf16[2,8,32,128]{3,2,1,0:T(8,128)(2,1)}, bf16[2,8,32,128]{3,2,1,0:T(8,128)(2,1)}, u32[]{:S(2)}, u32[]{:S(2)}) collective-permute-start(bf16[2,8,32,128]{3,2,1,0:T(8,128)(2,1)} %get-tuple-element.71), channel_id=1, source_target_pairs={{0,2},{1,3},{2,0},{3,1},{4,6},{5,7},{6,4},{7,5},{8,10},{9,11},{10,... | collective-permute-start | bytes 393224 | tf_op jit(solution)/shard_map/ppermute | solution.py:696
  79.1 20.5 %collective-permute-start.23 = (bf16[2,8,32,128]{3,2,1,0:T(8,128)(2,1)}, bf16[2,8,32,128]{3,2,1,0:T(8,128)(2,1)}, u32[]{:S(2)}, u32[]{:S(2)}) collective-permute-start(bf16[2,8,32,128]{3,2,1,0:T(8,128)(2,1)} %get-tuple-element.72), channel_id=1, source_target_pairs={{0,3},{1,2},{2,1},{3,0},{4,7},{5,6},{6,5},{7,4},{8,11},{9,10},{10,... | collective-permute-start | bytes 393224 | tf_op jit(solution)/shard_map/ppermute | solution.py:696
  82.1 18.5 %collective-permute-start.24 = (bf16[2,8,32,128]{3,2,1,0:T(8,128)(2,1)}, bf16[2,8,32,128]{3,2,1,0:T(8,128)(2,1)}, u32[]{:S(2)}, u32[]{:S(2)}) collective-permute-start(bf16[2,8,32,128]{3,2,1,0:T(8,128)(2,1)} %get-tuple-element.73), channel_id=1, source_target_pairs={{0,4},{1,5},{2,6},{3,7},{4,0},{5,1},{6,2},{7,3},{8,12},{9,13},{10,... | collective-permute-start | bytes 393224 | tf_op jit(solution)/shard_map/ppermute | solution.py:696
  85.2 19.0 %collective-permute-start.25 = (bf16[2,8,32,128]{3,2,1,0:T(8,128)(2,1)}, bf16[2,8,32,128]{3,2,1,0:T(8,128)(2,1)}, u32[]{:S(2)}, u32[]{:S(2)}) collective-permute-start(bf16[2,8,32,128]{3,2,1,0:T(8,128)(2,1)} %get-tuple-element.74), channel_id=1, source_target_pairs={{0,5},{1,4},{2,7},{3,6},{4,1},{5,0},{6,3},{7,2},{8,13},{9,12},{10,... | collective-permute-start | bytes 393224 | tf_op jit(solution)/shard_map/ppermute | solution.py:696
  90.5 13.7 %collective-permute-start.26 = (bf16[2,8,32,128]{3,2,1,0:T(8,128)(2,1)}, bf16[2,8,32,128]{3,2,1,0:T(8,128)(2,1)}, u32[]{:S(2)}, u32[]{:S(2)}) collective-permute-start(bf16[2,8,32,128]{3,2,1,0:T(8,128)(2,1)} %get-tuple-element.75), channel_id=1, source_target_pairs={{0,6},{1,7},{2,4},{3,5},{4,2},{5,3},{6,0},{7,1},{8,14},{9,15},{10,... | collective-permute-start | bytes 393224 | tf_op jit(solution)/shard_map/ppermute | solution.py:696
  99.6 16.3 %collective-permute-start.30 = (bf16[256,8,128]{2,1,0:T(8,128)(2,1)}, bf16[256,8,128]{2,1,0:T(8,128)(2,1)}, u32[]{:S(2)}, u32[]{:S(2)}) collective-permute-start(bf16[256,8,128]{2,1,0:T(8,128)(2,1)} %get-tuple-element.78), channel_id=1, source_target_pairs={{0,8},{8,0},{16,24},{24,16},{1,9},{9,1},{17,25},{25,17},{2,10},{10... | collective-permute-start | bytes 1572872 | tf_op jit(solution)/shard_map/ppermute | solution.py:702
  108.9 15.1 %collective-permute-start.28 = (bf16[256,8,128]{2,1,0:T(8,128)(2,1)}, bf16[256,8,128]{2,1,0:T(8,128)(2,1)}, u32[]{:S(2)}, u32[]{:S(2)}) collective-permute-start(bf16[256,8,128]{2,1,0:T(8,128)(2,1)} %turn.4.refs_8_.refs_2_), channel_id=1, source_target_pairs={{0,16},{8,24},{16,0},{24,8},{1,17},{9,25},{17,1},{25,9},{2,18},{10... | collective-permute-start | bytes 1572872 | tf_op jit(solution)/shard_map/ppermute | solution.py:702
  110.4 24.4 %collective-permute-start.29 = (bf16[256,8,128]{2,1,0:T(8,128)(2,1)}, bf16[256,8,128]{2,1,0:T(8,128)(2,1)}, u32[]{:S(2)}, u32[]{:S(2)}) collective-permute-start(bf16[256,8,128]{2,1,0:T(8,128)(2,1)} %turn.6.refs_8_.refs_3_), channel_id=1, source_target_pairs={{0,16},{8,24},{16,0},{24,8},{1,17},{9,25},{17,1},{25,9},{2,18},{10... | collective-permute-start | bytes 1572872 | tf_op jit(solution)/shard_map/ppermute | solution.py:702
  (10 other events, 95.5 us)

commit v9 on v8

--- a/solution.py
+++ b/solution.py
@@ -273,9 +273,12 @@
         places = range(first, min(first + group, len(chosen)))
         high = high_ref[first : first + len(places)].reshape(len(places) * rows, 2 * LANES)
         low = low_ref[first : first + len(places)].reshape(len(places) * rows, 2 * LANES)
-        total = lax.dot_general(wave_high, high, dims, preferred_element_type=jnp.float32)
-        total += lax.dot_general(wave_high, low, dims, preferred_element_type=jnp.float32)
-        total += lax.dot_general(wave_low, high, dims, preferred_element_type=jnp.float32)
+        total = lax.dot_general(
+            jnp.concatenate([wave_high, wave_high, wave_low], axis=1),
+            jnp.concatenate([high, low, high], axis=1),
+            dims,
+            preferred_element_type=jnp.float32,
+        )
 
         def put(place, side, half, part, value):
             k1 = chosen[place]

time: 149 us -> 149 us (level)
  no operation moved by 1% of the time
where the time goes in v9:
time: 149 us; the launch traced here: 146 us
  starting transfers between devices  62.9 us (42%)
  Pallas kernels  55.4 us (37%)
  waiting for transfers between devices  27.5 us (18%)
    ppermute x28, starting transfers between devices, over_chan(): lax.ppermute(blocks[pair], 'chan', [(c, c ^ pair) for c in range(chan_cou...  60.4 us
    pallas_call x3, Pallas kernels, correlate(): pl.pallas_call(functools.partial(correlate_kernel, len(chunks), spec_coun...  15.9 us
    ppermute x28, waiting for transfers between devices, over_chan(): lax.ppermute(blocks[pair], 'chan', [(c, c ^ pair) for c in range(chan_cou...  13.9 us
    ppermute x6, waiting for transfers between devices, to_mate(): lax.ppermute(value, 'grp', [(g, g ^ distance) for g in range(group_count)])  13.6 us
    pallas_call x3, Pallas kernels, filter_by_pair(): pl.pallas_call(functools.partial(filter_by_pair_kernel, pairs), out_shape...  13.3 us
    pallas_call x2, Pallas kernels, transform_by_pair(): pl.pallas_call(functools.partial(transform_by_pair_kernel, chan_count), o...  12 us
    pallas_call x4, Pallas kernels, turn(): pl.pallas_call(functools.partial(turn_kernel, other), out_shape=[jax.Shap...  9.23 us
    pallas_call x1, Pallas kernels, left_operand(): pl.pallas_call(functools.partial(left_kernel, chunk_count), out_shape=jax...  4.96 us
  transfers between devices with their start and end apart: 34, of which 8 were waited for; matrix products, arithmetic and copies ran while one was open for 0% of the time, Pallas kernels for 32%

profile of v9, /device:TPU:0, one launch (start us, length us, event | category | flops | bytes accessed | tf_op | source)
XLA Modules:
  0.0 145.9 jit_solution(12042078743226407361)
XLA Ops:
  0.0 4.0 %filter_by_pair.4 = (bf16[64,1024]{1,0:T(8,128)(2,1)}, bf16[64,1024]{1,0:T(8,128)(2,1)}, bf16[64,1024]{1,0:T(8,128)(2,1)}, bf16[64,1024]{1,0:T(8,128)(2,1)}) custom-call(s32[1]{0:T(128)} %bitcast.1.chan_ref.refs_0_, s32[31,64,1024]{2,1,0:T(8,128)} %bitcast.3, f32[8,16,1024]{2,1,0:T(8,128)} %constant.18.clone.coeff_ref), custom_call_target="tpu_custom_call" | custom-call | tf_op jit(solution)/shard_map/filter_by_pair/pallas_call | solution.py:99
  4.0 4.1 %collective-permute-start.3 = (bf16[64,1024]{1,0:T(8,128)(2,1)}, bf16[64,1024]{1,0:T(8,128)(2,1)}, u32[]{:S(2)}, u32[]{:S(2)}) collective-permute-start(bf16[64,1024]{1,0:T(8,128)(2,1)} %get-tuple-element.48), channel_id=1, source_target_pairs={{0,4},{1,5},{2,6},{3,7},{4,0},{5,1},{6,2},{7,3},{8,12},{9,13},{10,... | collective-permute-start | bytes 393224 | tf_op jit(solution)/shard_map/ppermute | solution.py:699
  9.3 3.6 %collective-permute-start.5 = (bf16[64,1024]{1,0:T(8,128)(2,1)}, bf16[64,1024]{1,0:T(8,128)(2,1)}, u32[]{:S(2)}, u32[]{:S(2)}) collective-permute-start(bf16[64,1024]{1,0:T(8,128)(2,1)} %get-tuple-element.50), channel_id=1, source_target_pairs={{0,6},{1,7},{2,4},{3,5},{4,2},{5,3},{6,0},{7,1},{8,14},{9,15},{10,... | collective-permute-start | bytes 393224 | tf_op jit(solution)/shard_map/ppermute | solution.py:699
  12.9 4.0 %filter_by_pair.3 = (bf16[64,1024]{1,0:T(8,128)(2,1)}, bf16[64,1024]{1,0:T(8,128)(2,1)}, bf16[64,1024]{1,0:T(8,128)(2,1)}, bf16[64,1024]{1,0:T(8,128)(2,1)}) custom-call(s32[1]{0:T(128)} %bitcast.1.chan_ref.refs_0_, s32[31,64,1024]{2,1,0:T(8,128)} %bitcast.4, f32[8,16,1024]{2,1,0:T(8,128)} %constant.18.clone.coeff_ref), custom_call_target="tpu_custom_call" | custom-call | tf_op jit(solution)/shard_map/filter_by_pair/pallas_call | solution.py:99
  18.5 5.3 %filter_by_pair.5 = (bf16[64,1024]{1,0:T(8,128)(2,1)}, bf16[64,1024]{1,0:T(8,128)(2,1)}, bf16[64,1024]{1,0:T(8,128)(2,1)}, bf16[64,1024]{1,0:T(8,128)(2,1)}, bf1...) custom-call(s32[1]{0:T(128)} %bitcast.1.chan_ref.refs_0_, ...), custom_call_target="tpu_custom_call" | custom-call | tf_op jit(solution)/shard_map/filter_by_pair/pallas_call | solution.py:99
  24.0 4.0 %collective-permute-done.4.refs_10_ = bf16[64,1024]{1,0:T(8,128)(2,1)} collective-permute-done((bf16[64,1024]{1,0:T(8,128)(2,1)}, bf16[64,1024]{1,0:T(8,128)(2,1)}, u32[]{:S(2)}, u32[]{:S(2)}) %collective-permute-start.4) | collective-permute-done | bytes 131104 | tf_op jit(solution)/shard_map/ppermute | solution.py:699
  28.2 6.9 %collective-permute-start.15 = (bf16[64,1024]{1,0:T(8,128)(2,1)}, bf16[64,1024]{1,0:T(8,128)(2,1)}, u32[]{:S(2)}, u32[]{:S(2)}) collective-permute-start(bf16[64,1024]{1,0:T(8,128)(2,1)} %get-tuple-element.63), channel_id=1, source_target_pairs={{0,2},{1,3},{2,0},{3,1},{4,6},{5,7},{6,4},{7,5},{8,10},{9,11},{10,... | collective-permute-start | bytes 393224 | tf_op jit(solution)/shard_map/ppermute | solution.py:699
  35.1 4.1 %collective-permute-start.17 = (bf16[64,1024]{1,0:T(8,128)(2,1)}, bf16[64,1024]{1,0:T(8,128)(2,1)}, u32[]{:S(2)}, u32[]{:S(2)}) collective-permute-start(bf16[64,1024]{1,0:T(8,128)(2,1)} %get-tuple-element.65), channel_id=1, source_target_pairs={{0,4},{1,5},{2,6},{3,7},{4,0},{5,1},{6,2},{7,3},{8,12},{9,13},{10,... | collective-permute-start | bytes 393224 | tf_op jit(solution)/shard_map/ppermute | solution.py:699
  44.7 6.1 %transform_by_pair.2 = (bf16[2,8,32,128]{3,2,1,0:T(8,128)(2,1)}, bf16[2,8,32,128]{3,2,1,0:T(8,128)(2,1)}, bf16[2,8,32,128]{3,2,1,0:T(8,128)(2,1)}, bf16[2,8,32,1...) custom-call(s32[1]{0:T(128)} %bitcast.1.chan_ref.refs_0_, ...), custom_call_target="tpu_custom_call" | custom-call | tf_op jit(solution)/shard_map/transform_by_pair/pallas_call | solution.py:384
  54.8 4.7 %collective-permute-done.18.refs_10_ = bf16[64,1024]{1,0:T(8,128)(2,1)} collective-permute-done((bf16[64,1024]{1,0:T(8,128)(2,1)}, bf16[64,1024]{1,0:T(8,128)(2,1)}, u32[]{:S(2)}, u32[]{:S(2)}) %collective-permute-start.18) | collective-permute-done | bytes 131104 | tf_op jit(solution)/shard_map/ppermute | solution.py:699
  59.5 2.8 %collective-permute-start.10 = (bf16[2,8,32,128]{3,2,1,0:T(8,128)(2,1)}, bf16[2,8,32,128]{3,2,1,0:T(8,128)(2,1)}, u32[]{:S(2)}, u32[]{:S(2)}) collective-permute-start(bf16[2,8,32,128]{3,2,1,0:T(8,128)(2,1)} %get-tuple-element.56), channel_id=1, source_target_pairs={{0,4},{1,5},{2,6},{3,7},{4,0},{5,1},{6,2},{7,3},{8,12},{9,13},{10,... | collective-permute-start | bytes 393224 | tf_op jit(solution)/shard_map/ppermute | solution.py:699
  62.3 4.9 %collective-permute-start.11 = (bf16[2,8,32,128]{3,2,1,0:T(8,128)(2,1)}, bf16[2,8,32,128]{3,2,1,0:T(8,128)(2,1)}, u32[]{:S(2)}, u32[]{:S(2)}) collective-permute-start(bf16[2,8,32,128]{3,2,1,0:T(8,128)(2,1)} %get-tuple-element.57), channel_id=1, source_target_pairs={{0,5},{1,4},{2,7},{3,6},{4,1},{5,0},{6,3},{7,2},{8,13},{9,12},{10,... | collective-permute-start | bytes 393224 | tf_op jit(solution)/shard_map/ppermute | solution.py:699
  67.2 6.0 %transform_by_pair.3 = (bf16[2,8,32,128]{3,2,1,0:T(8,128)(2,1)}, bf16[2,8,32,128]{3,2,1,0:T(8,128)(2,1)}, bf16[2,8,32,128]{3,2,1,0:T(8,128)(2,1)}, bf16[2,8,32,1...) custom-call(s32[1]{0:T(128)} %bitcast.1.chan_ref.refs_0_, ...), custom_call_target="tpu_custom_call" | custom-call | tf_op jit(solution)/shard_map/transform_by_pair/pallas_call | solution.py:384
  75.9 2.7 %collective-permute-start.13 = (bf16[2,8,32,128]{3,2,1,0:T(8,128)(2,1)}, bf16[2,8,32,128]{3,2,1,0:T(8,128)(2,1)}, u32[]{:S(2)}, u32[]{:S(2)}) collective-permute-start(bf16[2,8,32,128]{3,2,1,0:T(8,128)(2,1)} %get-tuple-element.59), channel_id=1, source_target_pairs={{0,7},{1,6},{2,5},{3,4},{4,3},{5,2},{6,1},{7,0},{8,15},{9,14},{10,... | collective-permute-start | bytes 393224 | tf_op jit(solution)/shard_map/ppermute | solution.py:699
  79.1 3.0 %collective-permute-start.23 = (bf16[2,8,32,128]{3,2,1,0:T(8,128)(2,1)}, bf16[2,8,32,128]{3,2,1,0:T(8,128)(2,1)}, u32[]{:S(2)}, u32[]{:S(2)}) collective-permute-start(bf16[2,8,32,128]{3,2,1,0:T(8,128)(2,1)} %get-tuple-element.72), channel_id=1, source_target_pairs={{0,3},{1,2},{2,1},{3,0},{4,7},{5,6},{6,5},{7,4},{8,11},{9,10},{10,... | collective-permute-start | bytes 393224 | tf_op jit(solution)/shard_map/ppermute | solution.py:699
  82.1 3.1 %collective-permute-start.24 = (bf16[2,8,32,128]{3,2,1,0:T(8,128)(2,1)}, bf16[2,8,32,128]{3,2,1,0:T(8,128)(2,1)}, u32[]{:S(2)}, u32[]{:S(2)}) collective-permute-start(bf16[2,8,32,128]{3,2,1,0:T(8,128)(2,1)} %get-tuple-element.73), channel_id=1, source_target_pairs={{0,4},{1,5},{2,6},{3,7},{4,0},{5,1},{6,2},{7,3},{8,12},{9,13},{10,... | collective-permute-start | bytes 393224 | tf_op jit(solution)/shard_map/ppermute | solution.py:699
  85.2 5.3 %collective-permute-start.25 = (bf16[2,8,32,128]{3,2,1,0:T(8,128)(2,1)}, bf16[2,8,32,128]{3,2,1,0:T(8,128)(2,1)}, u32[]{:S(2)}, u32[]{:S(2)}) collective-permute-start(bf16[2,8,32,128]{3,2,1,0:T(8,128)(2,1)} %get-tuple-element.74), channel_id=1, source_target_pairs={{0,5},{1,4},{2,7},{3,6},{4,1},{5,0},{6,3},{7,2},{8,13},{9,12},{10,... | collective-permute-start | bytes 393224 | tf_op jit(solution)/shard_map/ppermute | solution.py:699
  100.6 3.7 %collective-permute-done.25.refs_5_ = bf16[2,8,32,128]{3,2,1,0:T(8,128)(2,1)} collective-permute-done((bf16[2,8,32,128]{3,2,1,0:T(8,128)(2,1)}, bf16[2,8,32,128]{3,2,1,0:T(8,128)(2,1)}, u32[]{:S(2)}, u32[]{:S(2)}) %collective-permute-start.25) | collective-permute-done | bytes 131104 | tf_op jit(solution)/shard_map/ppermute | solution.py:699
  110.9 5.0 %left_operand.1.left_ref = bf16[2,64,64,128]{3,2,1,0:T(8,128)(2,1)} custom-call(bf16[256,8,128]{2,1,0:T(8,128)(2,1)} %get-tuple-element.60.refs_0_, bf16[256,8,128]{2,1,0:T(8,128)(2,1)} %get-tuple-element.77.refs_1_, bf16[256,8,128]{2,1,0:T(8,128)(2,1)} %turn.4.refs_8_.refs_2_, bf16[256,8,128]{2,1,0:T(8,128)(2,1)} %turn.6.refs_8_.refs_3_), custom_call_target="tpu_custom_call" | custom-call | tf_op jit(solution)/shard_map/left_operand/pallas_call | solution.py:519
  115.9 5.3 %correlate.3.refs_2_ = bf16[3,64,256,128]{3,2,1,0:T(8,128)(2,1)} custom-call(s32[1]{0:T(128)} %bitcast.group_ref, s32[3,4]{1,0:T(4,128)} %plan_ref.5, bf16[2,64,64,128]{3,2,1,0:T(8,128)(2,1)} %left_operand.1.left_ref, bf16[256,8,128]{2,1,0:T(8,128)(2,1)} %collective-permute-done.30.refs_0_, bf16[256,8,128]{2,1,0:T(8,128)(2,1)} %collective-permute-done.31.refs_1_), custom_call_target="tpu_custom_call" | custom-call | flops 536870912 | bytes 16777216 | tf_op jit(solution)/shard_map/correlate/pallas_call | solution.py:610
  121.2 2.8 %collective-permute-done.28.refs_0_ = bf16[256,8,128]{2,1,0:T(8,128)(2,1)} collective-permute-done((bf16[256,8,128]{2,1,0:T(8,128)(2,1)}, bf16[256,8,128]{2,1,0:T(8,128)(2,1)}, u32[]{:S(2)}, u32[]{:S(2)}) %collective-permute-start.28) | collective-permute-done | bytes 524320 | tf_op jit(solution)/shard_map/ppermute | solution.py:705
  124.0 10.8 %collective-permute-done.29.refs_1_ = bf16[256,8,128]{2,1,0:T(8,128)(2,1)} collective-permute-done((bf16[256,8,128]{2,1,0:T(8,128)(2,1)}, bf16[256,8,128]{2,1,0:T(8,128)(2,1)}, u32[]{:S(2)}, u32[]{:S(2)}) %collective-permute-start.29) | collective-permute-done | bytes 524320 | tf_op jit(solution)/shard_map/ppermute | solution.py:705
  135.3 5.3 %correlate.4.refs_2_ = bf16[3,64,256,128]{3,2,1,0:T(8,128)(2,1)} custom-call(s32[1]{0:T(128)} %bitcast.group_ref, s32[3,4]{1,0:T(4,128)} %plan_ref.5, bf16[2,64,64,128]{3,2,1,0:T(8,128)(2,1)} %left_operand.1.left_ref, bf16[256,8,128]{2,1,0:T(8,128)(2,1)} %collective-permute-done.28.refs_0_, ...), custom_call_target="tpu_custom_call", output_to_operand_aliasing={{}: (5, {})} | custom-call | flops 536870912 | bytes 16777216 | tf_op jit(solution)/shard_map/correlate/pallas_call | solution.py:610
  140.6 5.3 %correlate.5 = bf16[3,64,256,128]{3,2,1,0:T(8,128)(2,1)} custom-call(s32[1]{0:T(128)} %bitcast.group_ref, s32[3,4]{1,0:T(4,128)} %plan_ref.5, bf16[2,64,64,128]{3,2,1,0:T(8,128)(2,1)} %left_operand.1.left_ref, bf16[256,8,128]{2,1,0:T(8,128)(2,1)} %collective-permute-done.32.refs_0_, ...), custom_call_target="tpu_custom_call", output_to_operand_aliasing={{}: (5, {})} | custom-call | flops 536870912 | bytes 16777216 | tf_op jit(solution)/shard_map/correlate/pallas_call | solution.py:610
  (57 shorter events, 33.1 us)
Async XLA Ops:
  4.0 20.0 %collective-permute-start.3 = (bf16[64,1024]{1,0:T(8,128)(2,1)}, bf16[64,1024]{1,0:T(8,128)(2,1)}, u32[]{:S(2)}, u32[]{:S(2)}) collective-permute-start(bf16[64,1024]{1,0:T(8,128)(2,1)} %get-tuple-element.48), channel_id=1, source_target_pairs={{0,4},{1,5},{2,6},{3,7},{4,0},{5,1},{6,2},{7,3},{8,12},{9,13},{10,... | collective-permute-start | bytes 393224 | tf_op jit(solution)/shard_map/ppermute | solution.py:699
  8.0 20.0 %collective-permute-start.4 = (bf16[64,1024]{1,0:T(8,128)(2,1)}, bf16[64,1024]{1,0:T(8,128)(2,1)}, u32[]{:S(2)}, u32[]{:S(2)}) collective-permute-start(bf16[64,1024]{1,0:T(8,128)(2,1)} %get-tuple-element.49), channel_id=1, source_target_pairs={{0,5},{1,4},{2,7},{3,6},{4,1},{5,0},{6,3},{7,2},{8,13},{9,12},{10,... | collective-permute-start | bytes 393224 | tf_op jit(solution)/shard_map/ppermute | solution.py:699
  9.3 18.7 %collective-permute-start.5 = (bf16[64,1024]{1,0:T(8,128)(2,1)}, bf16[64,1024]{1,0:T(8,128)(2,1)}, u32[]{:S(2)}, u32[]{:S(2)}) collective-permute-start(bf16[64,1024]{1,0:T(8,128)(2,1)} %get-tuple-element.50), channel_id=1, source_target_pairs={{0,6},{1,7},{2,4},{3,5},{4,2},{5,3},{6,0},{7,1},{8,14},{9,15},{10,... | collective-permute-start | bytes 393224 | tf_op jit(solution)/shard_map/ppermute | solution.py:699
  12.9 15.3 %collective-permute-start.6 = (bf16[64,1024]{1,0:T(8,128)(2,1)}, bf16[64,1024]{1,0:T(8,128)(2,1)}, u32[]{:S(2)}, u32[]{:S(2)}) collective-permute-start(bf16[64,1024]{1,0:T(8,128)(2,1)} %get-tuple-element.51), channel_id=1, source_target_pairs={{0,7},{1,6},{2,5},{3,4},{4,3},{5,2},{6,1},{7,0},{8,15},{9,14},{10,... | collective-permute-start | bytes 393224 | tf_op jit(solution)/shard_map/ppermute | solution.py:699
  16.9 18.2 %collective-permute-start = (bf16[64,1024]{1,0:T(8,128)(2,1)}, bf16[64,1024]{1,0:T(8,128)(2,1)}, u32[]{:S(2)}, u32[]{:S(2)}) collective-permute-start(bf16[64,1024]{1,0:T(8,128)(2,1)} %get-tuple-element.45), channel_id=1, source_target_pairs={{0,1},{1,0},{2,3},{3,2},{4,5},{5,4},{6,7},{7,6},{8,9},{9,8},{10,11... | collective-permute-start | bytes 393224 | tf_op jit(solution)/shard_map/ppermute | solution.py:699
  28.2 14.9 %collective-permute-start.15 = (bf16[64,1024]{1,0:T(8,128)(2,1)}, bf16[64,1024]{1,0:T(8,128)(2,1)}, u32[]{:S(2)}, u32[]{:S(2)}) collective-permute-start(bf16[64,1024]{1,0:T(8,128)(2,1)} %get-tuple-element.63), channel_id=1, source_target_pairs={{0,2},{1,3},{2,0},{3,1},{4,6},{5,7},{6,4},{7,5},{8,10},{9,11},{10,... | collective-permute-start | bytes 393224 | tf_op jit(solution)/shard_map/ppermute | solution.py:699
  35.1 15.6 %collective-permute-start.16 = (bf16[64,1024]{1,0:T(8,128)(2,1)}, bf16[64,1024]{1,0:T(8,128)(2,1)}, u32[]{:S(2)}, u32[]{:S(2)}) collective-permute-start(bf16[64,1024]{1,0:T(8,128)(2,1)} %get-tuple-element.64), channel_id=1, source_target_pairs={{0,3},{1,2},{2,1},{3,0},{4,7},{5,6},{6,5},{7,4},{8,11},{9,10},{10,... | collective-permute-start | bytes 393224 | tf_op jit(solution)/shard_map/ppermute | solution.py:699
  35.1 17.8 %collective-permute-start.17 = (bf16[64,1024]{1,0:T(8,128)(2,1)}, bf16[64,1024]{1,0:T(8,128)(2,1)}, u32[]{:S(2)}, u32[]{:S(2)}) collective-permute-start(bf16[64,1024]{1,0:T(8,128)(2,1)} %get-tuple-element.65), channel_id=1, source_target_pairs={{0,4},{1,5},{2,6},{3,7},{4,0},{5,1},{6,2},{7,3},{8,12},{9,13},{10,... | collective-permute-start | bytes 393224 | tf_op jit(solution)/shard_map/ppermute | solution.py:699
  39.2 20.3 %collective-permute-start.18 = (bf16[64,1024]{1,0:T(8,128)(2,1)}, bf16[64,1024]{1,0:T(8,128)(2,1)}, u32[]{:S(2)}, u32[]{:S(2)}) collective-permute-start(bf16[64,1024]{1,0:T(8,128)(2,1)} %get-tuple-element.66), channel_id=1, source_target_pairs={{0,5},{1,4},{2,7},{3,6},{4,1},{5,0},{6,3},{7,2},{8,13},{9,12},{10,... | collective-permute-start | bytes 393224 | tf_op jit(solution)/shard_map/ppermute | solution.py:699
  40.8 18.6 %collective-permute-start.19 = (bf16[64,1024]{1,0:T(8,128)(2,1)}, bf16[64,1024]{1,0:T(8,128)(2,1)}, u32[]{:S(2)}, u32[]{:S(2)}) collective-permute-start(bf16[64,1024]{1,0:T(8,128)(2,1)} %get-tuple-element.67), channel_id=1, source_target_pairs={{0,6},{1,7},{2,4},{3,5},{4,2},{5,3},{6,0},{7,1},{8,14},{9,15},{10,... | collective-permute-start | bytes 393224 | tf_op jit(solution)/shard_map/ppermute | solution.py:699
  43.1 19.2 %collective-permute-start.20 = (bf16[64,1024]{1,0:T(8,128)(2,1)}, bf16[64,1024]{1,0:T(8,128)(2,1)}, u32[]{:S(2)}, u32[]{:S(2)}) collective-permute-start(bf16[64,1024]{1,0:T(8,128)(2,1)} %get-tuple-element.68), channel_id=1, source_target_pairs={{0,7},{1,6},{2,5},{3,4},{4,3},{5,2},{6,1},{7,0},{8,15},{9,14},{10,... | collective-permute-start | bytes 393224 | tf_op jit(solution)/shard_map/ppermute | solution.py:699
  50.7 22.5 %collective-permute-start.7 = (bf16[2,8,32,128]{3,2,1,0:T(8,128)(2,1)}, bf16[2,8,32,128]{3,2,1,0:T(8,128)(2,1)}, u32[]{:S(2)}, u32[]{:S(2)}) collective-permute-start(bf16[2,8,32,128]{3,2,1,0:T(8,128)(2,1)} %get-tuple-element.53), channel_id=1, source_target_pairs={{0,1},{1,0},{2,3},{3,2},{4,5},{5,4},{6,7},{7,6},{8,9},{9,8},{10,11... | collective-permute-start | bytes 393224 | tf_op jit(solution)/shard_map/ppermute | solution.py:699
  52.9 22.9 %collective-permute-start.8 = (bf16[2,8,32,128]{3,2,1,0:T(8,128)(2,1)}, bf16[2,8,32,128]{3,2,1,0:T(8,128)(2,1)}, u32[]{:S(2)}, u32[]{:S(2)}) collective-permute-start(bf16[2,8,32,128]{3,2,1,0:T(8,128)(2,1)} %get-tuple-element.54), channel_id=1, source_target_pairs={{0,2},{1,3},{2,0},{3,1},{4,6},{5,7},{6,4},{7,5},{8,10},{9,11},{10,... | collective-permute-start | bytes 393224 | tf_op jit(solution)/shard_map/ppermute | solution.py:699
  59.5 19.1 %collective-permute-start.9 = (bf16[2,8,32,128]{3,2,1,0:T(8,128)(2,1)}, bf16[2,8,32,128]{3,2,1,0:T(8,128)(2,1)}, u32[]{:S(2)}, u32[]{:S(2)}) collective-permute-start(bf16[2,8,32,128]{3,2,1,0:T(8,128)(2,1)} %get-tuple-element.55), channel_id=1, source_target_pairs={{0,3},{1,2},{2,1},{3,0},{4,7},{5,6},{6,5},{7,4},{8,11},{9,10},{10,... | collective-permute-start | bytes 393224 | tf_op jit(solution)/shard_map/ppermute | solution.py:699
  59.5 19.1 %collective-permute-start.10 = (bf16[2,8,32,128]{3,2,1,0:T(8,128)(2,1)}, bf16[2,8,32,128]{3,2,1,0:T(8,128)(2,1)}, u32[]{:S(2)}, u32[]{:S(2)}) collective-permute-start(bf16[2,8,32,128]{3,2,1,0:T(8,128)(2,1)} %get-tuple-element.56), channel_id=1, source_target_pairs={{0,4},{1,5},{2,6},{3,7},{4,0},{5,1},{6,2},{7,3},{8,12},{9,13},{10,... | collective-permute-start | bytes 393224 | tf_op jit(solution)/shard_map/ppermute | solution.py:699
  62.3 16.8 %collective-permute-start.11 = (bf16[2,8,32,128]{3,2,1,0:T(8,128)(2,1)}, bf16[2,8,32,128]{3,2,1,0:T(8,128)(2,1)}, u32[]{:S(2)}, u32[]{:S(2)}) collective-permute-start(bf16[2,8,32,128]{3,2,1,0:T(8,128)(2,1)} %get-tuple-element.57), channel_id=1, source_target_pairs={{0,5},{1,4},{2,7},{3,6},{4,1},{5,0},{6,3},{7,2},{8,13},{9,12},{10,... | collective-permute-start | bytes 393224 | tf_op jit(solution)/shard_map/ppermute | solution.py:699
  78.6 14.0 %collective-permute-start.22 = (bf16[2,8,32,128]{3,2,1,0:T(8,128)(2,1)}, bf16[2,8,32,128]{3,2,1,0:T(8,128)(2,1)}, u32[]{:S(2)}, u32[]{:S(2)}) collective-permute-start(bf16[2,8,32,128]{3,2,1,0:T(8,128)(2,1)} %get-tuple-element.71), channel_id=1, source_target_pairs={{0,2},{1,3},{2,0},{3,1},{4,6},{5,7},{6,4},{7,5},{8,10},{9,11},{10,... | collective-permute-start | bytes 393224 | tf_op jit(solution)/shard_map/ppermute | solution.py:699
  79.1 20.5 %collective-permute-start.23 = (bf16[2,8,32,128]{3,2,1,0:T(8,128)(2,1)}, bf16[2,8,32,128]{3,2,1,0:T(8,128)(2,1)}, u32[]{:S(2)}, u32[]{:S(2)}) collective-permute-start(bf16[2,8,32,128]{3,2,1,0:T(8,128)(2,1)} %get-tuple-element.72), channel_id=1, source_target_pairs={{0,3},{1,2},{2,1},{3,0},{4,7},{5,6},{6,5},{7,4},{8,11},{9,10},{10,... | collective-permute-start | bytes 393224 | tf_op jit(solution)/shard_map/ppermute | solution.py:699
  82.1 18.5 %collective-permute-start.24 = (bf16[2,8,32,128]{3,2,1,0:T(8,128)(2,1)}, bf16[2,8,32,128]{3,2,1,0:T(8,128)(2,1)}, u32[]{:S(2)}, u32[]{:S(2)}) collective-permute-start(bf16[2,8,32,128]{3,2,1,0:T(8,128)(2,1)} %get-tuple-element.73), channel_id=1, source_target_pairs={{0,4},{1,5},{2,6},{3,7},{4,0},{5,1},{6,2},{7,3},{8,12},{9,13},{10,... | collective-permute-start | bytes 393224 | tf_op jit(solution)/shard_map/ppermute | solution.py:699
  85.2 19.0 %collective-permute-start.25 = (bf16[2,8,32,128]{3,2,1,0:T(8,128)(2,1)}, bf16[2,8,32,128]{3,2,1,0:T(8,128)(2,1)}, u32[]{:S(2)}, u32[]{:S(2)}) collective-permute-start(bf16[2,8,32,128]{3,2,1,0:T(8,128)(2,1)} %get-tuple-element.74), channel_id=1, source_target_pairs={{0,5},{1,4},{2,7},{3,6},{4,1},{5,0},{6,3},{7,2},{8,13},{9,12},{10,... | collective-permute-start | bytes 393224 | tf_op jit(solution)/shard_map/ppermute | solution.py:699
  90.5 13.7 %collective-permute-start.26 = (bf16[2,8,32,128]{3,2,1,0:T(8,128)(2,1)}, bf16[2,8,32,128]{3,2,1,0:T(8,128)(2,1)}, u32[]{:S(2)}, u32[]{:S(2)}) collective-permute-start(bf16[2,8,32,128]{3,2,1,0:T(8,128)(2,1)} %get-tuple-element.75), channel_id=1, source_target_pairs={{0,6},{1,7},{2,4},{3,5},{4,2},{5,3},{6,0},{7,1},{8,14},{9,15},{10,... | collective-permute-start | bytes 393224 | tf_op jit(solution)/shard_map/ppermute | solution.py:699
  99.6 16.3 %collective-permute-start.30 = (bf16[256,8,128]{2,1,0:T(8,128)(2,1)}, bf16[256,8,128]{2,1,0:T(8,128)(2,1)}, u32[]{:S(2)}, u32[]{:S(2)}) collective-permute-start(bf16[256,8,128]{2,1,0:T(8,128)(2,1)} %get-tuple-element.78), channel_id=1, source_target_pairs={{0,8},{8,0},{16,24},{24,16},{1,9},{9,1},{17,25},{25,17},{2,10},{10... | collective-permute-start | bytes 1572872 | tf_op jit(solution)/shard_map/ppermute | solution.py:705
  108.9 15.1 %collective-permute-start.28 = (bf16[256,8,128]{2,1,0:T(8,128)(2,1)}, bf16[256,8,128]{2,1,0:T(8,128)(2,1)}, u32[]{:S(2)}, u32[]{:S(2)}) collective-permute-start(bf16[256,8,128]{2,1,0:T(8,128)(2,1)} %turn.4.refs_8_.refs_2_), channel_id=1, source_target_pairs={{0,16},{8,24},{16,0},{24,8},{1,17},{9,25},{17,1},{25,9},{2,18},{10... | collective-permute-start | bytes 1572872 | tf_op jit(solution)/shard_map/ppermute | solution.py:705
  110.4 24.4 %collective-permute-start.29 = (bf16[256,8,128]{2,1,0:T(8,128)(2,1)}, bf16[256,8,128]{2,1,0:T(8,128)(2,1)}, u32[]{:S(2)}, u32[]{:S(2)}) collective-permute-start(bf16[256,8,128]{2,1,0:T(8,128)(2,1)} %turn.6.refs_8_.refs_3_), channel_id=1, source_target_pairs={{0,16},{8,24},{16,0},{24,8},{1,17},{9,25},{17,1},{25,9},{2,18},{10... | collective-permute-start | bytes 1572872 | tf_op jit(solution)/shard_map/ppermute | solution.py:705
  (10 other events, 95.5 us)

commit v10 on v9

--- a/solution.py
+++ b/solution.py
@@ -459,7 +459,9 @@
             in_specs=[pl.BlockSpec((1, per, k2_count, lanes), half_at)] * chan_count
             + [whole] * other,
             out_specs=[whole] * (1 + other),
-            scratch_shapes=[pltpu.VMEM((k2_count * (per * chan_count + 1), lanes), jnp.float32)],
+            scratch_shapes=[
+                pltpu.VMEM(((k2_count + EIGHT) * (per * chan_count + 1), lanes), jnp.float32)
+            ],
         ),
         compiler_params=pltpu.CompilerParams(vmem_limit_bytes=VMEM_LIMIT),
         name="turn",
@@ -617,7 +619,7 @@
             out_specs=pl.BlockSpec(
                 (1, sig_count, tile, lanes), lambda i, g, p: (round_of(g, p), 0, i, 0)
             ),
-            scratch_shapes=[pltpu.VMEM((sig_count * (tile + 1), lanes), jnp.float32)],
+            scratch_shapes=[pltpu.VMEM(((sig_count + EIGHT) * (tile + 1), lanes), jnp.float32)],
         ),
         input_output_aliases=aliases,
         compiler_params=pltpu.CompilerParams(vmem_limit_bytes=VMEM_LIMIT),

time: 149 us -> 149 us (level)
  no operation moved by 1% of the time
where the time goes in v10:
time: 149 us; the launch traced here: 146 us
  starting transfers between devices  62.9 us (42%)
  Pallas kernels  55.4 us (37%)
  waiting for transfers between devices  27.5 us (18%)
    ppermute x28, starting transfers between devices, over_chan(): lax.ppermute(blocks[pair], 'chan', [(c, c ^ pair) for c in range(chan_cou...  60.4 us
    pallas_call x3, Pallas kernels, correlate(): pl.pallas_call(functools.partial(correlate_kernel, len(chunks), spec_coun...  15.9 us
    ppermute x28, waiting for transfers between devices, over_chan(): lax.ppermute(blocks[pair], 'chan', [(c, c ^ pair) for c in range(chan_cou...  13.9 us
    ppermute x6, waiting for transfers between devices, to_mate(): lax.ppermute(value, 'grp', [(g, g ^ distance) for g in range(group_count)])  13.6 us
    pallas_call x3, Pallas kernels, filter_by_pair(): pl.pallas_call(functools.partial(filter_by_pair_kernel, pairs), out_shape...  13.3 us
    pallas_call x2, Pallas kernels, transform_by_pair(): pl.pallas_call(functools.partial(transform_by_pair_kernel, chan_count), o...  12 us
    pallas_call x4, Pallas kernels, turn(): pl.pallas_call(functools.partial(turn_kernel, other), out_shape=[jax.Shap...  9.23 us
    pallas_call x1, Pallas kernels, left_operand(): pl.pallas_call(functools.partial(left_kernel, chunk_count), out_shape=jax...  4.96 us
  transfers between devices with their start and end apart: 34, of which 8 were waited for; matrix products, arithmetic and copies ran while one was open for 0% of the time, Pallas kernels for 32%

profile of v10, /device:TPU:0, one launch (start us, length us, event | category | flops | bytes accessed | tf_op | source)
XLA Modules:
  0.0 145.9 jit_solution(6250766319295964231)
XLA Ops:
  0.0 4.0 %filter_by_pair.4 = (bf16[64,1024]{1,0:T(8,128)(2,1)}, bf16[64,1024]{1,0:T(8,128)(2,1)}, bf16[64,1024]{1,0:T(8,128)(2,1)}, bf16[64,1024]{1,0:T(8,128)(2,1)}) custom-call(s32[1]{0:T(128)} %bitcast.1.chan_ref.refs_0_, s32[31,64,1024]{2,1,0:T(8,128)} %bitcast.3, f32[8,16,1024]{2,1,0:T(8,128)} %constant.18.clone.coeff_ref), custom_call_target="tpu_custom_call" | custom-call | tf_op jit(solution)/shard_map/filter_by_pair/pallas_call | solution.py:99
  4.0 4.1 %collective-permute-start.3 = (bf16[64,1024]{1,0:T(8,128)(2,1)}, bf16[64,1024]{1,0:T(8,128)(2,1)}, u32[]{:S(2)}, u32[]{:S(2)}) collective-permute-start(bf16[64,1024]{1,0:T(8,128)(2,1)} %get-tuple-element.48), channel_id=1, source_target_pairs={{0,4},{1,5},{2,6},{3,7},{4,0},{5,1},{6,2},{7,3},{8,12},{9,13},{10,... | collective-permute-start | bytes 393224 | tf_op jit(solution)/shard_map/ppermute | solution.py:701
  9.3 3.6 %collective-permute-start.5 = (bf16[64,1024]{1,0:T(8,128)(2,1)}, bf16[64,1024]{1,0:T(8,128)(2,1)}, u32[]{:S(2)}, u32[]{:S(2)}) collective-permute-start(bf16[64,1024]{1,0:T(8,128)(2,1)} %get-tuple-element.50), channel_id=1, source_target_pairs={{0,6},{1,7},{2,4},{3,5},{4,2},{5,3},{6,0},{7,1},{8,14},{9,15},{10,... | collective-permute-start | bytes 393224 | tf_op jit(solution)/shard_map/ppermute | solution.py:701
  12.9 4.0 %filter_by_pair.3 = (bf16[64,1024]{1,0:T(8,128)(2,1)}, bf16[64,1024]{1,0:T(8,128)(2,1)}, bf16[64,1024]{1,0:T(8,128)(2,1)}, bf16[64,1024]{1,0:T(8,128)(2,1)}) custom-call(s32[1]{0:T(128)} %bitcast.1.chan_ref.refs_0_, s32[31,64,1024]{2,1,0:T(8,128)} %bitcast.4, f32[8,16,1024]{2,1,0:T(8,128)} %constant.18.clone.coeff_ref), custom_call_target="tpu_custom_call" | custom-call | tf_op jit(solution)/shard_map/filter_by_pair/pallas_call | solution.py:99
  18.5 5.3 %filter_by_pair.5 = (bf16[64,1024]{1,0:T(8,128)(2,1)}, bf16[64,1024]{1,0:T(8,128)(2,1)}, bf16[64,1024]{1,0:T(8,128)(2,1)}, bf16[64,1024]{1,0:T(8,128)(2,1)}, bf1...) custom-call(s32[1]{0:T(128)} %bitcast.1.chan_ref.refs_0_, ...), custom_call_target="tpu_custom_call" | custom-call | tf_op jit(solution)/shard_map/filter_by_pair/pallas_call | solution.py:99
  24.0 4.0 %collective-permute-done.4.refs_10_ = bf16[64,1024]{1,0:T(8,128)(2,1)} collective-permute-done((bf16[64,1024]{1,0:T(8,128)(2,1)}, bf16[64,1024]{1,0:T(8,128)(2,1)}, u32[]{:S(2)}, u32[]{:S(2)}) %collective-permute-start.4) | collective-permute-done | bytes 131104 | tf_op jit(solution)/shard_map/ppermute | solution.py:701
  28.2 6.9 %collective-permute-start.15 = (bf16[64,1024]{1,0:T(8,128)(2,1)}, bf16[64,1024]{1,0:T(8,128)(2,1)}, u32[]{:S(2)}, u32[]{:S(2)}) collective-permute-start(bf16[64,1024]{1,0:T(8,128)(2,1)} %get-tuple-element.63), channel_id=1, source_target_pairs={{0,2},{1,3},{2,0},{3,1},{4,6},{5,7},{6,4},{7,5},{8,10},{9,11},{10,... | collective-permute-start | bytes 393224 | tf_op jit(solution)/shard_map/ppermute | solution.py:701
  35.1 4.1 %collective-permute-start.17 = (bf16[64,1024]{1,0:T(8,128)(2,1)}, bf16[64,1024]{1,0:T(8,128)(2,1)}, u32[]{:S(2)}, u32[]{:S(2)}) collective-permute-start(bf16[64,1024]{1,0:T(8,128)(2,1)} %get-tuple-element.65), channel_id=1, source_target_pairs={{0,4},{1,5},{2,6},{3,7},{4,0},{5,1},{6,2},{7,3},{8,12},{9,13},{10,... | collective-permute-start | bytes 393224 | tf_op jit(solution)/shard_map/ppermute | solution.py:701
  44.7 6.1 %transform_by_pair.2 = (bf16[2,8,32,128]{3,2,1,0:T(8,128)(2,1)}, bf16[2,8,32,128]{3,2,1,0:T(8,128)(2,1)}, bf16[2,8,32,128]{3,2,1,0:T(8,128)(2,1)}, bf16[2,8,32,1...) custom-call(s32[1]{0:T(128)} %bitcast.1.chan_ref.refs_0_, ...), custom_call_target="tpu_custom_call" | custom-call | tf_op jit(solution)/shard_map/transform_by_pair/pallas_call | solution.py:384
  54.8 4.7 %collective-permute-done.18.refs_10_ = bf16[64,1024]{1,0:T(8,128)(2,1)} collective-permute-done((bf16[64,1024]{1,0:T(8,128)(2,1)}, bf16[64,1024]{1,0:T(8,128)(2,1)}, u32[]{:S(2)}, u32[]{:S(2)}) %collective-permute-start.18) | collective-permute-done | bytes 131104 | tf_op jit(solution)/shard_map/ppermute | solution.py:701
  59.5 2.8 %collective-permute-start.10 = (bf16[2,8,32,128]{3,2,1,0:T(8,128)(2,1)}, bf16[2,8,32,128]{3,2,1,0:T(8,128)(2,1)}, u32[]{:S(2)}, u32[]{:S(2)}) collective-permute-start(bf16[2,8,32,128]{3,2,1,0:T(8,128)(2,1)} %get-tuple-element.56), channel_id=1, source_target_pairs={{0,4},{1,5},{2,6},{3,7},{4,0},{5,1},{6,2},{7,3},{8,12},{9,13},{10,... | collective-permute-start | bytes 393224 | tf_op jit(solution)/shard_map/ppermute | solution.py:701
  62.3 4.9 %collective-permute-start.11 = (bf16[2,8,32,128]{3,2,1,0:T(8,128)(2,1)}, bf16[2,8,32,128]{3,2,1,0:T(8,128)(2,1)}, u32[]{:S(2)}, u32[]{:S(2)}) collective-permute-start(bf16[2,8,32,128]{3,2,1,0:T(8,128)(2,1)} %get-tuple-element.57), channel_id=1, source_target_pairs={{0,5},{1,4},{2,7},{3,6},{4,1},{5,0},{6,3},{7,2},{8,13},{9,12},{10,... | collective-permute-start | bytes 393224 | tf_op jit(solution)/shard_map/ppermute | solution.py:701
  67.2 6.0 %transform_by_pair.3 = (bf16[2,8,32,128]{3,2,1,0:T(8,128)(2,1)}, bf16[2,8,32,128]{3,2,1,0:T(8,128)(2,1)}, bf16[2,8,32,128]{3,2,1,0:T(8,128)(2,1)}, bf16[2,8,32,1...) custom-call(s32[1]{0:T(128)} %bitcast.1.chan_ref.refs_0_, ...), custom_call_target="tpu_custom_call" | custom-call | tf_op jit(solution)/shard_map/transform_by_pair/pallas_call | solution.py:384
  75.9 2.7 %collective-permute-start.13 = (bf16[2,8,32,128]{3,2,1,0:T(8,128)(2,1)}, bf16[2,8,32,128]{3,2,1,0:T(8,128)(2,1)}, u32[]{:S(2)}, u32[]{:S(2)}) collective-permute-start(bf16[2,8,32,128]{3,2,1,0:T(8,128)(2,1)} %get-tuple-element.59), channel_id=1, source_target_pairs={{0,7},{1,6},{2,5},{3,4},{4,3},{5,2},{6,1},{7,0},{8,15},{9,14},{10,... | collective-permute-start | bytes 393224 | tf_op jit(solution)/shard_map/ppermute | solution.py:701
  79.1 3.0 %collective-permute-start.23 = (bf16[2,8,32,128]{3,2,1,0:T(8,128)(2,1)}, bf16[2,8,32,128]{3,2,1,0:T(8,128)(2,1)}, u32[]{:S(2)}, u32[]{:S(2)}) collective-permute-start(bf16[2,8,32,128]{3,2,1,0:T(8,128)(2,1)} %get-tuple-element.72), channel_id=1, source_target_pairs={{0,3},{1,2},{2,1},{3,0},{4,7},{5,6},{6,5},{7,4},{8,11},{9,10},{10,... | collective-permute-start | bytes 393224 | tf_op jit(solution)/shard_map/ppermute | solution.py:701
  82.1 3.1 %collective-permute-start.24 = (bf16[2,8,32,128]{3,2,1,0:T(8,128)(2,1)}, bf16[2,8,32,128]{3,2,1,0:T(8,128)(2,1)}, u32[]{:S(2)}, u32[]{:S(2)}) collective-permute-start(bf16[2,8,32,128]{3,2,1,0:T(8,128)(2,1)} %get-tuple-element.73), channel_id=1, source_target_pairs={{0,4},{1,5},{2,6},{3,7},{4,0},{5,1},{6,2},{7,3},{8,12},{9,13},{10,... | collective-permute-start | bytes 393224 | tf_op jit(solution)/shard_map/ppermute | solution.py:701
  85.2 5.3 %collective-permute-start.25 = (bf16[2,8,32,128]{3,2,1,0:T(8,128)(2,1)}, bf16[2,8,32,128]{3,2,1,0:T(8,128)(2,1)}, u32[]{:S(2)}, u32[]{:S(2)}) collective-permute-start(bf16[2,8,32,128]{3,2,1,0:T(8,128)(2,1)} %get-tuple-element.74), channel_id=1, source_target_pairs={{0,5},{1,4},{2,7},{3,6},{4,1},{5,0},{6,3},{7,2},{8,13},{9,12},{10,... | collective-permute-start | bytes 393224 | tf_op jit(solution)/shard_map/ppermute | solution.py:701
  100.6 3.7 %collective-permute-done.25.refs_5_ = bf16[2,8,32,128]{3,2,1,0:T(8,128)(2,1)} collective-permute-done((bf16[2,8,32,128]{3,2,1,0:T(8,128)(2,1)}, bf16[2,8,32,128]{3,2,1,0:T(8,128)(2,1)}, u32[]{:S(2)}, u32[]{:S(2)}) %collective-permute-start.25) | collective-permute-done | bytes 131104 | tf_op jit(solution)/shard_map/ppermute | solution.py:701
  110.9 5.0 %left_operand.1.left_ref = bf16[2,64,64,128]{3,2,1,0:T(8,128)(2,1)} custom-call(bf16[256,8,128]{2,1,0:T(8,128)(2,1)} %get-tuple-element.60.refs_0_, bf16[256,8,128]{2,1,0:T(8,128)(2,1)} %get-tuple-element.77.refs_1_, bf16[256,8,128]{2,1,0:T(8,128)(2,1)} %turn.4.refs_8_.refs_2_, bf16[256,8,128]{2,1,0:T(8,128)(2,1)} %turn.6.refs_8_.refs_3_), custom_call_target="tpu_custom_call" | custom-call | tf_op jit(solution)/shard_map/left_operand/pallas_call | solution.py:521
  115.9 5.3 %correlate.3.refs_2_ = bf16[3,64,256,128]{3,2,1,0:T(8,128)(2,1)} custom-call(s32[1]{0:T(128)} %bitcast.group_ref, s32[3,4]{1,0:T(4,128)} %plan_ref.5, bf16[2,64,64,128]{3,2,1,0:T(8,128)(2,1)} %left_operand.1.left_ref, bf16[256,8,128]{2,1,0:T(8,128)(2,1)} %collective-permute-done.30.refs_0_, bf16[256,8,128]{2,1,0:T(8,128)(2,1)} %collective-permute-done.31.refs_1_), custom_call_target="tpu_custom_call" | custom-call | flops 536870912 | bytes 16777216 | tf_op jit(solution)/shard_map/correlate/pallas_call | solution.py:612
  121.2 2.8 %collective-permute-done.28.refs_0_ = bf16[256,8,128]{2,1,0:T(8,128)(2,1)} collective-permute-done((bf16[256,8,128]{2,1,0:T(8,128)(2,1)}, bf16[256,8,128]{2,1,0:T(8,128)(2,1)}, u32[]{:S(2)}, u32[]{:S(2)}) %collective-permute-start.28) | collective-permute-done | bytes 524320 | tf_op jit(solution)/shard_map/ppermute | solution.py:707
  124.0 10.8 %collective-permute-done.29.refs_1_ = bf16[256,8,128]{2,1,0:T(8,128)(2,1)} collective-permute-done((bf16[256,8,128]{2,1,0:T(8,128)(2,1)}, bf16[256,8,128]{2,1,0:T(8,128)(2,1)}, u32[]{:S(2)}, u32[]{:S(2)}) %collective-permute-start.29) | collective-permute-done | bytes 524320 | tf_op jit(solution)/shard_map/ppermute | solution.py:707
  135.3 5.3 %correlate.4.refs_2_ = bf16[3,64,256,128]{3,2,1,0:T(8,128)(2,1)} custom-call(s32[1]{0:T(128)} %bitcast.group_ref, s32[3,4]{1,0:T(4,128)} %plan_ref.5, bf16[2,64,64,128]{3,2,1,0:T(8,128)(2,1)} %left_operand.1.left_ref, bf16[256,8,128]{2,1,0:T(8,128)(2,1)} %collective-permute-done.28.refs_0_, ...), custom_call_target="tpu_custom_call", output_to_operand_aliasing={{}: (5, {})} | custom-call | flops 536870912 | bytes 16777216 | tf_op jit(solution)/shard_map/correlate/pallas_call | solution.py:612
  140.6 5.3 %correlate.5 = bf16[3,64,256,128]{3,2,1,0:T(8,128)(2,1)} custom-call(s32[1]{0:T(128)} %bitcast.group_ref, s32[3,4]{1,0:T(4,128)} %plan_ref.5, bf16[2,64,64,128]{3,2,1,0:T(8,128)(2,1)} %left_operand.1.left_ref, bf16[256,8,128]{2,1,0:T(8,128)(2,1)} %collective-permute-done.32.refs_0_, ...), custom_call_target="tpu_custom_call", output_to_operand_aliasing={{}: (5, {})} | custom-call | flops 536870912 | bytes 16777216 | tf_op jit(solution)/shard_map/correlate/pallas_call | solution.py:612
  (57 shorter events, 33.1 us)
Async XLA Ops:
  4.0 20.0 %collective-permute-start.3 = (bf16[64,1024]{1,0:T(8,128)(2,1)}, bf16[64,1024]{1,0:T(8,128)(2,1)}, u32[]{:S(2)}, u32[]{:S(2)}) collective-permute-start(bf16[64,1024]{1,0:T(8,128)(2,1)} %get-tuple-element.48), channel_id=1, source_target_pairs={{0,4},{1,5},{2,6},{3,7},{4,0},{5,1},{6,2},{7,3},{8,12},{9,13},{10,... | collective-permute-start | bytes 393224 | tf_op jit(solution)/shard_map/ppermute | solution.py:701
  8.0 20.0 %collective-permute-start.4 = (bf16[64,1024]{1,0:T(8,128)(2,1)}, bf16[64,1024]{1,0:T(8,128)(2,1)}, u32[]{:S(2)}, u32[]{:S(2)}) collective-permute-start(bf16[64,1024]{1,0:T(8,128)(2,1)} %get-tuple-element.49), channel_id=1, source_target_pairs={{0,5},{1,4},{2,7},{3,6},{4,1},{5,0},{6,3},{7,2},{8,13},{9,12},{10,... | collective-permute-start | bytes 393224 | tf_op jit(solution)/shard_map/ppermute | solution.py:701
  9.3 18.7 %collective-permute-start.5 = (bf16[64,1024]{1,0:T(8,128)(2,1)}, bf16[64,1024]{1,0:T(8,128)(2,1)}, u32[]{:S(2)}, u32[]{:S(2)}) collective-permute-start(bf16[64,1024]{1,0:T(8,128)(2,1)} %get-tuple-element.50), channel_id=1, source_target_pairs={{0,6},{1,7},{2,4},{3,5},{4,2},{5,3},{6,0},{7,1},{8,14},{9,15},{10,... | collective-permute-start | bytes 393224 | tf_op jit(solution)/shard_map/ppermute | solution.py:701
  12.9 15.3 %collective-permute-start.6 = (bf16[64,1024]{1,0:T(8,128)(2,1)}, bf16[64,1024]{1,0:T(8,128)(2,1)}, u32[]{:S(2)}, u32[]{:S(2)}) collective-permute-start(bf16[64,1024]{1,0:T(8,128)(2,1)} %get-tuple-element.51), channel_id=1, source_target_pairs={{0,7},{1,6},{2,5},{3,4},{4,3},{5,2},{6,1},{7,0},{8,15},{9,14},{10,... | collective-permute-start | bytes 393224 | tf_op jit(solution)/shard_map/ppermute | solution.py:701
  16.9 18.2 %collective-permute-start = (bf16[64,1024]{1,0:T(8,128)(2,1)}, bf16[64,1024]{1,0:T(8,128)(2,1)}, u32[]{:S(2)}, u32[]{:S(2)}) collective-permute-start(bf16[64,1024]{1,0:T(8,128)(2,1)} %get-tuple-element.45), channel_id=1, source_target_pairs={{0,1},{1,0},{2,3},{3,2},{4,5},{5,4},{6,7},{7,6},{8,9},{9,8},{10,11... | collective-permute-start | bytes 393224 | tf_op jit(solution)/shard_map/ppermute | solution.py:701
  28.2 14.9 %collective-permute-start.15 = (bf16[64,1024]{1,0:T(8,128)(2,1)}, bf16[64,1024]{1,0:T(8,128)(2,1)}, u32[]{:S(2)}, u32[]{:S(2)}) collective-permute-start(bf16[64,1024]{1,0:T(8,128)(2,1)} %get-tuple-element.63), channel_id=1, source_target_pairs={{0,2},{1,3},{2,0},{3,1},{4,6},{5,7},{6,4},{7,5},{8,10},{9,11},{10,... | collective-permute-start | bytes 393224 | tf_op jit(solution)/shard_map/ppermute | solution.py:701
  35.1 15.6 %collective-permute-start.16 = (bf16[64,1024]{1,0:T(8,128)(2,1)}, bf16[64,1024]{1,0:T(8,128)(2,1)}, u32[]{:S(2)}, u32[]{:S(2)}) collective-permute-start(bf16[64,1024]{1,0:T(8,128)(2,1)} %get-tuple-element.64), channel_id=1, source_target_pairs={{0,3},{1,2},{2,1},{3,0},{4,7},{5,6},{6,5},{7,4},{8,11},{9,10},{10,... | collective-permute-start | bytes 393224 | tf_op jit(solution)/shard_map/ppermute | solution.py:701
  35.1 17.8 %collective-permute-start.17 = (bf16[64,1024]{1,0:T(8,128)(2,1)}, bf16[64,1024]{1,0:T(8,128)(2,1)}, u32[]{:S(2)}, u32[]{:S(2)}) collective-permute-start(bf16[64,1024]{1,0:T(8,128)(2,1)} %get-tuple-element.65), channel_id=1, source_target_pairs={{0,4},{1,5},{2,6},{3,7},{4,0},{5,1},{6,2},{7,3},{8,12},{9,13},{10,... | collective-permute-start | bytes 393224 | tf_op jit(solution)/shard_map/ppermute | solution.py:701
  39.2 20.3 %collective-permute-start.18 = (bf16[64,1024]{1,0:T(8,128)(2,1)}, bf16[64,1024]{1,0:T(8,128)(2,1)}, u32[]{:S(2)}, u32[]{:S(2)}) collective-permute-start(bf16[64,1024]{1,0:T(8,128)(2,1)} %get-tuple-element.66), channel_id=1, source_target_pairs={{0,5},{1,4},{2,7},{3,6},{4,1},{5,0},{6,3},{7,2},{8,13},{9,12},{10,... | collective-permute-start | bytes 393224 | tf_op jit(solution)/shard_map/ppermute | solution.py:701
  40.8 18.6 %collective-permute-start.19 = (bf16[64,1024]{1,0:T(8,128)(2,1)}, bf16[64,1024]{1,0:T(8,128)(2,1)}, u32[]{:S(2)}, u32[]{:S(2)}) collective-permute-start(bf16[64,1024]{1,0:T(8,128)(2,1)} %get-tuple-element.67), channel_id=1, source_target_pairs={{0,6},{1,7},{2,4},{3,5},{4,2},{5,3},{6,0},{7,1},{8,14},{9,15},{10,... | collective-permute-start | bytes 393224 | tf_op jit(solution)/shard_map/ppermute | solution.py:701
  43.1 19.2 %collective-permute-start.20 = (bf16[64,1024]{1,0:T(8,128)(2,1)}, bf16[64,1024]{1,0:T(8,128)(2,1)}, u32[]{:S(2)}, u32[]{:S(2)}) collective-permute-start(bf16[64,1024]{1,0:T(8,128)(2,1)} %get-tuple-element.68), channel_id=1, source_target_pairs={{0,7},{1,6},{2,5},{3,4},{4,3},{5,2},{6,1},{7,0},{8,15},{9,14},{10,... | collective-permute-start | bytes 393224 | tf_op jit(solution)/shard_map/ppermute | solution.py:701
  50.7 22.5 %collective-permute-start.7 = (bf16[2,8,32,128]{3,2,1,0:T(8,128)(2,1)}, bf16[2,8,32,128]{3,2,1,0:T(8,128)(2,1)}, u32[]{:S(2)}, u32[]{:S(2)}) collective-permute-start(bf16[2,8,32,128]{3,2,1,0:T(8,128)(2,1)} %get-tuple-element.53), channel_id=1, source_target_pairs={{0,1},{1,0},{2,3},{3,2},{4,5},{5,4},{6,7},{7,6},{8,9},{9,8},{10,11... | collective-permute-start | bytes 393224 | tf_op jit(solution)/shard_map/ppermute | solution.py:701
  52.9 22.9 %collective-permute-start.8 = (bf16[2,8,32,128]{3,2,1,0:T(8,128)(2,1)}, bf16[2,8,32,128]{3,2,1,0:T(8,128)(2,1)}, u32[]{:S(2)}, u32[]{:S(2)}) collective-permute-start(bf16[2,8,32,128]{3,2,1,0:T(8,128)(2,1)} %get-tuple-element.54), channel_id=1, source_target_pairs={{0,2},{1,3},{2,0},{3,1},{4,6},{5,7},{6,4},{7,5},{8,10},{9,11},{10,... | collective-permute-start | bytes 393224 | tf_op jit(solution)/shard_map/ppermute | solution.py:701
  59.5 19.1 %collective-permute-start.9 = (bf16[2,8,32,128]{3,2,1,0:T(8,128)(2,1)}, bf16[2,8,32,128]{3,2,1,0:T(8,128)(2,1)}, u32[]{:S(2)}, u32[]{:S(2)}) collective-permute-start(bf16[2,8,32,128]{3,2,1,0:T(8,128)(2,1)} %get-tuple-element.55), channel_id=1, source_target_pairs={{0,3},{1,2},{2,1},{3,0},{4,7},{5,6},{6,5},{7,4},{8,11},{9,10},{10,... | collective-permute-start | bytes 393224 | tf_op jit(solution)/shard_map/ppermute | solution.py:701
  59.5 19.1 %collective-permute-start.10 = (bf16[2,8,32,128]{3,2,1,0:T(8,128)(2,1)}, bf16[2,8,32,128]{3,2,1,0:T(8,128)(2,1)}, u32[]{:S(2)}, u32[]{:S(2)}) collective-permute-start(bf16[2,8,32,128]{3,2,1,0:T(8,128)(2,1)} %get-tuple-element.56), channel_id=1, source_target_pairs={{0,4},{1,5},{2,6},{3,7},{4,0},{5,1},{6,2},{7,3},{8,12},{9,13},{10,... | collective-permute-start | bytes 393224 | tf_op jit(solution)/shard_map/ppermute | solution.py:701
  62.3 16.8 %collective-permute-start.11 = (bf16[2,8,32,128]{3,2,1,0:T(8,128)(2,1)}, bf16[2,8,32,128]{3,2,1,0:T(8,128)(2,1)}, u32[]{:S(2)}, u32[]{:S(2)}) collective-permute-start(bf16[2,8,32,128]{3,2,1,0:T(8,128)(2,1)} %get-tuple-element.57), channel_id=1, source_target_pairs={{0,5},{1,4},{2,7},{3,6},{4,1},{5,0},{6,3},{7,2},{8,13},{9,12},{10,... | collective-permute-start | bytes 393224 | tf_op jit(solution)/shard_map/ppermute | solution.py:701
  78.6 14.0 %collective-permute-start.22 = (bf16[2,8,32,128]{3,2,1,0:T(8,128)(2,1)}, bf16[2,8,32,128]{3,2,1,0:T(8,128)(2,1)}, u32[]{:S(2)}, u32[]{:S(2)}) collective-permute-start(bf16[2,8,32,128]{3,2,1,0:T(8,128)(2,1)} %get-tuple-element.71), channel_id=1, source_target_pairs={{0,2},{1,3},{2,0},{3,1},{4,6},{5,7},{6,4},{7,5},{8,10},{9,11},{10,... | collective-permute-start | bytes 393224 | tf_op jit(solution)/shard_map/ppermute | solution.py:701
  79.1 20.5 %collective-permute-start.23 = (bf16[2,8,32,128]{3,2,1,0:T(8,128)(2,1)}, bf16[2,8,32,128]{3,2,1,0:T(8,128)(2,1)}, u32[]{:S(2)}, u32[]{:S(2)}) collective-permute-start(bf16[2,8,32,128]{3,2,1,0:T(8,128)(2,1)} %get-tuple-element.72), channel_id=1, source_target_pairs={{0,3},{1,2},{2,1},{3,0},{4,7},{5,6},{6,5},{7,4},{8,11},{9,10},{10,... | collective-permute-start | bytes 393224 | tf_op jit(solution)/shard_map/ppermute | solution.py:701
  82.1 18.5 %collective-permute-start.24 = (bf16[2,8,32,128]{3,2,1,0:T(8,128)(2,1)}, bf16[2,8,32,128]{3,2,1,0:T(8,128)(2,1)}, u32[]{:S(2)}, u32[]{:S(2)}) collective-permute-start(bf16[2,8,32,128]{3,2,1,0:T(8,128)(2,1)} %get-tuple-element.73), channel_id=1, source_target_pairs={{0,4},{1,5},{2,6},{3,7},{4,0},{5,1},{6,2},{7,3},{8,12},{9,13},{10,... | collective-permute-start | bytes 393224 | tf_op jit(solution)/shard_map/ppermute | solution.py:701
  85.2 19.0 %collective-permute-start.25 = (bf16[2,8,32,128]{3,2,1,0:T(8,128)(2,1)}, bf16[2,8,32,128]{3,2,1,0:T(8,128)(2,1)}, u32[]{:S(2)}, u32[]{:S(2)}) collective-permute-start(bf16[2,8,32,128]{3,2,1,0:T(8,128)(2,1)} %get-tuple-element.74), channel_id=1, source_target_pairs={{0,5},{1,4},{2,7},{3,6},{4,1},{5,0},{6,3},{7,2},{8,13},{9,12},{10,... | collective-permute-start | bytes 393224 | tf_op jit(solution)/shard_map/ppermute | solution.py:701
  90.5 13.7 %collective-permute-start.26 = (bf16[2,8,32,128]{3,2,1,0:T(8,128)(2,1)}, bf16[2,8,32,128]{3,2,1,0:T(8,128)(2,1)}, u32[]{:S(2)}, u32[]{:S(2)}) collective-permute-start(bf16[2,8,32,128]{3,2,1,0:T(8,128)(2,1)} %get-tuple-element.75), channel_id=1, source_target_pairs={{0,6},{1,7},{2,4},{3,5},{4,2},{5,3},{6,0},{7,1},{8,14},{9,15},{10,... | collective-permute-start | bytes 393224 | tf_op jit(solution)/shard_map/ppermute | solution.py:701
  99.6 16.3 %collective-permute-start.30 = (bf16[256,8,128]{2,1,0:T(8,128)(2,1)}, bf16[256,8,128]{2,1,0:T(8,128)(2,1)}, u32[]{:S(2)}, u32[]{:S(2)}) collective-permute-start(bf16[256,8,128]{2,1,0:T(8,128)(2,1)} %get-tuple-element.78), channel_id=1, source_target_pairs={{0,8},{8,0},{16,24},{24,16},{1,9},{9,1},{17,25},{25,17},{2,10},{10... | collective-permute-start | bytes 1572872 | tf_op jit(solution)/shard_map/ppermute | solution.py:707
  108.9 15.1 %collective-permute-start.28 = (bf16[256,8,128]{2,1,0:T(8,128)(2,1)}, bf16[256,8,128]{2,1,0:T(8,128)(2,1)}, u32[]{:S(2)}, u32[]{:S(2)}) collective-permute-start(bf16[256,8,128]{2,1,0:T(8,128)(2,1)} %turn.4.refs_8_.refs_2_), channel_id=1, source_target_pairs={{0,16},{8,24},{16,0},{24,8},{1,17},{9,25},{17,1},{25,9},{2,18},{10... | collective-permute-start | bytes 1572872 | tf_op jit(solution)/shard_map/ppermute | solution.py:707
  110.4 24.4 %collective-permute-start.29 = (bf16[256,8,128]{2,1,0:T(8,128)(2,1)}, bf16[256,8,128]{2,1,0:T(8,128)(2,1)}, u32[]{:S(2)}, u32[]{:S(2)}) collective-permute-start(bf16[256,8,128]{2,1,0:T(8,128)(2,1)} %turn.6.refs_8_.refs_3_), channel_id=1, source_target_pairs={{0,16},{8,24},{16,0},{24,8},{1,17},{9,25},{17,1},{25,9},{2,18},{10... | collective-permute-start | bytes 1572872 | tf_op jit(solution)/shard_map/ppermute | solution.py:707
  (10 other events, 95.5 us)
